TPU v7x, 256 devices: a whole 4x4x8 slice. The times are simulated.
256 devices in a mesh: prow: 32 (over z_hi, y, x), pcol: 8 (over z_lo, core).
Axes of the slice: x: 4, y: 4, z: 8 (z_hi: 2, z_lo: 4; z = z_hi * 4 + z_lo), core: 2. Of those that a mesh axis runs over, the one named last changes fastest.
Arguments:
- design: float32 [1024, 32768], P('pcol', 'prow'), may hold values from -0.1875 to 0.1875
- damping: float32 [512], replicated, may hold values from 0.1 to 2
Outputs:
- factored: float32 [32768, 8192], P('prow', 'pcol')
All inputs are finite; a program needn't handle non-finite values.
Results may differ from a plain program's by a relative error of at most 0.00011.
Values sent between devices are 32-bit elements; how exact they have to be, the bound alone decides.
No kernel may reach another device: no remote copies, remote signals or barrier semaphores. Data moves between devices by JAX's collectives and lax.ppermute only.
A program may use at most 128 MiB of HBM per device.

v0:
```python
import jax
import jax.numpy as jnp
from jax import lax
from jax.sharding import PartitionSpec as P

BLOCK = 512
BATCHES = 4


def spread(shard, axis, root):
    mine = lax.axis_index(axis) == root
    return lax.psum(jnp.where(mine, shard, jnp.zeros_like(shard)), axis)


def joined_along(parts, dim):
    lengths = list(parts.shape[1:])
    lengths[dim] *= parts.shape[0]
    return jnp.moveaxis(parts, 0, dim).reshape(lengths)


def from_everyone(shard, axis):
    copies = jnp.broadcast_to(shard, (lax.axis_size(axis), *shard.shape))
    return lax.all_to_all(copies, axis, split_axis=0, concat_axis=0, tiled=True)


def collect(shard, axis, dim):
    return joined_along(from_everyone(shard, axis), dim)


def gram_block(row_block, column_block):
    return lax.dot_general(
        row_block,
        column_block,
        (((0,), (0,)), ((), ())),
        precision=lax.Precision.HIGHEST,
        preferred_element_type=jnp.float32,
    )


def per_device(design, damping):
    tile_size = design.shape[1]
    batch_size = design.shape[0] // BATCHES
    column_index = lax.axis_index("pcol")
    row_index = lax.axis_index("prow")
    column_count = lax.axis_size("pcol")
    row_global = row_index * tile_size + jnp.arange(tile_size, dtype=jnp.int32)
    column_global = column_index * tile_size + jnp.arange(tile_size, dtype=jnp.int32)
    padded_damping = jnp.pad(damping, (0, tile_size - BLOCK))
    lead_local = spread(design[:, :BLOCK], "prow", 0)
    lead_all = collect(lead_local, "pcol", 0)
    accumulated = jnp.zeros((tile_size, tile_size), jnp.float32)
    row_list = []
    column_list = []
    for batch in range(BATCHES):
        batch_rows = design[batch * batch_size : (batch + 1) * batch_size]
        row_block = collect(batch_rows, "pcol", 0)
        column_block = spread(row_block, "prow", column_index)
        accumulated = accumulated + gram_block(row_block, column_block)
        row_list.append(row_block)
        column_list.append(column_block)
    on_diagonal = (row_global[:, None] == column_global[None, :]) & (column_global[None, :] < BLOCK)
    shifted = accumulated + jnp.where(on_diagonal, padded_damping[None, :], 0.0)
    lead_order = (
        lead_all.reshape(column_count, BATCHES, batch_size, BLOCK)
        .transpose(1, 0, 2, 3)
        .reshape(-1, BLOCK)
    )
    lead_gram = gram_block(lead_order, lead_order) + jnp.diag(damping)
    factor = jnp.linalg.cholesky(lead_gram)
    whitened = jax.scipy.linalg.solve_triangular(factor, lead_order.T, lower=True).T
    inverse_upper = jax.scipy.linalg.solve_triangular(
        factor, jnp.eye(BLOCK, dtype=jnp.float32), lower=True
    ).T
    damped_rows = jnp.pad(damping[:, None] * inverse_upper, ((0, tile_size - BLOCK), (0, 0)))
    row_all = jnp.concatenate(row_list, axis=0)
    column_all = jnp.concatenate(column_list, axis=0)
    panel_mine = gram_block(row_all, whitened) + jnp.where(row_index == 0, damped_rows, 0.0)
    panel_other = gram_block(column_all, whitened) + jnp.where(column_index == 0, damped_rows, 0.0)
    update = lax.dot_general(
        panel_mine,
        panel_other,
        (((1,), (1,)), ((), ())),
        precision=lax.Precision.HIGHEST,
        preferred_element_type=jnp.float32,
    )
    trailing = shifted - update
    panel_padded = jnp.pad(panel_mine, ((0, 0), (0, tile_size - BLOCK)))
    return jnp.where(column_global[None, :] < BLOCK, panel_padded, trailing)


def solution(mesh):
    in_specs = (P("pcol", "prow"), P())
    out_specs = P("prow", "pcol")
    return jax.shard_map(
        per_device, mesh=mesh, in_specs=in_specs, out_specs=out_specs, check_vma=False
    )
```

profile of v0, /device:TPU:1, one launch (start us, length us, event | category | flops | bytes accessed | tf_op | source)
XLA Modules:
  0.0 864.9 jit_solution(16178710520691920352)
XLA Ops:
  7.8 32.7 %all_to_all.25 = f32[8,32,1024]{2,1,0:T(8,128)S(1)} all-to-all(f32[8,32,1024]{2,1,0:T(8,128)S(1)} %broadcast_in_dim.75), channel_id=1, replica_groups=mesh['prow'=32,'pcol'=8] {'pcol'}, dimensions={0} | all-to-all | bytes 2097152 | tf_op jit(solution)/shard_map/all_to_all | solution.py:23
  40.6 29.0 %all_to_all.26 = f32[8,32,1024]{2,1,0:T(8,128)S(1)} all-to-all(f32[8,32,1024]{2,1,0:T(8,128)S(1)} %broadcast_in_dim.74), channel_id=1, replica_groups=mesh['prow'=32,'pcol'=8] {'pcol'}, dimensions={0} | all-to-all | bytes 2097152 | tf_op jit(solution)/shard_map/all_to_all | solution.py:23
  69.7 29.0 %all_to_all.27 = f32[8,32,1024]{2,1,0:T(8,128)S(1)} all-to-all(f32[8,32,1024]{2,1,0:T(8,128)S(1)} %broadcast_in_dim.73), channel_id=1, replica_groups=mesh['prow'=32,'pcol'=8] {'pcol'}, dimensions={0} | all-to-all | bytes 2097152 | tf_op jit(solution)/shard_map/all_to_all | solution.py:23
  99.8 5.2 all-to-all-start
  109.8 20.9 %all-to-all-done = f32[8,32,1024]{2,1,0:T(8,128)} async-done(((f32[8,32,1024]{2,1,0:T(8,128)}), f32[8,32,1024]{2,1,0:T(8,128)}, u32[]{:S(2)}, u32[]{:S(2)}) %all-to-all-start) | async-done | bytes 1048608 | tf_op jit(solution)/shard_map/all_to_all | solution.py:23
  133.0 434.6 %all-reduce.7.cloned.1.call-done = (f32[256,1024]{1,0:T(8,128)}, f32[256,1024]{1,0:T(8,128)}, f32[256,1024]{1,0:T(8,128)}, f32[256,1024]{1,0:T(8,128)}, f32[128,512]{1,0:T(8,128)}) async-done(((f32[256,1024]{1,0:T(8,128)}, f32[256,1024]{1,0:T(8,128)}, f32[256,1024]{1,0:T(8,128)}, f32[256,1024]{1,0:T(8,128)}, f32[128,512]{1,0:T(8,128)}), (f32[256,1024]{1,0:T(8,128)}, f32[256,1024]{1,0:T(8,128)}, ...) | async-done | bytes 4456464 | tf_op jit(solution)/shard_map/psum | solution.py:12
  570.2 23.8 %all-to-all-start.4 = ((f32[8,128,512]{2,1,0:T(8,128)}), f32[8,128,512]{2,1,0:T(8,128)}, u32[]{:S(2)}, u32[]{:S(2)}) async-start(f32[8,128,512]{2,1,0:T(8,128)} %broadcast_in_dim.77), calls=%async_computation.4 | async-start | bytes 4194304 | tf_op jit(solution)/shard_map/all_to_all | solution.py:23
  596.0 7.1 fusion.91
  603.1 5.2 fusion.92
  608.3 5.1 fusion.93
  613.4 5.3 fusion.94
  618.6 23.5 %all-to-all-done.4 = f32[8,128,512]{2,1,0:T(8,128)} async-done(((f32[8,128,512]{2,1,0:T(8,128)}), f32[8,128,512]{2,1,0:T(8,128)}, u32[]{:S(2)}, u32[]{:S(2)}) %all-to-all-start.4) | async-done | bytes 2097184 | tf_op jit(solution)/shard_map/all_to_all | solution.py:23
  642.1 6.7 fusion.31
  654.2 11.7 %cholesky.103 = f32[128,128]{1,0:T(8,128)S(1)} custom-call(f32[128,128]{1,0:T(8,128)S(1)} %cholesky.263), custom_call_target="Cholesky" | custom-call | tf_op jit(solution)/shard_map/jit(cholesky)/cholesky | solution.py:69
  667.1 3.2 copy.7
  670.3 9.8 %custom-call.34 = f32[1,128,128]{1,2,0:T(8,128)S(1)} custom-call(f32[1,128,128]{2,1,0:T(8,128)S(1)} %get-tuple-element.41), custom_call_target="InvertDiagBlocksLowerTriangular" | custom-call | tf_op jit(solution)/shard_map/jit(cholesky)/cholesky | solution.py:69
  683.3 12.1 %cholesky.215 = f32[128,128]{1,0:T(8,128)S(1)} custom-call(f32[128,128]{1,0:T(8,128)S(1)} %cholesky.267), custom_call_target="Cholesky" | custom-call | tf_op jit(solution)/shard_map/jit(cholesky)/cholesky | solution.py:69
  696.1 9.8 %custom-call.35 = f32[1,128,128]{1,2,0:T(8,128)S(1)} custom-call(f32[1,128,128]{2,1,0:T(8,128)S(1)} %get-tuple-element.38), custom_call_target="InvertDiagBlocksLowerTriangular" | custom-call | tf_op jit(solution)/shard_map/jit(cholesky)/cholesky | solution.py:69
  708.3 11.7 %cholesky.236 = f32[128,128]{1,0:T(8,128)S(1)} custom-call(f32[128,128]{1,0:T(8,128)S(1)} %cholesky.272), custom_call_target="Cholesky" | custom-call | tf_op jit(solution)/shard_map/jit(cholesky)/cholesky | solution.py:69
  721.4 9.8 %custom-call.36 = f32[1,128,128]{1,2,0:T(8,128)S(1)} custom-call(f32[1,128,128]{2,1,0:T(8,128)S(1)} %get-tuple-element.35), custom_call_target="InvertDiagBlocksLowerTriangular" | custom-call | tf_op jit(solution)/shard_map/jit(cholesky)/cholesky | solution.py:69
  733.5 11.9 %cholesky.253 = f32[128,128]{1,0:T(8,128)S(1)} custom-call(f32[128,128]{1,0:T(8,128)S(1)} %convolution_subtract_fusion.7), custom_call_target="Cholesky" | custom-call | tf_op jit(solution)/shard_map/jit(cholesky)/cholesky | solution.py:69
  752.1 14.0 %while.1 = (s32[]{:T(128)}, f32[512,512]{1,0:T(8,128)}, s32[4,2]{0,1:T(2,128)S(1)}, f32[4,128,128]{2,1,0:T(8,128)}, s32[]{:T(128)}) while((s32[]{:T(128)}, f32[512,512]{1,0:T(8,128)}, s32[4,2]{0,1:T(2,128)S(1)}, f32[4,128,128]{2,1,0:T(8,128)}, s32[]{:T(128)}) %tuple.31), condition=%wide.while_cond, body=%wide.while_body.sunk | while | flops 2 | bytes 132705 | solution.py:70
  752.8 2.9 bitcast_dynamic-update-slice_fusion.2
  756.3 2.9 bitcast_dynamic-update-slice_fusion.2
  759.8 2.9 bitcast_dynamic-update-slice_fusion.2
  763.3 2.8 bitcast_dynamic-update-slice_fusion.2
  766.1 40.1 %custom-call.37 = f32[4,128,128]{1,2,0:T(8,128)S(1)} custom-call(f32[4,128,128]{2,1,0:T(8,128)} %get-tuple-element.12), custom_call_target="InvertDiagBlocksLowerTriangular" | custom-call | tf_op jit(solution)/shard_map/jit(_solve_triangular)/triangular_solve | solution.py:70
  813.4 2.8 fusion.34
  816.9 8.4 fusion.8
  829.4 9.6 %fusion.18 = f32[1024,512]{0,1:T(8,128)} fusion(f32[512,512]{0,1:T(8,128)S(1)} %fusion.40, f32[256,1024]{1,0:T(8,128)S(1)} %bitcast.98, f32[256,1024]{1,0:T(8,128)S(1)} %bitcast.100, f32[256,1024]{1,0:T(8,128)S(1)} %bitcast.102, f32[256,1024]{1,0:T(8,128)} %bitcast, f32[128,1024]{1,0:T(8,128)S(1)} %fusion.78, f32[128,1024]{1,0:T(8,128)S(1)} %fusion.76, ...), kind=kOutput, calls=%fused_computation.23 | convolution fusion | flops 6448218112 | bytes 9437185 | tf_op jit(solution)/shard_map/dot_general | solution.py:31
  839.0 13.3 %fusion.17 = f32[1024,1024]{0,1:T(8,128)} fusion(f32[1024,1024]{1,0:T(8,128)S(1)} %copy-done.3, f32[1024,1024]{1,0:T(8,128)S(1)} %copy-done.2, f32[1024,1024]{1,0:T(8,128)S(1)} %copy-done, f32[1024,1024]{1,0:T(8,128)S(1)} %copy-done.1, f32[1024,512]{0,1:T(8,128)} %fusion.18, f32[1024,512]{0,1:T(8,128)} %fusion.8, f32[512,512]{0,1:T(8,128)S(1)} %fusion.40, ...), kind=kOutput, calls=%fused_computation.20 | convolution fusion | flops 6452936704 | bytes 26227712 | tf_op jit(solution)/shard_map/dot_general | solution.py:79
  852.3 5.3 copy.11
  (95 shorter events, 49.0 us)
Async XLA Ops:
  99.8 30.9 %all-to-all-start = ((f32[8,32,1024]{2,1,0:T(8,128)}), f32[8,32,1024]{2,1,0:T(8,128)}, u32[]{:S(2)}, u32[]{:S(2)}) async-start(f32[8,32,1024]{2,1,0:T(8,128)} %broadcast_in_dim.72), calls=%async_computation | async-start | bytes 2097152 | tf_op jit(solution)/shard_map/all_to_all | solution.py:23
  105.0 462.7 %all-reduce.7.cloned.1.call-start = ((), (), s32[]{:S(2)}) async-start(), calls=%async_computation.5 | async-start | bytes 8912896 | tf_op jit(solution)/shard_map/psum | solution.py:12
  570.2 23.8 %copy-start.15 = (f32[512]{0:T(512)S(1)}, f32[512]{0:T(512)}, u32[]{:S(2)}) copy-start(f32[512]{0:T(512)} %param.3) | copy-start | bytes 6148
  570.2 71.9 %all-to-all-start.4 = ((f32[8,128,512]{2,1,0:T(8,128)}), f32[8,128,512]{2,1,0:T(8,128)}, u32[]{:S(2)}, u32[]{:S(2)}) async-start(f32[8,128,512]{2,1,0:T(8,128)} %broadcast_in_dim.77), calls=%async_computation.4 | async-start | bytes 4194304 | tf_op jit(solution)/shard_map/all_to_all | solution.py:23
  596.0 7.1 copy-start.13
  603.1 5.2 copy-start.10
  608.3 5.1 copy-start.8
  653.2 1.0 copy-start.7
  806.3 4.6 copy-start.4
  806.3 4.6 copy-start.5
  812.7 4.1 copy-start.14
  813.4 3.5 copy-start.9
  813.4 3.5 copy-start.11
  813.4 3.5 copy-start.12
  816.9 9.5 %copy-start.6 = (f32[512,512]{1,0:T(8,128)S(1)}, f32[512,512]{1,0:T(8,128)}, u32[]{:S(2)}) copy-start(f32[512,512]{1,0:T(8,128)} %fusion.50) | copy-start | bytes 3145732
  829.3 9.7 %copy-start = (f32[1024,1024]{1,0:T(8,128)S(1)}, f32[1024,1024]{1,0:T(8,128)}, u32[]{:S(2)}) copy-start(f32[1024,1024]{1,0:T(8,128)} %fusion.91) | copy-start | bytes 12582916
  829.3 9.6 %copy-start.1 = (f32[1024,1024]{1,0:T(8,128)S(1)}, f32[1024,1024]{1,0:T(8,128)}, u32[]{:S(2)}) copy-start(f32[1024,1024]{1,0:T(8,128)} %fusion.92) | copy-start | bytes 12582916
  829.3 9.6 %copy-start.2 = (f32[1024,1024]{1,0:T(8,128)S(1)}, f32[1024,1024]{1,0:T(8,128)}, u32[]{:S(2)}) copy-start(f32[1024,1024]{1,0:T(8,128)} %fusion.93) | copy-start | bytes 12582916
  829.4 9.6 %copy-start.3 = (f32[1024,1024]{1,0:T(8,128)S(1)}, f32[1024,1024]{1,0:T(8,128)}, u32[]{:S(2)}) copy-start(f32[1024,1024]{1,0:T(8,128)} %fusion.94) | copy-start | bytes 12582916
Sparse Core Ops, SparseCore 0:
  133.2 434.4 all-reduce.6
where the time goes:
time: 874 us; the launch traced here: 865 us
  waiting for transfers between devices  479 us (55%)
  other arithmetic  134 us (15%)
  blocking collectives  90.7 us (10%)
  matrix products  82.7 us (9%)
  local copies, waits for them, and re-layouts  32.4 us (4%)
  starting transfers between devices  29 us (3%)
  between operations  16.8 us (2%)
    psum x1, waiting for transfers between devices, spread(): return lax.psum(jnp.where(mine, shard, jnp.zeros_like(shard)), axis)  435 us
    all_to_all x3, blocking collectives, from_everyone(): return lax.all_to_all(copies, axis, split_axis=0, concat_axis=0, tiled=True)  90.7 us
    another operation x14, other arithmetic, per_device(): factor = jnp.linalg.cholesky(lead_gram)  80.8 us
    dot_general x7, matrix products, gram_block(): lax.dot_general(row_block, column_block, (((0,), (0,)), ((), ())), precis...  47.4 us
    all_to_all x2, waiting for transfers between devices, from_everyone(): return lax.all_to_all(copies, axis, split_axis=0, concat_axis=0, tiled=True)  44.4 us
    another operation x3, other arithmetic, per_device(): jax.scipy.linalg.solve_triangular(factor, lead_order.T, lower=True)  42.5 us
    all_to_all x2, starting transfers between devices, from_everyone(): return lax.all_to_all(copies, axis, split_axis=0, concat_axis=0, tiled=True)  29 us
  transfers between devices with their start and end apart: 3, of which 3 were waited for; matrix products, arithmetic and copies ran while one was open for 3% of the time, Pallas kernels for 0%

commit v1 on v0

v1 whole, which is shorter than its diff:
```python
import jax
import jax.numpy as jnp
from jax import lax
from jax.sharding import Mesh
from jax.sharding import PartitionSpec as P

BLOCK = 512
AXES = ("zh", "y", "x", "zl", "core")
SIZES = (2, 4, 4, 4, 2)
ROW = ("zh", "y", "x")
COL = ("zl", "core")


def device_id(zh, y, x, zl, core):
    return (((zh * 4 + y) * 4 + x) * 4 + zl) * 2 + core


def ring(n, shift):
    return [(i, (i + shift) % n) for i in range(n)]


def spread_lead(value):
    columns = [(zl, core) for zl in range(4) for core in range(2)]

    def stage(value, moves):
        received = [
            lax.ppermute(value, AXES, [(device_id(*s, *c), device_id(*t, *c)) for s, t in move for c in columns])
            for move in moves
        ]
        for piece in received:
            value = value + piece
        return value

    value = stage(value, [[((0, 0, 0), (0, 0, x))] for x in (1, 3, 2)])
    value = stage(value, [[((0, 0, x), (0, y, x)) for x in range(4)] for y in (1, 3, 2)])
    return stage(value, [[((0, y, x), (1, y, x)) for y in range(4) for x in range(4)]])


def gather_lead(value):
    mine = jnp.stack([value] + [lax.ppermute(value, "zl", ring(4, k)) for k in (1, 2, 3)])
    other = lax.ppermute(mine, "core", ring(2, 1))
    both = jnp.stack([mine, other])
    zl, core = lax.axis_index("zl"), lax.axis_index("core")
    pieces = []
    for k in range(8):
        which = (core + k) % 2
        step = (zl - k // 2 + 4) % 4
        pieces.append(lax.dynamic_slice(both, (which, step, 0, 0), (1, 1, *value.shape)).reshape(value.shape))
    return jnp.concatenate(pieces)


def scatter_columns(design):
    half = design.shape[0] // 2
    mine = 0.0
    for zh in range(2):
        for j in range(2):
            pairs = []
            for c in range(8):
                for k in range(8):
                    p = 2 * k + j
                    pairs.append(
                        (device_id(0, c // 4, c % 4, k // 2, k % 2), device_id(zh, p // 4, p % 4, c // 2, c % 2))
                    )
            mine = mine + lax.ppermute(design[j * half : (j + 1) * half], AXES, pairs)
    return mine


def mm(a, b, dims, precision=lax.Precision.HIGH):
    return lax.dot_general(a, b, (dims, ((), ())), precision=precision, preferred_element_type=jnp.float32)


def per_device(design, damping):
    row = lax.axis_index(ROW)
    col = lax.axis_index(COL)
    is_root = row == 0
    lead_mine = jnp.where(is_root, design[:, :BLOCK], 0.0)
    lead = gather_lead(spread_lead(lead_mine))
    rows = lax.all_gather(design, COL, tiled=True)
    columns = lax.all_gather(scatter_columns(design), ("y", "x"), tiled=True)

    highest = lax.Precision.HIGHEST
    lead_gram = mm(lead, lead, ((0,), (0,)), highest) + jnp.diag(damping)
    factor = jnp.linalg.cholesky(lead_gram)
    inverse = jax.scipy.linalg.solve_triangular(factor, jnp.eye(BLOCK, dtype=jnp.float32), lower=True)
    white = mm(lead, inverse, ((1,), (1,)), highest)
    other = mm(white, columns, ((0,), (0,)))
    projected = columns - mm(white, other, ((1,), (0,)))
    is_panel = (col == 0) & (jnp.arange(columns.shape[1]) < BLOCK)
    width = columns.shape[1] - BLOCK
    right = jnp.where(is_panel[None, :], jnp.pad(white, ((0, 0), (0, width))), projected)
    out = mm(rows, right, ((0,), (0,)))
    correction = jnp.where(
        is_panel[None, :], jnp.pad(inverse.T, ((0, 0), (0, width))), -mm(inverse, other, ((0,), (0,)))
    )
    correction = jnp.where(is_root, damping[:, None] * correction, 0.0)
    return out + jnp.pad(correction, ((0, width), (0, 0)))


def solution(mesh):
    fine = Mesh(mesh.devices.reshape(SIZES), AXES)
    return jax.shard_map(per_device, mesh=fine, in_specs=(P(COL, ROW), P()), out_specs=P(ROW, COL), check_vma=False)
```

time: 874 us -> 333 us (0.38)
  the two profiles are of different devices: /device:TPU:1 before, /device:TPU:201 now
where the time goes in v1:
time: 333 us; the launch traced here: 329 us
  other arithmetic  124 us (37%)
  waiting for transfers between devices  94.9 us (28%)
  matrix products  46 us (14%)
  starting transfers between devices  25.9 us (8%)
  local copies, waits for them, and re-layouts  20.4 us (6%)
  between operations  17 us (5%)
    another operation x14, other arithmetic, per_device(): factor = jnp.linalg.cholesky(lead_gram)  79 us
    ppermute x7, waiting for transfers between devices, stage(): lax.ppermute(value, AXES, [(device_id(*s, *c), device_id(*t, *c)) for s,...  60.4 us
    another operation x3, other arithmetic, per_device(): jax.scipy.linalg.solve_triangular(factor, jnp.eye(BLOCK, dtype=jnp.float3...  40.3 us
    dot_general x6, matrix products, mm(): lax.dot_general(a, b, (dims, ((), ())), precision=precision, preferred_el...  34.7 us
    ppermute x3, waiting for transfers between devices, gather_lead(): lax.ppermute(value, 'zl', ring(4, k))  22.1 us
    ppermute x3, starting transfers between devices, gather_lead(): lax.ppermute(value, 'zl', ring(4, k))  15.8 us
    ppermute x4, waiting for transfers between devices, scatter_columns(): mine = mine + lax.ppermute(design[j * half:(j + 1) * half], AXES, pairs)  11.1 us
    another operation x12, local copies, waits for them, and re-layouts  10.8 us
  transfers between devices with their start and end apart: 17, of which 6 were waited for; matrix products, arithmetic and copies ran while one was open for 51% of the time, Pallas kernels for 0%

profile of v1, /device:TPU:201, one launch (start us, length us, event | category | flops | bytes accessed | tf_op | source)
XLA Modules:
  0.0 328.7 jit_solution(15515029980785414487)
XLA Ops:
  7.7 1.3 collective-permute-start.13
  11.0 11.1 %collective-permute-done.13 = f32[64,1024]{1,0:T(8,128)S(1)} collective-permute-done((f32[64,1024]{1,0:T(8,128)S(1)}, f32[64,1024]{1,0:T(8,128)S(1)}, u32[]{:S(2)}, u32[]{:S(2)}) %collective-permute-start.13) | collective-permute-done | bytes 262176 | tf_op jit(solution)/shard_map/ppermute | solution.py:64
  28.7 60.4 %collective-permute-done.6 = f32[128,512]{1,0:T(8,128)S(1)} collective-permute-done((f32[128,512]{1,0:T(8,128)S(1)}, f32[128,512]{1,0:T(8,128)S(1)}, u32[]{:S(2)}, u32[]{:S(2)}) %collective-permute-start.6) | collective-permute-done | bytes 262176 | tf_op jit(solution)/shard_map/ppermute | solution.py:27
  89.1 2.6 collective-permute-start.9
  91.7 13.2 %collective-permute-start.8 = (f32[128,512]{1,0:T(8,128)S(1)}, f32[128,512]{1,0:T(8,128)S(1)}, u32[]{:S(2)}, u32[]{:S(2)}) collective-permute-start(f32[128,512]{1,0:T(8,128)S(1)} %add.231), channel_id=1, source_target_pairs={{0,4},{2,6},{4,0},{6,2},{1,5},{3,7},{5,1},{7,3},{8,12},{10,14},{12... | collective-permute-start | bytes 786440 | tf_op jit(solution)/shard_map/ppermute | solution.py:40
  104.9 3.0 collective-permute-done.9
  107.9 7.5 %collective-permute-done.8 = f32[128,512]{1,0:T(8,128)S(1)} collective-permute-done((f32[128,512]{1,0:T(8,128)S(1)}, f32[128,512]{1,0:T(8,128)S(1)}, u32[]{:S(2)}, u32[]{:S(2)}) %collective-permute-start.8) | collective-permute-done | bytes 262176 | tf_op jit(solution)/shard_map/ppermute | solution.py:40
  115.4 11.5 %collective-permute-done.7 = f32[128,512]{1,0:T(8,128)S(1)} collective-permute-done((f32[128,512]{1,0:T(8,128)S(1)}, f32[128,512]{1,0:T(8,128)S(1)}, u32[]{:S(2)}, u32[]{:S(2)}) %collective-permute-start.7) | collective-permute-done | bytes 262176 | tf_op jit(solution)/shard_map/ppermute | solution.py:40
  128.2 1.4 collective-permute-start.10
  132.7 1.3 copy-done
  134.0 3.7 %fusion.72 = f32[512,512]{1,0:T(8,128)S(1)} fusion(f32[1024,512]{1,0:T(8,128)S(1)} %fusion.20), kind=kOutput, calls=%fused_computation.132 | convolution fusion | flops 3221225472 | bytes 3145728 | tf_op jit(solution)/shard_map/dot_general | solution.py:69
  139.6 11.7 %cholesky.103 = f32[128,128]{1,0:T(8,128)S(1)} custom-call(f32[128,128]{1,0:T(8,128)S(1)} %cholesky.263), custom_call_target="Cholesky" | custom-call | tf_op jit(solution)/shard_map/jit(cholesky)/cholesky | solution.py:83
  151.4 9.8 %custom-call.31 = f32[1,128,128]{1,2,0:T(8,128)S(1)} custom-call(f32[1,128,128]{2,1,0:T(8,128)S(1)} %get-tuple-element.36), custom_call_target="InvertDiagBlocksLowerTriangular" | custom-call | tf_op jit(solution)/shard_map/jit(cholesky)/cholesky | solution.py:83
  163.9 12.1 %cholesky.215 = f32[128,128]{1,0:T(8,128)S(1)} custom-call(f32[128,128]{1,0:T(8,128)S(1)} %cholesky.267), custom_call_target="Cholesky" | custom-call | tf_op jit(solution)/shard_map/jit(cholesky)/cholesky | solution.py:83
  176.0 9.8 %custom-call.32 = f32[1,128,128]{1,2,0:T(8,128)S(1)} custom-call(f32[1,128,128]{2,1,0:T(8,128)S(1)} %get-tuple-element.33), custom_call_target="InvertDiagBlocksLowerTriangular" | custom-call | tf_op jit(solution)/shard_map/jit(cholesky)/cholesky | solution.py:83
  187.4 11.7 %cholesky.236 = f32[128,128]{1,0:T(8,128)S(1)} custom-call(f32[128,128]{1,0:T(8,128)S(1)} %cholesky.272), custom_call_target="Cholesky" | custom-call | tf_op jit(solution)/shard_map/jit(cholesky)/cholesky | solution.py:83
  199.1 9.9 %custom-call.33 = f32[1,128,128]{1,2,0:T(8,128)S(1)} custom-call(f32[1,128,128]{2,1,0:T(8,128)S(1)} %get-tuple-element.30), custom_call_target="InvertDiagBlocksLowerTriangular" | custom-call | tf_op jit(solution)/shard_map/jit(cholesky)/cholesky | solution.py:83
  210.5 11.7 %cholesky.253 = f32[128,128]{1,0:T(8,128)S(1)} custom-call(f32[128,128]{1,0:T(8,128)S(1)} %convolution_subtract_fusion.5), custom_call_target="Cholesky" | custom-call | tf_op jit(solution)/shard_map/jit(cholesky)/cholesky | solution.py:83
  227.1 10.9 %while.1 = (s32[]{:T(128)}, f32[512,512]{1,0:T(8,128)S(1)}, s32[4,2]{0,1:T(2,128)S(1)}, f32[4,128,128]{2,1,0:T(8,128)}, s32[]{:T(128)}) while((s32[]{:T(128)}, f32[512,512]{1,0:T(8,128)S(1)}, s32[4,2]{0,1:T(2,128)S(1)}, f32[4,128,128]{2,1,0:T(8,128)}, s32[]{:T(128)}) %tuple.29), condition=%wide.while_cond, body=%wide.while_body.sunk | while | flops 2 | bytes 132205 | solution.py:84
  227.8 2.0 bitcast_dynamic-update-slice_fusion.2
  230.5 2.0 bitcast_dynamic-update-slice_fusion.2
  233.2 2.0 bitcast_dynamic-update-slice_fusion.2
  235.9 2.0 bitcast_dynamic-update-slice_fusion.2
  237.9 40.1 %custom-call.34 = f32[4,128,128]{1,2,0:T(8,128)S(1)} custom-call(f32[4,128,128]{2,1,0:T(8,128)} %get-tuple-element.12), custom_call_target="InvertDiagBlocksLowerTriangular" | custom-call | tf_op jit(solution)/shard_map/jit(_solve_triangular)/triangular_solve | solution.py:84
  280.0 1.4 convolution_subtract_fusion
  281.8 1.7 convolution_subtract_fusion.2
  285.1 3.5 %fusion.50 = f32[1024,512]{1,0:T(8,128)S(1)} fusion(f32[1024,512]{1,0:T(8,128)S(1)} %copy-done.1, f32[128,512]{1,0:T(8,128)S(1)} %fusion.54, f32[128,512]{1,0:T(8,128)S(1)} %fusion.55, f32[128,512]{1,0:T(8,128)S(1)} %fusion.57, f32[128,512]{1,0:T(8,128)S(1)} %fusion.43), kind=kOutput, calls=%fused_computation.87 | convolution fusion | flops 3222011904 | bytes 5242880 | tf_op jit(solution)/shard_map/dot_general | solution.py:69
  288.6 5.8 %fusion.73 = f32[512,1024]{1,0:T(8,128)S(1)} fusion(f32[1024,512]{1,0:T(8,128)S(1)} %fusion.50, f32[1024,1024]{1,0:T(8,128)} %all-gather.3.cloned.1.call-done), kind=kOutput, calls=%fused_computation.133 | convolution fusion | flops 3221225472 | bytes 8388608 | tf_op jit(solution)/shard_map/dot_general | solution.py:69
  294.4 3.5 %multiply_select_fusion = f32[512,1024]{0,1:T(8,128)} fusion(f32[512,512]{0,1:T(8,128)S(1)} %copy-done.5, f32[512,1024]{1,0:T(8,128)S(1)} %fusion.73, f32[512]{0:T(512)S(1)} %copy-done.6, pred[1024]{0:T(1024)(128)(4,1)S(1)} %fusion.63, pred[]{:T(512)S(6)} %eq.40, f32[128,512]{1,0:T(8,128)S(1)} %fusion.54, f32[128,512]{1,0:T(8,128)S(1)} %fusion.55, ...), kind=kOutput, calls=%fused_computation.23 | convolution fusion | flops 1613496320 | bytes 6294529 | tf_op jit(solution)/shard_map/dot_general | solution.py:69
  298.0 5.0 %fusion.74 = f32[1024,1024]{1,0:T(8,128)} fusion(f32[1024,512]{1,0:T(8,128)S(1)} %fusion.50, f32[512,1024]{1,0:T(8,128)S(1)} %fusion.73), kind=kOutput, calls=%fused_computation.134 | convolution fusion | flops 3221225472 | bytes 8388608 | tf_op jit(solution)/shard_map/dot_general | solution.py:69
  302.9 13.3 %bitcast_add_fusion = f32[1024,1024]{0,1:T(8,128)} fusion(f32[512,1024]{0,1:T(8,128)} %multiply_select_fusion, f32[1024,1024]{1,0:T(8,128)} %all-gather.5.cloned.1.call-done, f32[1024,1024]{1,0:T(8,128)} %all-gather.3.cloned.1.call-done, f32[1024,1024]{1,0:T(8,128)} %fusion.74, f32[1024,512]{1,0:T(8,128)S(1)} %fusion.50, pred[1024]{0:T(1024)(128)(4,1)S(1)} %fusion.63), kind=kOutput, calls=%fused_computation.18 | convolution fusion | flops 6445596672 | bytes 20972544 | tf_op jit(solution)/shard_map/dot_general | solution.py:69
  316.2 5.3 %copy.5 = f32[1024,1024]{1,0:T(8,128)} copy(f32[1024,1024]{0,1:T(8,128)} %bitcast_add_fusion) | data formatting | bytes 8388608 | tf_op jit(solution)/shard_map/add | solution.py:96
  (95 shorter events, 30.0 us)
Async XLA Ops:
  6.5 16.5 %copy-start.2 = (f32[128,1024]{1,0:T(8,128)S(1)}, f32[128,1024]{1,0:T(8,128)}, u32[]{:S(2)}) copy-start(f32[128,1024]{1,0:T(8,128)} %param.2) | copy-start | bytes 1572868
  6.5 282.1 %all-gather.3.cloned.1.call-start = ((), (), s32[]{:S(2)}) async-start(), calls=%async_computation | async-start | bytes 4456448 | tf_op jit(solution)/shard_map/all_gather | solution.py:79
  7.7 14.5 %collective-permute-start.13 = (f32[64,1024]{1,0:T(8,128)S(1)}, f32[64,1024]{1,0:T(8,128)S(1)}, u32[]{:S(2)}, u32[]{:S(2)}) collective-permute-start(f32[64,1024]{1,0:T(8,128)S(1)} %get-tuple-element.25), channel_id=1, source_target_pairs={{0,128},{1,144},{2,160},{3,176},{4,192},{5,208},{6,224},{7,240},{8... | collective-permute-start | bytes 786440 | tf_op jit(solution)/shard_map/ppermute | solution.py:64
  9.0 13.2 %collective-permute-start.11 = (f32[64,1024]{1,0:T(8,128)S(1)}, f32[64,1024]{1,0:T(8,128)S(1)}, u32[]{:S(2)}, u32[]{:S(2)}) collective-permute-start(f32[64,1024]{1,0:T(8,128)S(1)} %get-tuple-element.25), channel_id=1, source_target_pairs={{0,0},{1,16},{2,32},{3,48},{4,64},{5,80},{6,96},{7,112},{8,1},{9,1... | collective-permute-start | bytes 786440 | tf_op jit(solution)/shard_map/ppermute | solution.py:64
  9.7 12.5 %collective-permute-start.14 = (f32[64,1024]{1,0:T(8,128)S(1)}, f32[64,1024]{1,0:T(8,128)S(1)}, u32[]{:S(2)}, u32[]{:S(2)}) collective-permute-start(f32[64,1024]{1,0:T(8,128)S(1)} %get-tuple-element.26), channel_id=1, source_target_pairs={{0,136},{1,152},{2,168},{3,184},{4,200},{5,216},{6,232},{7,248},{8... | collective-permute-start | bytes 786440 | tf_op jit(solution)/shard_map/ppermute | solution.py:64
  10.3 11.8 %collective-permute-start.12 = (f32[64,1024]{1,0:T(8,128)S(1)}, f32[64,1024]{1,0:T(8,128)S(1)}, u32[]{:S(2)}, u32[]{:S(2)}) collective-permute-start(f32[64,1024]{1,0:T(8,128)S(1)} %get-tuple-element.26), channel_id=1, source_target_pairs={{0,8},{1,24},{2,40},{3,56},{4,72},{5,88},{6,104},{7,120},{8,9},{9,... | collective-permute-start | bytes 786440 | tf_op jit(solution)/shard_map/ppermute | solution.py:64
  22.9 280.0 %all-gather.5.cloned.1.call-start = ((), (), s32[]{:S(2)}) async-start(), calls=%async_computation.1 | async-start | bytes 4718592 | tf_op jit(solution)/shard_map/all_gather | solution.py:78
  23.0 2.1 collective-permute-start.1
  23.7 1.4 collective-permute-start.2
  24.4 0.7 collective-permute-start
  25.2 2.1 collective-permute-start.5
  25.9 1.4 collective-permute-start.4
  26.6 0.7 collective-permute-start.3
  27.4 61.7 %collective-permute-start.6 = (f32[128,512]{1,0:T(8,128)S(1)}, f32[128,512]{1,0:T(8,128)S(1)}, u32[]{:S(2)}, u32[]{:S(2)}) collective-permute-start(f32[128,512]{1,0:T(8,128)S(1)} %add_add_fusion.1), channel_id=1, source_target_pairs={{0,128},{1,129},{2,130},{3,131},{4,132},{5,133},{6,134},{7,135},{8... | collective-permute-start | bytes 786440 | tf_op jit(solution)/shard_map/ppermute | solution.py:27
  89.1 18.8 %collective-permute-start.9 = (f32[128,512]{1,0:T(8,128)S(1)}, f32[128,512]{1,0:T(8,128)S(1)}, u32[]{:S(2)}, u32[]{:S(2)}) collective-permute-start(f32[128,512]{1,0:T(8,128)S(1)} %add.231), channel_id=1, source_target_pairs={{0,6},{2,0},{4,2},{6,4},{1,7},{3,1},{5,3},{7,5},{8,14},{10,8},{12,... | collective-permute-start | bytes 786440 | tf_op jit(solution)/shard_map/ppermute | solution.py:40
  91.7 23.7 %collective-permute-start.8 = (f32[128,512]{1,0:T(8,128)S(1)}, f32[128,512]{1,0:T(8,128)S(1)}, u32[]{:S(2)}, u32[]{:S(2)}) collective-permute-start(f32[128,512]{1,0:T(8,128)S(1)} %add.231), channel_id=1, source_target_pairs={{0,4},{2,6},{4,0},{6,2},{1,5},{3,7},{5,1},{7,3},{8,12},{10,14},{12... | collective-permute-start | bytes 786440 | tf_op jit(solution)/shard_map/ppermute | solution.py:40
  104.9 22.1 %collective-permute-start.7 = (f32[128,512]{1,0:T(8,128)S(1)}, f32[128,512]{1,0:T(8,128)S(1)}, u32[]{:S(2)}, u32[]{:S(2)}) collective-permute-start(f32[128,512]{1,0:T(8,128)S(1)} %add.231), channel_id=1, source_target_pairs={{0,2},{2,4},{4,6},{6,0},{1,3},{3,5},{5,7},{7,1},{8,10},{10,12},{12... | collective-permute-start | bytes 786440 | tf_op jit(solution)/shard_map/ppermute | solution.py:40
  128.2 3.9 %collective-permute-start.10 = (f32[4,128,512]{2,1,0:T(8,128)}, f32[4,128,512]{2,1,0:T(8,128)S(1)}, u32[]{:S(2)}, u32[]{:S(2)}) collective-permute-start(f32[4,128,512]{2,1,0:T(8,128)} %get-tuple-element.23), channel_id=1, source_target_pairs={{0,1},{1,0},{2,3},{3,2},{4,5},{5,4},{6,7},{7,6},{8,9},{9,8},{10,11... | collective-permute-start | bytes 3145736 | tf_op jit(solution)/shard_map/ppermute | solution.py:41
  130.8 148.3 %copy-start.3 = (f32[512,512]{1,0:T(8,128)}, f32[512,512]{1,0:T(8,128)S(1)}, u32[]{:S(2)}) copy-start(f32[512,512]{1,0:T(8,128)S(1)} %fusion.14) | copy-start | bytes 3145732
  132.7 1.3 copy-start
  137.7 0.7 copy-start.6
  138.6 1.0 copy-start.4
  281.8 3.3 %copy-start.1 = (f32[1024,512]{1,0:T(8,128)S(1)}, f32[1024,512]{1,0:T(8,128)}, u32[]{:S(2)}) copy-start(f32[1024,512]{1,0:T(8,128)} %copy-done) | copy-start | bytes 6291460
  288.6 5.8 %copy-start.5 = (f32[512,512]{0,1:T(8,128)S(1)}, f32[512,512]{0,1:T(8,128)}, u32[]{:S(2)}) copy-start(f32[512,512]{0,1:T(8,128)} %fusion.49) | copy-start | bytes 3145732
Sparse Core Ops, SparseCore 0:
  23.1 95.7 all-gather.2
  129.8 47.9 all-gather.4

commit v2 on v1

v2 whole, which is shorter than its diff:
```python
import jax
import jax.numpy as jnp
from jax import lax
from jax.experimental import pallas as pl
from jax.experimental.pallas import tpu as pltpu
from jax.sharding import Mesh
from jax.sharding import PartitionSpec as P

BLOCK = 512
SUB = 128
TILE = 256
AXES = ("zh", "y", "x", "zl", "core")
SIZES = (2, 4, 4, 4, 2)
ROW = ("zh", "y", "x")
COL = ("zl", "core")


def device_id(zh, y, x, zl, core):
    return (((zh * 4 + y) * 4 + x) * 4 + zl) * 2 + core


def ring(n, shift):
    return [(i, (i + shift) % n) for i in range(n)]


def spread_lead(value):
    columns = [(zl, core) for zl in range(4) for core in range(2)]

    def stage(value, moves):
        received = [
            lax.ppermute(value, AXES, [(device_id(*s, *c), device_id(*t, *c)) for s, t in move for c in columns])
            for move in moves
        ]
        for piece in received:
            value = value + piece
        return value

    value = stage(value, [[((0, 0, 0), (0, 0, x))] for x in (1, 3, 2)])
    value = stage(value, [[((0, 0, x), (0, y, x)) for x in range(4)] for y in (1, 3, 2)])
    return stage(value, [[((0, y, x), (1, y, x)) for y in range(4) for x in range(4)]])


def gather_lead(value):
    mine = jnp.stack([value] + [lax.ppermute(value, "zl", ring(4, k)) for k in (1, 2, 3)])
    other = lax.ppermute(mine, "core", ring(2, 1))
    zl, core = lax.axis_index("zl"), lax.axis_index("core")
    chip = (zl - jnp.arange(4) + 4) & 3
    return mine, other, jnp.concatenate([2 * chip + core, 2 * chip + 1 - core]).astype(jnp.int32)


def scatter_columns(design):
    half = design.shape[0] // 2
    mine = 0.0
    for zh in range(2):
        for j in range(2):
            pairs = []
            for c in range(8):
                for k in range(8):
                    p = 2 * k + j
                    pairs.append(
                        (device_id(0, c // 4, c % 4, k // 2, k % 2), device_id(zh, p // 4, p % 4, c // 2, c % 2))
                    )
            mine = mine + lax.ppermute(design[j * half : (j + 1) * half], AXES, pairs)
    return mine


def dot(a, b, dims, precision=None):
    return lax.dot_general(a, b, (dims, ((), ())), precision=precision, preferred_element_type=jnp.float32)


def split(a):
    high = a.astype(jnp.bfloat16)
    return high, (a - high.astype(jnp.float32)).astype(jnp.bfloat16)


def dot3(a, b, dims):
    return dot(a[0], b[0], dims) + (dot(a[0], b[1], dims) + dot(a[1], b[0], dims))


def eliminate(m_ref):
    lane = lax.broadcasted_iota(jnp.int32, (8, SUB), 1)
    sub = lax.broadcasted_iota(jnp.int32, (8, SUB), 0)
    for o in range(0, SUB, 8):
        left = [jnp.broadcast_to(m_ref[o + i : o + i + 1, :SUB], (8, SUB)) for i in range(8)]
        right = [jnp.broadcast_to(m_ref[o + i : o + i + 1, SUB:], (8, SUB)) for i in range(8)]
        e = {
            (i, j): jnp.broadcast_to(left[i][:, o + j : o + j + 1], (8, SUB)) for i in range(8) for j in range(i, 8)
        }
        strip_left = jnp.zeros((8, SUB), jnp.float32)
        strip_right = strip_left
        for i in range(8):
            r = lax.rsqrt(e[i, i])
            for j in range(i + 1, 8):
                e[i, j] = e[i, j] * r
            for j in range(i + 1, 8):
                for k in range(j, 8):
                    e[j, k] = e[j, k] - e[i, j] * e[i, k]
            a, b = left[i] * r, right[i] * r
            for j in range(i + 1, 8):
                left[j] = left[j] - e[i, j] * a
                right[j] = right[j] - e[i, j] * b
            strip_left = jnp.where(sub == i, a, strip_left)
            strip_right = jnp.where(sub == i, b, strip_right)
        m_ref[o : o + 8, :SUB] = strip_left
        m_ref[o : o + 8, SUB:] = strip_right
        if o + 8 < SUB:
            masked = jnp.where(lane >= o + 8, strip_left, 0.0)
            strip = jnp.concatenate([strip_left, strip_right], axis=1)
            update = dot(masked, strip, ((0,), (0,)), lax.Precision.HIGHEST)
            m_ref[o + 8 :, :] = m_ref[o + 8 :, :] - update[o + 8 :, :]


def lead_kernel(place_ref, mine_ref, other_ref, damping_ref, white_ref, inverse_ref, g_ref, m_ref):
    highest = lax.Precision.HIGHEST
    pieces = mine_ref.shape[0]
    depth = mine_ref.shape[1]
    both = [ref[...].reshape(pieces * depth, BLOCK) for ref in (mine_ref, other_ref)]
    same = lax.broadcasted_iota(jnp.int32, (BLOCK, BLOCK), 0) == lax.broadcasted_iota(jnp.int32, (BLOCK, BLOCK), 1)
    gram = dot(both[0], both[0], ((0,), (0,)), highest) + dot(both[1], both[1], ((0,), (0,)), highest)
    g_ref[:, :BLOCK] = gram + jnp.where(same, damping_ref[...], 0.0)
    g_ref[:, BLOCK:] = jnp.where(same, 1.0, 0.0)

    def step(p, carry):
        start = pl.multiple_of(p * SUB, SUB)
        m_ref[:, :SUB] = g_ref[pl.ds(start, SUB), pl.ds(start, SUB)]
        m_ref[:, SUB:] = jnp.where(same[:SUB, :SUB], 1.0, 0.0)
        eliminate(m_ref)
        inverse = m_ref[:, SUB:]
        for q in range(BLOCK // SUB):

            @pl.when(p == q)
            def _():
                lo, hi = q * SUB, (q + 1) * SUB
                strip = dot(inverse, g_ref[lo:hi, hi : hi + BLOCK], ((1,), (0,)), highest)
                g_ref[lo:hi, hi : hi + BLOCK] = strip
                if hi < BLOCK:
                    g_ref[hi:BLOCK, hi : hi + BLOCK] = g_ref[hi:BLOCK, hi : hi + BLOCK] - dot(
                        strip[:, : BLOCK - hi], strip, ((0,), (0,)), highest
                    )

        return carry

    lax.fori_loop(0, BLOCK // SUB, step, 0)
    inverse = g_ref[:, BLOCK:]
    inverse_ref[...] = inverse * damping_ref[...]
    pair = split(inverse)
    for h, ref in enumerate((mine_ref, other_ref)):
        for i in range(pieces):
            start = pl.multiple_of(place_ref[h * pieces + i] * depth, depth)
            white_ref[pl.ds(start, depth), :] = dot3(split(ref[i]), pair, ((1,), (1,)))


def lead_call(mine, other, place, damping):
    vmem = pl.BlockSpec(memory_space=pltpu.VMEM)
    rows = 2 * mine.shape[0] * mine.shape[1]
    return pl.pallas_call(
        lead_kernel,
        out_shape=(jax.ShapeDtypeStruct((rows, BLOCK), jnp.float32), jax.ShapeDtypeStruct((BLOCK, BLOCK), jnp.float32)),
        in_specs=[pl.BlockSpec(memory_space=pltpu.SMEM), vmem, vmem, vmem],
        out_specs=(vmem, vmem),
        scratch_shapes=[pltpu.VMEM((BLOCK, 2 * BLOCK), jnp.float32), pltpu.VMEM((SUB, 2 * SUB), jnp.float32)],
        name="lead",
    )(place, mine, other, damping.reshape(1, BLOCK))


def apply_kernel(where_ref, rows_ref, columns_ref, white_ref, inverse_ref, out_ref, wh, wl, vh, vl, rh, rl):
    t = pl.program_id(0)
    tiles = out_ref.shape[1] // TILE
    is_root = where_ref[0] == 0
    has_panel = where_ref[1] == 0
    white = (wh, wl)

    def put(refs, value, index):
        refs[0][index], refs[1][index] = split(value)

    def get(refs, index=...):
        return refs[0][index], refs[1][index]

    @pl.when(t == 0)
    def _():
        put(white, white_ref[...], ...)

    for j in range(tiles):

        @pl.when(t == j)
        def _():
            here = (slice(None), slice(j * TILE, (j + 1) * TILE))

            def trailing():
                block = columns_ref[...]
                put((vh, vl), dot3(get(white), split(block), ((0,), (0,))), here)
                put((rh, rl), block - dot3(get(white), get((vh, vl), here), ((1,), (0,))), here)

            if j * TILE < BLOCK:
                pl.when(jnp.logical_not(has_panel))(trailing)

                @pl.when(has_panel)
                def _():
                    row = lax.broadcasted_iota(jnp.int32, (BLOCK, TILE), 0)
                    column = lax.broadcasted_iota(jnp.int32, (BLOCK, TILE), 1) + j * TILE
                    put((vh, vl), jnp.where(row == column, -1.0, 0.0), here)
                    rh[here], rl[here] = get(white, here)
            else:
                trailing()

    @pl.when(t >= tiles)
    def _():
        out_ref[...] = dot3(split(rows_ref[...]), get((rh, rl)), ((0,), (0,)))

    for i in range(BLOCK // TILE):

        @pl.when((t == tiles + i) & is_root)
        def _():
            scaled = split(inverse_ref[:, i * TILE : (i + 1) * TILE])
            out_ref[...] = out_ref[...] - dot3(scaled, get((vh, vl)), ((0,), (0,)))


def apply_call(where, rows, columns, white, inverse):
    depth, size = rows.shape
    tiles = size // TILE
    bf16 = jnp.bfloat16
    grid_spec = pltpu.PrefetchScalarGridSpec(
        num_scalar_prefetch=1,
        grid=(2 * tiles,),
        in_specs=[
            pl.BlockSpec((depth, TILE), lambda t, w: (0, jnp.maximum(t - tiles, 0))),
            pl.BlockSpec((depth, TILE), lambda t, w: (0, jnp.minimum(t, tiles - 1))),
            pl.BlockSpec((depth, BLOCK), lambda t, w: (0, 0)),
            pl.BlockSpec((BLOCK, BLOCK), lambda t, w: (0, 0)),
        ],
        out_specs=pl.BlockSpec((TILE, size), lambda t, w: (jnp.maximum(t - tiles, 0), 0)),
        scratch_shapes=[pltpu.VMEM((depth, BLOCK), bf16)] * 2
        + [pltpu.VMEM((BLOCK, size), bf16)] * 2
        + [pltpu.VMEM((depth, size), bf16)] * 2,
    )
    return pl.pallas_call(
        apply_kernel, grid_spec=grid_spec, out_shape=jax.ShapeDtypeStruct((size, size), jnp.float32), name="apply"
    )(where, rows, columns, white, inverse)


def per_device(design, damping):
    row = lax.axis_index(ROW)
    col = lax.axis_index(COL)
    mine, other, place = gather_lead(spread_lead(jnp.where(row == 0, design[:, :BLOCK], 0.0)))
    rows = lax.all_gather(design, COL, tiled=True)
    columns = lax.all_gather(scatter_columns(design), ("y", "x"), tiled=True)
    white, inverse = lead_call(mine, other, place, damping)
    return apply_call(jnp.stack([row, col]).astype(jnp.int32), rows, columns, white, inverse)


def solution(mesh):
    fine = Mesh(mesh.devices.reshape(SIZES), AXES)
    return jax.shard_map(per_device, mesh=fine, in_specs=(P(COL, ROW), P()), out_specs=P(ROW, COL), check_vma=False)
```

time: 333 us -> 224 us (0.67)
  the two profiles are of different devices: /device:TPU:201 before, /device:TPU:1 now
where the time goes in v2:
time: 224 us
  Pallas kernels  75.2 us (34%)
  starting transfers between devices  64.6 us (29%)
  waiting for transfers between devices  64.3 us (29%)
  between operations  13.5 us (6%)
  other arithmetic  4.2 us (2%)
    pallas_call x1, Pallas kernels, lead_call(): pl.pallas_call(lead_kernel, out_shape=(jax.ShapeDtypeStruct((rows, BLOCK)...  46.8 us
    ppermute x7, waiting for transfers between devices, stage(): lax.ppermute(value, AXES, [(device_id(*s, *c), device_id(*t, *c)) for s,...  32.6 us
    pallas_call x1, Pallas kernels, apply_call(): pl.pallas_call(apply_kernel, grid_spec=grid_spec, out_shape=jax.ShapeDtyp...  28.4 us
    ppermute x4, starting transfers between devices, scatter_columns(): mine = mine + lax.ppermute(design[j * half:(j + 1) * half], AXES, pairs)  21.8 us
    ppermute x3, waiting for transfers between devices, gather_lead(): lax.ppermute(value, 'zl', ring(4, k))  21.5 us
    ppermute x7, starting transfers between devices, stage(): lax.ppermute(value, AXES, [(device_id(*s, *c), device_id(*t, *c)) for s,...  21.1 us
    ppermute x3, starting transfers between devices, gather_lead(): lax.ppermute(value, 'zl', ring(4, k))  20.5 us
    ppermute x4, waiting for transfers between devices, scatter_columns(): mine = mine + lax.ppermute(design[j * half:(j + 1) * half], AXES, pairs)  8.43 us
  transfers between devices with their start and end apart: 17, of which 11 were waited for; matrix products, arithmetic and copies ran while one was open for 2% of the time, Pallas kernels for 21%

profile of v2, /device:TPU:1, one launch (start us, length us, event | category | flops | bytes accessed | tf_op | source)
XLA Modules:
  0.0 223.9 jit_solution(3000669321395420494)
XLA Ops:
  7.3 1.1 fusion
  8.4 12.7 %collective-permute-start.2 = (f32[64,1024]{1,0:T(8,128)S(1)}, f32[64,1024]{1,0:T(8,128)S(1)}, u32[]{:S(2)}, u32[]{:S(2)}) collective-permute-start(f32[64,1024]{1,0:T(8,128)S(1)} %get-tuple-element.9), channel_id=1, source_target_pairs={{0,128},{1,144},{2,160},{3,176},{4,192},{5,208},{6,224},{7,240},{8... | collective-permute-start | bytes 786440 | tf_op jit(solution)/shard_map/ppermute | solution.py:63
  21.0 2.0 collective-permute-start
  23.0 1.3 collective-permute-start.3
  24.3 5.8 %collective-permute-start.1 = (f32[64,1024]{1,0:T(8,128)S(1)}, f32[64,1024]{1,0:T(8,128)S(1)}, u32[]{:S(2)}, u32[]{:S(2)}) collective-permute-start(f32[64,1024]{1,0:T(8,128)S(1)} %get-tuple-element.10), channel_id=1, source_target_pairs={{0,8},{1,24},{2,40},{3,56},{4,72},{5,88},{6,104},{7,120},{8,9},{9,... | collective-permute-start | bytes 786440 | tf_op jit(solution)/shard_map/ppermute | solution.py:63
  30.2 2.0 collective-permute-done
  32.2 6.4 %collective-permute-done.3 = f32[64,1024]{1,0:T(8,128)S(1)} collective-permute-done((f32[64,1024]{1,0:T(8,128)S(1)}, f32[64,1024]{1,0:T(8,128)S(1)}, u32[]{:S(2)}, u32[]{:S(2)}) %collective-permute-start.3) | collective-permute-done | bytes 262176 | tf_op jit(solution)/shard_map/ppermute | solution.py:63
  39.4 1.0 slice_select_fusion
  40.4 10.6 %collective-permute-start.5 = (f32[128,512]{1,0:T(8,128)S(1)}, f32[128,512]{1,0:T(8,128)S(1)}, u32[]{:S(2)}, u32[]{:S(2)}) collective-permute-start(f32[128,512]{1,0:T(8,128)S(1)} %slice_select_fusion), channel_id=1, source_target_pairs={{0,24},{1,25},{2,26},{3,27},{4,28},{5,29},{6,30},{7,31}} | collective-permute-start | bytes 786440 | tf_op jit(solution)/shard_map/ppermute | solution.py:31
  51.0 3.9 %collective-permute-start.6 = (f32[128,512]{1,0:T(8,128)S(1)}, f32[128,512]{1,0:T(8,128)S(1)}, u32[]{:S(2)}, u32[]{:S(2)}) collective-permute-start(f32[128,512]{1,0:T(8,128)S(1)} %slice_select_fusion), channel_id=1, source_target_pairs={{0,16},{1,17},{2,18},{3,19},{4,20},{5,21},{6,22},{7,23}} | collective-permute-start | bytes 786440 | tf_op jit(solution)/shard_map/ppermute | solution.py:31
  55.0 1.3 collective-permute-start.4
  56.3 4.9 %collective-permute-done.5 = f32[128,512]{1,0:T(8,128)S(1)} collective-permute-done((f32[128,512]{1,0:T(8,128)S(1)}, f32[128,512]{1,0:T(8,128)S(1)}, u32[]{:S(2)}, u32[]{:S(2)}) %collective-permute-start.5) | collective-permute-done | bytes 262176 | tf_op jit(solution)/shard_map/ppermute | solution.py:31
  61.1 2.2 collective-permute-done.6
  63.3 7.2 %collective-permute-done.4 = f32[128,512]{1,0:T(8,128)S(1)} collective-permute-done((f32[128,512]{1,0:T(8,128)S(1)}, f32[128,512]{1,0:T(8,128)S(1)}, u32[]{:S(2)}, u32[]{:S(2)}) %collective-permute-start.4) | collective-permute-done | bytes 262176 | tf_op jit(solution)/shard_map/ppermute | solution.py:31
  70.5 1.1 add_add_fusion.1
  71.6 1.3 collective-permute-start.9
  72.9 1.3 collective-permute-start.8
  74.2 1.3 collective-permute-start.7
  75.5 1.7 collective-permute-done.9
  77.2 1.3 collective-permute-done.8
  78.5 4.3 %collective-permute-done.7 = f32[128,512]{1,0:T(8,128)S(1)} collective-permute-done((f32[128,512]{1,0:T(8,128)S(1)}, f32[128,512]{1,0:T(8,128)S(1)}, u32[]{:S(2)}, u32[]{:S(2)}) %collective-permute-start.7) | collective-permute-done | bytes 262176 | tf_op jit(solution)/shard_map/ppermute | solution.py:31
  82.9 1.3 collective-permute-start.10
  84.2 11.1 %collective-permute-done.10 = f32[128,512]{1,0:T(8,128)S(1)} collective-permute-done((f32[128,512]{1,0:T(8,128)S(1)}, f32[128,512]{1,0:T(8,128)S(1)}, u32[]{:S(2)}, u32[]{:S(2)}) %collective-permute-start.10) | collective-permute-done | bytes 262176 | tf_op jit(solution)/shard_map/ppermute | solution.py:31
  95.3 4.9 %collective-permute-start.13 = (f32[128,512]{1,0:T(8,128)S(1)}, f32[128,512]{1,0:T(8,128)S(1)}, u32[]{:S(2)}, u32[]{:S(2)}) collective-permute-start(f32[128,512]{1,0:T(8,128)S(1)} %add.67), channel_id=1, source_target_pairs={{0,6},{2,0},{4,2},{6,4},{1,7},{3,1},{5,3},{7,5},{8,14},{10,8},{12,... | collective-permute-start | bytes 786440 | tf_op jit(solution)/shard_map/ppermute | solution.py:44
  100.2 14.2 %collective-permute-start.12 = (f32[128,512]{1,0:T(8,128)S(1)}, f32[128,512]{1,0:T(8,128)S(1)}, u32[]{:S(2)}, u32[]{:S(2)}) collective-permute-start(f32[128,512]{1,0:T(8,128)S(1)} %add.67), channel_id=1, source_target_pairs={{0,4},{2,6},{4,0},{6,2},{1,5},{3,7},{5,1},{7,3},{8,12},{10,14},{12... | collective-permute-start | bytes 786440 | tf_op jit(solution)/shard_map/ppermute | solution.py:44
  114.4 1.4 collective-permute-start.11
  115.8 21.5 %collective-permute-done.12 = f32[128,512]{1,0:T(8,128)S(1)} collective-permute-done((f32[128,512]{1,0:T(8,128)S(1)}, f32[128,512]{1,0:T(8,128)S(1)}, u32[]{:S(2)}, u32[]{:S(2)}) %collective-permute-start.12) | collective-permute-done | bytes 262176 | tf_op jit(solution)/shard_map/ppermute | solution.py:44
  137.4 1.3 collective-permute-start.14
  139.9 1.1 collective-permute-done.14.other_ref
  140.9 1.0 copy-done.1
  141.9 46.8 %lead.1 = (f32[1024,512]{1,0:T(8,128)}, f32[512,512]{1,0:T(8,128)}) custom-call(s32[8]{0:T(128)} %pad_add_fusion.1.place_ref, f32[4,128,512]{2,1,0:T(8,128)} %copy-done, f32[4,128,512]{2,1,0:T(8,128)} %copy-done.1, f32[1,512]{1,0:T(1,128)} %bitcast.11), custom_call_target="tpu_custom_call" | custom-call | tf_op jit(solution)/shard_map/lead/pallas_call | solution.py:156
  188.7 28.4 %apply.1 = f32[1024,1024]{1,0:T(8,128)} custom-call(s32[2]{0:T(128)} %pad_add_fusion.where_ref, f32[1024,1024]{1,0:T(8,128)} %all-gather.3.cloned.1.call-done.rows_ref, f32[1024,1024]{1,0:T(8,128)} %all-gather.5.cloned.1.call-done.columns_ref, f32[1024,512]{1,0:T(8,128)} %get-tuple-element.7.white_ref, f32[512,512]{1,0:T(8,128)} %get-tuple-element.8.inverse_ref), custom_call_target="tpu_custom_call" | custom-call | tf_op jit(solution)/shard_map/apply/pallas_call | solution.py:236
  (20 shorter events, 3.0 us)
Async XLA Ops:
  6.5 182.2 %all-gather.3.cloned.1.call-start = ((), (), s32[]{:S(2)}) async-start(), calls=%async_computation | async-start | bytes 4718592 | tf_op jit(solution)/shard_map/all_gather | solution.py:245
  7.3 181.5 %all-gather.5.cloned.1.call-start = ((), (), s32[]{:S(2)}) async-start(), calls=%async_computation.1 | async-start | bytes 4456448 | tf_op jit(solution)/shard_map/all_gather | solution.py:246
  8.4 21.8 %collective-permute-start.2 = (f32[64,1024]{1,0:T(8,128)S(1)}, f32[64,1024]{1,0:T(8,128)S(1)}, u32[]{:S(2)}, u32[]{:S(2)}) collective-permute-start(f32[64,1024]{1,0:T(8,128)S(1)} %get-tuple-element.9), channel_id=1, source_target_pairs={{0,128},{1,144},{2,160},{3,176},{4,192},{5,208},{6,224},{7,240},{8... | collective-permute-start | bytes 786440 | tf_op jit(solution)/shard_map/ppermute | solution.py:63
  21.0 11.1 %collective-permute-start = (f32[64,1024]{1,0:T(8,128)S(1)}, f32[64,1024]{1,0:T(8,128)S(1)}, u32[]{:S(2)}, u32[]{:S(2)}) collective-permute-start(f32[64,1024]{1,0:T(8,128)S(1)} %get-tuple-element.9), channel_id=1, source_target_pairs={{0,0},{1,16},{2,32},{3,48},{4,64},{5,80},{6,96},{7,112},{8,1},{9,1... | collective-permute-start | bytes 786440 | tf_op jit(solution)/shard_map/ppermute | solution.py:63
  23.0 15.6 %collective-permute-start.3 = (f32[64,1024]{1,0:T(8,128)S(1)}, f32[64,1024]{1,0:T(8,128)S(1)}, u32[]{:S(2)}, u32[]{:S(2)}) collective-permute-start(f32[64,1024]{1,0:T(8,128)S(1)} %get-tuple-element.10), channel_id=1, source_target_pairs={{0,136},{1,152},{2,168},{3,184},{4,200},{5,216},{6,232},{7,248},{8... | collective-permute-start | bytes 786440 | tf_op jit(solution)/shard_map/ppermute | solution.py:63
  24.3 14.3 %collective-permute-start.1 = (f32[64,1024]{1,0:T(8,128)S(1)}, f32[64,1024]{1,0:T(8,128)S(1)}, u32[]{:S(2)}, u32[]{:S(2)}) collective-permute-start(f32[64,1024]{1,0:T(8,128)S(1)} %get-tuple-element.10), channel_id=1, source_target_pairs={{0,8},{1,24},{2,40},{3,56},{4,72},{5,88},{6,104},{7,120},{8,9},{9,... | collective-permute-start | bytes 786440 | tf_op jit(solution)/shard_map/ppermute | solution.py:63
  40.4 20.7 %collective-permute-start.5 = (f32[128,512]{1,0:T(8,128)S(1)}, f32[128,512]{1,0:T(8,128)S(1)}, u32[]{:S(2)}, u32[]{:S(2)}) collective-permute-start(f32[128,512]{1,0:T(8,128)S(1)} %slice_select_fusion), channel_id=1, source_target_pairs={{0,24},{1,25},{2,26},{3,27},{4,28},{5,29},{6,30},{7,31}} | collective-permute-start | bytes 786440 | tf_op jit(solution)/shard_map/ppermute | solution.py:31
  51.0 12.3 %collective-permute-start.6 = (f32[128,512]{1,0:T(8,128)S(1)}, f32[128,512]{1,0:T(8,128)S(1)}, u32[]{:S(2)}, u32[]{:S(2)}) collective-permute-start(f32[128,512]{1,0:T(8,128)S(1)} %slice_select_fusion), channel_id=1, source_target_pairs={{0,16},{1,17},{2,18},{3,19},{4,20},{5,21},{6,22},{7,23}} | collective-permute-start | bytes 786440 | tf_op jit(solution)/shard_map/ppermute | solution.py:31
  55.0 15.6 %collective-permute-start.4 = (f32[128,512]{1,0:T(8,128)S(1)}, f32[128,512]{1,0:T(8,128)S(1)}, u32[]{:S(2)}, u32[]{:S(2)}) collective-permute-start(f32[128,512]{1,0:T(8,128)S(1)} %slice_select_fusion), channel_id=1, source_target_pairs={{0,8},{1,9},{2,10},{3,11},{4,12},{5,13},{6,14},{7,15}} | collective-permute-start | bytes 786440 | tf_op jit(solution)/shard_map/ppermute | solution.py:31
  71.6 5.6 %collective-permute-start.9 = (f32[128,512]{1,0:T(8,128)S(1)}, f32[128,512]{1,0:T(8,128)S(1)}, u32[]{:S(2)}, u32[]{:S(2)}) collective-permute-start(f32[128,512]{1,0:T(8,128)S(1)} %add_add_fusion.1), channel_id=1, source_target_pairs={{0,64},{1,65},{2,66},{3,67},{4,68},{5,69},{6,70},{7,71},{8,72},{9,... | collective-permute-start | bytes 786440 | tf_op jit(solution)/shard_map/ppermute | solution.py:31
  72.9 5.6 %collective-permute-start.8 = (f32[128,512]{1,0:T(8,128)S(1)}, f32[128,512]{1,0:T(8,128)S(1)}, u32[]{:S(2)}, u32[]{:S(2)}) collective-permute-start(f32[128,512]{1,0:T(8,128)S(1)} %add_add_fusion.1), channel_id=1, source_target_pairs={{0,96},{1,97},{2,98},{3,99},{4,100},{5,101},{6,102},{7,103},{8,104... | collective-permute-start | bytes 786440 | tf_op jit(solution)/shard_map/ppermute | solution.py:31
  74.2 8.6 %collective-permute-start.7 = (f32[128,512]{1,0:T(8,128)S(1)}, f32[128,512]{1,0:T(8,128)S(1)}, u32[]{:S(2)}, u32[]{:S(2)}) collective-permute-start(f32[128,512]{1,0:T(8,128)S(1)} %add_add_fusion.1), channel_id=1, source_target_pairs={{0,32},{1,33},{2,34},{3,35},{4,36},{5,37},{6,38},{7,39},{8,40},{9,... | collective-permute-start | bytes 786440 | tf_op jit(solution)/shard_map/ppermute | solution.py:31
  82.9 12.4 %collective-permute-start.10 = (f32[128,512]{1,0:T(8,128)S(1)}, f32[128,512]{1,0:T(8,128)S(1)}, u32[]{:S(2)}, u32[]{:S(2)}) collective-permute-start(f32[128,512]{1,0:T(8,128)S(1)} %add_add_fusion), channel_id=1, source_target_pairs={{0,128},{1,129},{2,130},{3,131},{4,132},{5,133},{6,134},{7,135},{8... | collective-permute-start | bytes 786440 | tf_op jit(solution)/shard_map/ppermute | solution.py:31
  95.3 20.5 %collective-permute-start.13 = (f32[128,512]{1,0:T(8,128)S(1)}, f32[128,512]{1,0:T(8,128)S(1)}, u32[]{:S(2)}, u32[]{:S(2)}) collective-permute-start(f32[128,512]{1,0:T(8,128)S(1)} %add.67), channel_id=1, source_target_pairs={{0,6},{2,0},{4,2},{6,4},{1,7},{3,1},{5,3},{7,5},{8,14},{10,8},{12,... | collective-permute-start | bytes 786440 | tf_op jit(solution)/shard_map/ppermute | solution.py:44
  100.2 37.0 %collective-permute-start.12 = (f32[128,512]{1,0:T(8,128)S(1)}, f32[128,512]{1,0:T(8,128)S(1)}, u32[]{:S(2)}, u32[]{:S(2)}) collective-permute-start(f32[128,512]{1,0:T(8,128)S(1)} %add.67), channel_id=1, source_target_pairs={{0,4},{2,6},{4,0},{6,2},{1,5},{3,7},{5,1},{7,3},{8,12},{10,14},{12... | collective-permute-start | bytes 786440 | tf_op jit(solution)/shard_map/ppermute | solution.py:44
  114.4 22.8 %collective-permute-start.11 = (f32[128,512]{1,0:T(8,128)S(1)}, f32[128,512]{1,0:T(8,128)S(1)}, u32[]{:S(2)}, u32[]{:S(2)}) collective-permute-start(f32[128,512]{1,0:T(8,128)S(1)} %add.67), channel_id=1, source_target_pairs={{0,2},{2,4},{4,6},{6,0},{1,3},{3,5},{5,7},{7,1},{8,10},{10,12},{12... | collective-permute-start | bytes 786440 | tf_op jit(solution)/shard_map/ppermute | solution.py:44
  137.3 3.6 %copy-start = (f32[4,128,512]{2,1,0:T(8,128)}, f32[4,128,512]{2,1,0:T(8,128)S(1)}, u32[]{:S(2)}) copy-start(f32[4,128,512]{2,1,0:T(8,128)S(1)} %pad_maximum_fusion.mine_ref) | copy-start | bytes 3145732
  137.4 3.6 %collective-permute-start.14 = (f32[4,128,512]{2,1,0:T(8,128)S(1)}, f32[4,128,512]{2,1,0:T(8,128)S(1)}, u32[]{:S(2)}, u32[]{:S(2)}) collective-permute-start(f32[4,128,512]{2,1,0:T(8,128)S(1)} %pad_maximum_fusion.mine_ref), channel_id=1, source_target_pairs={{0,1},{1,0},{2,3},{3,2},{4,5},{5,4},{6,7},{7,6},{8,9},{9,8},{10,11... | collective-permute-start | bytes 3145736 | tf_op jit(solution)/shard_map/ppermute | solution.py:45
  140.9 1.0 copy-start.1
Sparse Core Ops, SparseCore 0:
  9.1 94.1 all-gather.2
  105.7 60.1 all-gather.4

commit v3 on v2

v3 whole, which is shorter than its diff:
```python
import functools
import itertools

import jax
import jax.numpy as jnp
from jax import lax
from jax.experimental import pallas as pl
from jax.experimental.pallas import tpu as pltpu
from jax.sharding import Mesh
from jax.sharding import PartitionSpec as P


BLOCK = 512
SUB = 128
TILE = 256
PIECES = 8
LEAD_SHIFTS = (0, 1, 3, 2)
ROW_SHIFTS = (0, 1, 2, 3)
AXES = ("zh", "y", "x", "zl", "core")
SIZES = (2, 4, 4, 4, 2)
ROW = ("zh", "y", "x")
COL = ("zl", "core")


def device_id(zh, y, x, zl, core):
    return (((zh * 4 + y) * 4 + x) * 4 + zl) * 2 + core


def ring(n, shift):
    return [(i, (i + shift) % n) for i in range(n)]


def permute_rows(value, moves):
    columns = [(zl, core) for zl in range(4) for core in range(2)]
    values = value if isinstance(value, list) else [value] * len(moves)
    return [
        lax.ppermute(values[i], AXES, [(device_id(*s, *c), device_id(*t, *c)) for s, t in move for c in columns])
        for i, move in enumerate(moves)
    ]


def total(values):
    return functools.reduce(jnp.add, values)


def spread_lead(design, is_root):
    quarters = jnp.split(jnp.where(is_root, design[:, :BLOCK], 0.0), 4)
    others = (1, 3, 2)
    mine = quarters[0] + total(permute_rows([quarters[x] for x in others], [[((0, 0, 0), (0, 0, x))] for x in others]))
    mine = mine + total(permute_rows(mine, [[((0, 0, x), (0, y, x)) for x in range(4)] for y in others]))
    mine = mine + total(permute_rows(mine, [[((0, y, x), (1, y, x)) for y in range(4) for x in range(4)]]))
    mine = jnp.concatenate([mine] + [lax.ppermute(mine, "x", ring(4, k)) for k in LEAD_SHIFTS[1:]])
    line = [mine]
    for k in LEAD_SHIFTS[1:]:
        pairs = []
        for y, x, z, core in itertools.product(range(4), range(4), range(8), range(2)):
            to = (z + (-k if k == 2 and core else k)) % 8
            pairs.append((device_id(z // 4, y, x, z % 4, core), device_id(to // 4, y, x, to % 4, core)))
        line.append(lax.ppermute(mine, AXES, pairs))
    return swap_cores(line)


def swap_cores(line):
    return line + [lax.ppermute(piece, "core", ring(2, 1)) for piece in line]


def gather_rows(design):
    return swap_cores([design] + [lax.ppermute(design, "zl", ring(4, k)) for k in ROW_SHIFTS[1:]])


def places(shifts):
    zl, core = lax.axis_index("zl"), lax.axis_index("core")
    chip = (zl + 4 - jnp.array(shifts, jnp.int32)) & 3
    return jnp.concatenate([2 * chip + core, 2 * chip + 1 - core])


def inverse_of(place):
    index = jnp.arange(PIECES, dtype=jnp.int32)
    return jnp.sum(jnp.where(place[None, :] == index[:, None], index[None, :], 0), axis=1)


def scatter_columns(design):
    halves = jnp.split(design, 2)
    planes = []
    for j in range(2):
        pairs = []
        for c, k in itertools.product(range(8), range(8)):
            p = (2 * (k + c) + j) % 16
            pairs.append((device_id(0, c // 4, c % 4, k // 2, k % 2), device_id(0, p // 4, p % 4, k // 2, k % 2)))
        planes.append(lax.ppermute(halves[j], AXES, pairs))
    mine = planes[0] + planes[1]
    lines = []
    for zh in range(2):
        pairs = []
        for p, k in itertools.product(range(16), range(8)):
            c = (p // 2 - k) % 8
            pairs.append((device_id(0, p // 4, p % 4, k // 2, k % 2), device_id(zh, p // 4, p % 4, c // 2, c % 2)))
        lines.append(lax.ppermute(mine, AXES, pairs))
    return lines[0] + lines[1]


def dot(a, b, dims, precision=None):
    return lax.dot_general(a, b, (dims, ((), ())), precision=precision, preferred_element_type=jnp.float32)


def split(a):
    high = a.astype(jnp.bfloat16)
    return high, (a - high.astype(jnp.float32)).astype(jnp.bfloat16)


def dot3(a, b, dims):
    return dot(a[0], b[0], dims) + (dot(a[0], b[1], dims) + dot(a[1], b[0], dims))


def eliminate(m_ref):
    lane = lax.broadcasted_iota(jnp.int32, (8, SUB), 1)
    sub = lax.broadcasted_iota(jnp.int32, (8, SUB), 0)
    for o in range(0, SUB, 8):
        left = [jnp.broadcast_to(m_ref[o + i : o + i + 1, :SUB], (8, SUB)) for i in range(8)]
        right = [jnp.broadcast_to(m_ref[o + i : o + i + 1, SUB:], (8, SUB)) for i in range(8)]
        e = {
            (i, j): jnp.broadcast_to(left[i][:, o + j : o + j + 1], (8, SUB)) for i in range(8) for j in range(i, 8)
        }
        strip_left = jnp.zeros((8, SUB), jnp.float32)
        strip_right = strip_left
        for i in range(8):
            r = lax.rsqrt(e[i, i])
            for j in range(i + 1, 8):
                e[i, j] = e[i, j] * r
            for j in range(i + 1, 8):
                for k in range(j, 8):
                    e[j, k] = e[j, k] - e[i, j] * e[i, k]
            a, b = left[i] * r, right[i] * r
            for j in range(i + 1, 8):
                left[j] = left[j] - e[i, j] * a
                right[j] = right[j] - e[i, j] * b
            strip_left = jnp.where(sub == i, a, strip_left)
            strip_right = jnp.where(sub == i, b, strip_right)
        m_ref[o : o + 8, :SUB] = strip_left
        m_ref[o : o + 8, SUB:] = strip_right
        if o + 8 < SUB:
            masked = jnp.where(lane >= o + 8, strip_left, 0.0)
            strip = jnp.concatenate([strip_left, strip_right], axis=1)
            update = dot(masked, strip, ((0,), (0,)), lax.Precision.HIGHEST)
            m_ref[o + 8 :, :] = m_ref[o + 8 :, :] - update[o + 8 :, :]


def lead_kernel(place_ref, *refs):
    pieces, (damping_ref, white_ref, inverse_ref, g_ref, m_ref) = refs[:PIECES], refs[PIECES:]
    highest = lax.Precision.HIGHEST
    depth = pieces[0].shape[0]
    same = lax.broadcasted_iota(jnp.int32, (BLOCK, BLOCK), 0) == lax.broadcasted_iota(jnp.int32, (BLOCK, BLOCK), 1)
    gram = jnp.where(same, damping_ref[...], 0.0)
    for i in range(0, PIECES, 4):
        stack = jnp.concatenate([ref[...] for ref in pieces[i : i + 4]])
        gram = gram + dot(stack, stack, ((0,), (0,)), highest)
    g_ref[:, :BLOCK] = gram
    g_ref[:, BLOCK:] = jnp.where(same, 1.0, 0.0)

    def step(p, carry):
        start = pl.multiple_of(p * SUB, SUB)
        m_ref[:, :SUB] = g_ref[pl.ds(start, SUB), pl.ds(start, SUB)]
        m_ref[:, SUB:] = jnp.where(same[:SUB, :SUB], 1.0, 0.0)
        eliminate(m_ref)
        inverse = m_ref[:, SUB:]
        for q in range(BLOCK // SUB):

            @pl.when(p == q)
            def _():
                lo, hi = q * SUB, (q + 1) * SUB
                strip = dot(inverse, g_ref[lo:hi, hi : hi + BLOCK], ((1,), (0,)), highest)
                g_ref[lo:hi, hi : hi + BLOCK] = strip
                if hi < BLOCK:
                    g_ref[hi:BLOCK, hi : hi + BLOCK] = g_ref[hi:BLOCK, hi : hi + BLOCK] - dot(
                        strip[:, : BLOCK - hi], strip, ((0,), (0,)), highest
                    )

        return carry

    lax.fori_loop(0, BLOCK // SUB, step, 0)
    inverse = g_ref[:, BLOCK:]
    inverse_ref[...] = inverse * damping_ref[...]
    pair = split(inverse)
    for i, ref in enumerate(pieces):
        white = dot3(split(ref[...]), pair, ((1,), (1,)))
        part = depth // 4
        for x in range(4):
            start = pl.multiple_of(place_ref[i] * depth + place_ref[PIECES + x] * part, part)
            white_ref[pl.ds(start, part), :] = white[x * part : (x + 1) * part]


def lead_call(pieces, place, damping):
    vmem = pl.BlockSpec(memory_space=pltpu.VMEM)
    rows = PIECES * pieces[0].shape[0]
    return pl.pallas_call(
        lead_kernel,
        out_shape=(jax.ShapeDtypeStruct((rows, BLOCK), jnp.float32), jax.ShapeDtypeStruct((BLOCK, BLOCK), jnp.float32)),
        in_specs=[pl.BlockSpec(memory_space=pltpu.SMEM)] + [vmem] * (PIECES + 1),
        out_specs=(vmem, vmem),
        scratch_shapes=[pltpu.VMEM((BLOCK, 2 * BLOCK), jnp.float32), pltpu.VMEM((SUB, 2 * SUB), jnp.float32)],
        name="lead",
    )(place, *pieces, damping.reshape(1, BLOCK))


def apply_kernel(where_ref, *refs):
    pieces, (columns_ref, white_ref, inverse_ref, out_ref, wh, wl, vh, vl, rh, rl) = refs[:PIECES], refs[PIECES:]
    depth = pieces[0].shape[0]
    t = pl.program_id(0)
    tiles = out_ref.shape[1] // TILE
    is_root = where_ref[0] == 0
    has_panel = where_ref[1] == 0
    white = (wh, wl)

    def put(refs, value, index):
        refs[0][index], refs[1][index] = split(value)

    def get(refs, index=...):
        return refs[0][index], refs[1][index]

    def put_rows(value, columns):
        for k in range(PIECES):
            start = pl.multiple_of(where_ref[2 + k] * depth, depth)
            chunk = slice(k * depth, (k + 1) * depth)
            rh[pl.ds(start, depth), columns] = value[0][chunk]
            rl[pl.ds(start, depth), columns] = value[1][chunk]

    @pl.when(t == 0)
    def _():
        put(white, white_ref[...], ...)

    @pl.when(t < tiles)
    def _():
        here = pl.ds(pl.multiple_of(t * TILE, TILE), TILE)
        in_panel = has_panel & (t * TILE < BLOCK)

        @pl.when(jnp.logical_not(in_panel))
        def _():
            block = columns_ref[...]
            v = split(dot3(get(white), split(block), ((0,), (0,))))
            vh[:, here], vl[:, here] = v
            put_rows(split(block - dot3(get(white), v, ((1,), (0,)))), here)

        @pl.when(in_panel)
        def _():
            row = lax.broadcasted_iota(jnp.int32, (BLOCK, TILE), 0)
            column = lax.broadcasted_iota(jnp.int32, (BLOCK, TILE), 1) + t * TILE
            vh[:, here], vl[:, here] = split(jnp.where(row == column, -1.0, 0.0))
            put_rows((wh[:, here], wl[:, here]), here)

    @pl.when(t >= tiles)
    def _():
        rows = jnp.concatenate([ref[...] for ref in pieces])
        out_ref[...] = dot3(split(rows), get((rh, rl)), ((0,), (0,)))

    for i in range(BLOCK // TILE):

        @pl.when((t == tiles + i) & is_root)
        def _():
            scaled = split(inverse_ref[:, i * TILE : (i + 1) * TILE])
            out_ref[...] = out_ref[...] - dot3(scaled, get((vh, vl)), ((0,), (0,)))


def apply_call(where, pieces, columns, white, inverse):
    depth, size = columns.shape
    tiles = size // TILE
    bf16 = jnp.bfloat16
    grid_spec = pltpu.PrefetchScalarGridSpec(
        num_scalar_prefetch=1,
        grid=(2 * tiles,),
        in_specs=[
            pl.BlockSpec((depth // PIECES, TILE), lambda t, w: (0, jnp.maximum(t - tiles, 0)))
            for _ in range(PIECES)
        ]
        + [
            pl.BlockSpec((depth, TILE), lambda t, w: (0, jnp.minimum(t, tiles - 1))),
            pl.BlockSpec((depth, BLOCK), lambda t, w: (0, 0)),
            pl.BlockSpec((BLOCK, BLOCK), lambda t, w: (0, 0)),
        ],
        out_specs=pl.BlockSpec((TILE, size), lambda t, w: (jnp.maximum(t - tiles, 0), 0)),
        scratch_shapes=[pltpu.VMEM((depth, BLOCK), bf16)] * 2
        + [pltpu.VMEM((BLOCK, size), bf16)] * 2
        + [pltpu.VMEM((depth, size), bf16)] * 2,
    )
    return pl.pallas_call(
        apply_kernel, grid_spec=grid_spec, out_shape=jax.ShapeDtypeStruct((size, size), jnp.float32), name="apply"
    )(where, *pieces, columns, white, inverse)


def per_device(design, damping):
    row = lax.axis_index(ROW)
    col = lax.axis_index(COL)
    quarter = (lax.axis_index("x") + 4 - jnp.array(LEAD_SHIFTS, jnp.int32)) & 3
    place = jnp.concatenate([(places(LEAD_SHIFTS) + col) & 7, quarter]).astype(jnp.int32)
    slots = inverse_of((places(ROW_SHIFTS) + col) & 7)
    where = jnp.concatenate([jnp.stack([row, col]), slots]).astype(jnp.int32)
    columns = lax.all_gather(scatter_columns(design), ("y", "x"), tiled=True)
    lead = spread_lead(design, row == 0)
    rows = gather_rows(design)
    white, inverse = lead_call(lead, place, damping)
    return apply_call(where, rows, columns, white, inverse)


def solution(mesh):
    fine = Mesh(mesh.devices.reshape(SIZES), AXES)
    return jax.shard_map(per_device, mesh=fine, in_specs=(P(COL, ROW), P()), out_specs=P(ROW, COL), check_vma=False)
```

time: 224 us -> 235 us (1.049)
  the two profiles are of different devices: /device:TPU:1 before, /device:TPU:65 now
where the time goes in v3:
time: 235 us
  Pallas kernels  75.6 us (32%)
  waiting for transfers between devices  72.2 us (31%)
  starting transfers between devices  68.1 us (29%)
  between operations  13.7 us (6%)
  other arithmetic  3.23 us (1%)
    pallas_call x1, Pallas kernels, lead_call(): pl.pallas_call(lead_kernel, out_shape=(jax.ShapeDtypeStruct((rows, BLOCK)...  46.8 us
    ppermute x3, waiting for transfers between devices, spread_lead(): line.append(lax.ppermute(mine, AXES, pairs))  41.9 us
    ppermute x8, starting transfers between devices, swap_cores(): return line + [lax.ppermute(piece, 'core', ring(2, 1)) for piece in line]  31 us
    pallas_call x1, Pallas kernels, apply_call(): pl.pallas_call(apply_kernel, grid_spec=grid_spec, out_shape=jax.ShapeDtyp...  28.8 us
    ppermute x7, starting transfers between devices, permute_rows(): lax.ppermute(values[i], AXES, [(device_id(*s, *c), device_id(*t, *c)) for...  12.3 us
    ppermute x2, waiting for transfers between devices, scatter_columns(): lines.append(lax.ppermute(mine, AXES, pairs))  10.4 us
    ppermute x2, starting transfers between devices, scatter_columns(): planes.append(lax.ppermute(halves[j], AXES, pairs))  8.95 us
    ppermute x2, waiting for transfers between devices, scatter_columns(): planes.append(lax.ppermute(halves[j], AXES, pairs))  8.46 us
  transfers between devices with their start and end apart: 29, of which 14 were waited for; matrix products, arithmetic and copies ran while one was open for 1% of the time, Pallas kernels for 20%

profile of v3, /device:TPU:65, one launch (start us, length us, event | category | flops | bytes accessed | tf_op | source)
XLA Modules:
  0.0 234.9 jit_solution(18182387029605178692)
XLA Ops:
  7.7 7.0 %collective-permute-start.8 = (f32[64,1024]{1,0:T(8,128)S(1)}, f32[64,1024]{1,0:T(8,128)S(1)}, u32[]{:S(2)}, u32[]{:S(2)}) collective-permute-start(f32[64,1024]{1,0:T(8,128)S(1)} %get-tuple-element.9), channel_id=1, source_target_pairs={{0,8},{1,25},{2,42},{3,59},{4,76},{5,93},{6,110},{7,127},{8,24},{9... | collective-permute-start | bytes 786440 | tf_op jit(solution)/shard_map/ppermute | solution.py:90
  14.7 1.9 collective-permute-start.7
  16.6 2.6 %collective-permute-done.8 = f32[64,1024]{1,0:T(8,128)S(1)} collective-permute-done((f32[64,1024]{1,0:T(8,128)S(1)}, f32[64,1024]{1,0:T(8,128)S(1)}, u32[]{:S(2)}, u32[]{:S(2)}) %collective-permute-start.8) | collective-permute-done | bytes 262176 | tf_op jit(solution)/shard_map/ppermute | solution.py:90
  19.2 5.9 %collective-permute-done.7 = f32[64,1024]{1,0:T(8,128)S(1)} collective-permute-done((f32[64,1024]{1,0:T(8,128)S(1)}, f32[64,1024]{1,0:T(8,128)S(1)}, u32[]{:S(2)}, u32[]{:S(2)}) %collective-permute-start.7) | collective-permute-done | bytes 262176 | tf_op jit(solution)/shard_map/ppermute | solution.py:90
  25.1 1.3 collective-permute-start.10
  26.4 1.9 collective-permute-start.9
  28.4 2.0 collective-permute-done.10
  30.3 8.5 %collective-permute-done.9 = f32[64,1024]{1,0:T(8,128)S(1)} collective-permute-done((f32[64,1024]{1,0:T(8,128)S(1)}, f32[64,1024]{1,0:T(8,128)S(1)}, u32[]{:S(2)}, u32[]{:S(2)}) %collective-permute-start.9) | collective-permute-done | bytes 262176 | tf_op jit(solution)/shard_map/ppermute | solution.py:98
  40.6 3.9 %collective-permute-start.12 = (f32[32,512]{1,0:T(8,128)S(1)}, f32[32,512]{1,0:T(8,128)S(1)}, u32[]{:S(2)}, u32[]{:S(2)}) collective-permute-start(f32[32,512]{1,0:T(8,128)S(1)} %get-tuple-element.11), channel_id=1, source_target_pairs={{0,24},{1,25},{2,26},{3,27},{4,28},{5,29},{6,30},{7,31}} | collective-permute-start | bytes 196616 | tf_op jit(solution)/shard_map/ppermute | solution.py:37
  44.5 1.9 collective-permute-start.13
  46.4 1.3 collective-permute-start.11
  47.7 1.5 collective-permute-done.11
  49.2 1.3 collective-permute-start.16
  50.5 1.3 collective-permute-start.15
  51.8 1.3 collective-permute-start.14
  55.8 1.3 collective-permute-done.17
  57.1 2.0 collective-permute-start.20
  59.1 2.8 %collective-permute-start.19 = (f32[32,512]{1,0:T(8,128)S(1)}, f32[32,512]{1,0:T(8,128)S(1)}, u32[]{:S(2)}, u32[]{:S(2)}) collective-permute-start(f32[32,512]{1,0:T(8,128)S(1)} %add.94), channel_id=1, source_target_pairs={{0,24},{8,0},{16,8},{24,16},{1,25},{9,1},{17,9},{25,17},{2,26},{10... | collective-permute-start | bytes 196616 | tf_op jit(solution)/shard_map/ppermute | solution.py:52
  63.1 1.6 collective-permute-done.19
  64.6 2.8 %collective-permute-done.18 = f32[32,512]{1,0:T(8,128)S(1)} collective-permute-done((f32[32,512]{1,0:T(8,128)S(1)}, f32[32,512]{1,0:T(8,128)S(1)}, u32[]{:S(2)}, u32[]{:S(2)}) %collective-permute-start.18) | collective-permute-done | bytes 65568 | tf_op jit(solution)/shard_map/ppermute | solution.py:52
  67.5 3.1 %collective-permute-start.24 = (f32[128,512]{1,0:T(8,128)S(1)}, f32[128,512]{1,0:T(8,128)S(1)}, u32[]{:S(2)}, u32[]{:S(2)}) collective-permute-start(f32[128,512]{1,0:T(8,128)S(1)} %pad_maximum_fusion.refs_0_), channel_id=1, source_target_pairs={{0,1},{1,0},{2,3},{3,2},{4,5},{5,4},{6,7},{7,6},{8,9},{9,8},{10,11... | collective-permute-start | bytes 786440 | tf_op jit(solution)/shard_map/ppermute | solution.py:64
  70.6 2.7 %collective-permute-start.22 = (f32[128,512]{1,0:T(8,128)S(1)}, f32[128,512]{1,0:T(8,128)}, u32[]{:S(2)}, u32[]{:S(2)}) collective-permute-start(f32[128,512]{1,0:T(8,128)S(1)} %pad_maximum_fusion.refs_0_), channel_id=1, source_target_pairs={{0,6},{1,7},{2,128},{3,129},{4,130},{5,131},{6,132},{7,133},{128,1... | collective-permute-start | bytes 786440 | tf_op jit(solution)/shard_map/ppermute | solution.py:59
  73.4 2.0 collective-permute-start.2
  75.4 3.2 %collective-permute-start.1 = (f32[128,1024]{1,0:T(8,128)S(1)}, f32[128,1024]{1,0:T(8,128)S(1)}, u32[]{:S(2)}, u32[]{:S(2)}) collective-permute-start(f32[128,1024]{1,0:T(8,128)S(1)} %copy-done), channel_id=1, source_target_pairs={{0,4},{2,6},{4,0},{6,2},{1,5},{3,7},{5,1},{7,3},{8,12},{10,14},{12... | collective-permute-start | bytes 1572872 | tf_op jit(solution)/shard_map/ppermute | solution.py:68
  78.6 1.6 collective-permute-done.23.refs_3_
  80.1 4.0 %collective-permute-done.22.refs_2_ = f32[128,512]{1,0:T(8,128)} collective-permute-done((f32[128,512]{1,0:T(8,128)S(1)}, f32[128,512]{1,0:T(8,128)}, u32[]{:S(2)}, u32[]{:S(2)}) %collective-permute-start.22) | collective-permute-done | bytes 262176 | tf_op jit(solution)/shard_map/ppermute | solution.py:59
  84.1 24.5 %collective-permute-start.27 = (f32[128,512]{1,0:T(8,128)}, f32[128,512]{1,0:T(8,128)}, u32[]{:S(2)}, u32[]{:S(2)}) collective-permute-start(f32[128,512]{1,0:T(8,128)} %collective-permute-done.23.refs_3_), channel_id=1, source_target_pairs={{0,1},{1,0},{2,3},{3,2},{4,5},{5,4},{6,7},{7,6},{8,9},{9,8},{10,11... | collective-permute-start | bytes 786440 | tf_op jit(solution)/shard_map/ppermute | solution.py:64
  108.7 36.4 %collective-permute-done.21.refs_1_ = f32[128,512]{1,0:T(8,128)S(1)} collective-permute-done((f32[128,512]{1,0:T(8,128)S(1)}, f32[128,512]{1,0:T(8,128)S(1)}, u32[]{:S(2)}, u32[]{:S(2)}) %collective-permute-start.21) | collective-permute-done | bytes 262176 | tf_op jit(solution)/shard_map/ppermute | solution.py:59
  145.0 1.4 collective-permute-start.26
  149.8 1.6 collective-permute-done.25.refs_5_
  151.4 46.8 %lead.1 = (f32[1024,512]{1,0:T(8,128)}, f32[512,512]{1,0:T(8,128)}) custom-call(s32[12]{0:T(128)} %pad_add_fusion.1.place_ref, f32[128,512]{1,0:T(8,128)} %copy-done.1, f32[128,512]{1,0:T(8,128)} %copy-done.8, f32[128,512]{1,0:T(8,128)} %collective-permute-done.22.refs_2_, f32[128,512]{1,0:T(8,128)} %collective-permute-done.23.refs_3_, ...), custom_call_target="tpu_custom_call" | custom-call | tf_op jit(solution)/shard_map/lead/pallas_call | solution.py:195
  199.2 28.8 %apply.1 = f32[1024,1024]{1,0:T(8,128)} custom-call(s32[10]{0:T(128)} %pad_add_fusion.where_ref, f32[128,1024]{1,0:T(8,128)} %refs_0_.1, f32[128,1024]{1,0:T(8,128)} %copy-done.4, f32[128,1024]{1,0:T(8,128)} %copy-done.3, f32[128,1024]{1,0:T(8,128)} %copy-done.2, f32[128,1024]{1,0:T(8,128)} %copy-done.5, f32[128,1024]{1,0:T(8,128)} %collective-permute-done.4.refs_5_, ...), custom_call_target="tpu_custom_call" | custom-call | tf_op jit(solution)/shard_map/apply/pallas_call | solution.py:284
  (65 shorter events, 11.1 us)
Async XLA Ops:
  6.5 102.1 %copy-start.9 = (s32[4]{0:T(128)S(1)}, s32[4]{0:T(128)}, u32[]{:S(2)}) copy-start(s32[4]{0:T(128)} %constant.41) | copy-start | bytes 52
  6.5 66.8 %copy-start = (f32[128,1024]{1,0:T(8,128)S(1)}, f32[128,1024]{1,0:T(8,128)}, u32[]{:S(2)}) copy-start(f32[128,1024]{1,0:T(8,128)} %refs_0_.1) | copy-start | bytes 1572868
  6.5 191.7 %all-gather.2.cloned.1.call-start = ((), (), s32[]{:S(2)}) async-start(), calls=%async_computation | async-start | bytes 4456448 | tf_op jit(solution)/shard_map/all_gather | solution.py:296
  7.7 11.6 %collective-permute-start.8 = (f32[64,1024]{1,0:T(8,128)S(1)}, f32[64,1024]{1,0:T(8,128)S(1)}, u32[]{:S(2)}, u32[]{:S(2)}) collective-permute-start(f32[64,1024]{1,0:T(8,128)S(1)} %get-tuple-element.9), channel_id=1, source_target_pairs={{0,8},{1,25},{2,42},{3,59},{4,76},{5,93},{6,110},{7,127},{8,24},{9... | collective-permute-start | bytes 786440 | tf_op jit(solution)/shard_map/ppermute | solution.py:90
  14.7 10.4 %collective-permute-start.7 = (f32[64,1024]{1,0:T(8,128)S(1)}, f32[64,1024]{1,0:T(8,128)S(1)}, u32[]{:S(2)}, u32[]{:S(2)}) collective-permute-start(f32[64,1024]{1,0:T(8,128)S(1)} %get-tuple-element.10), channel_id=1, source_target_pairs={{0,0},{1,17},{2,34},{3,51},{4,68},{5,85},{6,102},{7,119},{8,16},{9... | collective-permute-start | bytes 786440 | tf_op jit(solution)/shard_map/ppermute | solution.py:90
  25.1 5.2 %collective-permute-start.10 = (f32[64,1024]{1,0:T(8,128)S(1)}, f32[64,1024]{1,0:T(8,128)S(1)}, u32[]{:S(2)}, u32[]{:S(2)}) collective-permute-start(f32[64,1024]{1,0:T(8,128)S(1)} %add.82), channel_id=1, source_target_pairs={{0,128},{1,135},{2,134},{3,133},{4,132},{5,131},{6,130},{7,129},{8... | collective-permute-start | bytes 786440 | tf_op jit(solution)/shard_map/ppermute | solution.py:98
  26.4 12.4 %collective-permute-start.9 = (f32[64,1024]{1,0:T(8,128)S(1)}, f32[64,1024]{1,0:T(8,128)S(1)}, u32[]{:S(2)}, u32[]{:S(2)}) collective-permute-start(f32[64,1024]{1,0:T(8,128)S(1)} %add.82), channel_id=1, source_target_pairs={{0,0},{1,7},{2,6},{3,5},{4,4},{5,3},{6,2},{7,1},{8,8},{9,15},{10,1... | collective-permute-start | bytes 786440 | tf_op jit(solution)/shard_map/ppermute | solution.py:98
  40.6 7.1 %collective-permute-start.12 = (f32[32,512]{1,0:T(8,128)S(1)}, f32[32,512]{1,0:T(8,128)S(1)}, u32[]{:S(2)}, u32[]{:S(2)}) collective-permute-start(f32[32,512]{1,0:T(8,128)S(1)} %get-tuple-element.11), channel_id=1, source_target_pairs={{0,24},{1,25},{2,26},{3,27},{4,28},{5,29},{6,30},{7,31}} | collective-permute-start | bytes 196616 | tf_op jit(solution)/shard_map/ppermute | solution.py:37
  44.5 3.2 %collective-permute-start.13 = (f32[32,512]{1,0:T(8,128)S(1)}, f32[32,512]{1,0:T(8,128)S(1)}, u32[]{:S(2)}, u32[]{:S(2)}) collective-permute-start(f32[32,512]{1,0:T(8,128)S(1)} %get-tuple-element.12), channel_id=1, source_target_pairs={{0,16},{1,17},{2,18},{3,19},{4,20},{5,21},{6,22},{7,23}} | collective-permute-start | bytes 196616 | tf_op jit(solution)/shard_map/ppermute | solution.py:37
  46.4 2.8 %collective-permute-start.11 = (f32[32,512]{1,0:T(8,128)S(1)}, f32[32,512]{1,0:T(8,128)S(1)}, u32[]{:S(2)}, u32[]{:S(2)}) collective-permute-start(f32[32,512]{1,0:T(8,128)S(1)} %get-tuple-element.13), channel_id=1, source_target_pairs={{0,8},{1,9},{2,10},{3,11},{4,12},{5,13},{6,14},{7,15}} | collective-permute-start | bytes 196616 | tf_op jit(solution)/shard_map/ppermute | solution.py:37
  49.2 3.9 %collective-permute-start.16 = (f32[32,512]{1,0:T(8,128)S(1)}, f32[32,512]{1,0:T(8,128)S(1)}, u32[]{:S(2)}, u32[]{:S(2)}) collective-permute-start(f32[32,512]{1,0:T(8,128)S(1)} %slice_add_fusion), channel_id=1, source_target_pairs={{0,64},{1,65},{2,66},{3,67},{4,68},{5,69},{6,70},{7,71},{8,72},{9,... | collective-permute-start | bytes 196616 | tf_op jit(solution)/shard_map/ppermute | solution.py:37
  50.5 2.6 %collective-permute-start.15 = (f32[32,512]{1,0:T(8,128)S(1)}, f32[32,512]{1,0:T(8,128)S(1)}, u32[]{:S(2)}, u32[]{:S(2)}) collective-permute-start(f32[32,512]{1,0:T(8,128)S(1)} %slice_add_fusion), channel_id=1, source_target_pairs={{0,96},{1,97},{2,98},{3,99},{4,100},{5,101},{6,102},{7,103},{8,104... | collective-permute-start | bytes 196616 | tf_op jit(solution)/shard_map/ppermute | solution.py:37
  51.8 2.6 %collective-permute-start.14 = (f32[32,512]{1,0:T(8,128)S(1)}, f32[32,512]{1,0:T(8,128)S(1)}, u32[]{:S(2)}, u32[]{:S(2)}) collective-permute-start(f32[32,512]{1,0:T(8,128)S(1)} %slice_add_fusion), channel_id=1, source_target_pairs={{0,32},{1,33},{2,34},{3,35},{4,36},{5,37},{6,38},{7,39},{8,40},{9,... | collective-permute-start | bytes 196616 | tf_op jit(solution)/shard_map/ppermute | solution.py:37
  54.5 2.6 %collective-permute-start.17 = (f32[32,512]{1,0:T(8,128)S(1)}, f32[32,512]{1,0:T(8,128)S(1)}, u32[]{:S(2)}, u32[]{:S(2)}) collective-permute-start(f32[32,512]{1,0:T(8,128)S(1)} %add_add_fusion), channel_id=1, source_target_pairs={{0,128},{1,129},{2,130},{3,131},{4,132},{5,133},{6,134},{7,135},{8... | collective-permute-start | bytes 196616 | tf_op jit(solution)/shard_map/ppermute | solution.py:37
  57.1 6.0 %collective-permute-start.20 = (f32[32,512]{1,0:T(8,128)S(1)}, f32[32,512]{1,0:T(8,128)S(1)}, u32[]{:S(2)}, u32[]{:S(2)}) collective-permute-start(f32[32,512]{1,0:T(8,128)S(1)} %add.94), channel_id=1, source_target_pairs={{0,16},{8,24},{16,0},{24,8},{1,17},{9,25},{17,1},{25,9},{2,18},{10... | collective-permute-start | bytes 196616 | tf_op jit(solution)/shard_map/ppermute | solution.py:52
  59.1 5.5 %collective-permute-start.19 = (f32[32,512]{1,0:T(8,128)S(1)}, f32[32,512]{1,0:T(8,128)S(1)}, u32[]{:S(2)}, u32[]{:S(2)}) collective-permute-start(f32[32,512]{1,0:T(8,128)S(1)} %add.94), channel_id=1, source_target_pairs={{0,24},{8,0},{16,8},{24,16},{1,25},{9,1},{17,9},{25,17},{2,26},{10... | collective-permute-start | bytes 196616 | tf_op jit(solution)/shard_map/ppermute | solution.py:52
  61.9 5.6 %collective-permute-start.18 = (f32[32,512]{1,0:T(8,128)S(1)}, f32[32,512]{1,0:T(8,128)S(1)}, u32[]{:S(2)}, u32[]{:S(2)}) collective-permute-start(f32[32,512]{1,0:T(8,128)S(1)} %add.94), channel_id=1, source_target_pairs={{0,8},{8,16},{16,24},{24,0},{1,9},{9,17},{17,25},{25,1},{2,10},{10... | collective-permute-start | bytes 196616 | tf_op jit(solution)/shard_map/ppermute | solution.py:52
  67.5 83.9 %copy-start.1 = (f32[128,512]{1,0:T(8,128)}, f32[128,512]{1,0:T(8,128)S(1)}, u32[]{:S(2)}) copy-start(f32[128,512]{1,0:T(8,128)S(1)} %pad_maximum_fusion.refs_0_) | copy-start | bytes 786436
  67.5 11.1 %collective-permute-start.24 = (f32[128,512]{1,0:T(8,128)S(1)}, f32[128,512]{1,0:T(8,128)S(1)}, u32[]{:S(2)}, u32[]{:S(2)}) collective-permute-start(f32[128,512]{1,0:T(8,128)S(1)} %pad_maximum_fusion.refs_0_), channel_id=1, source_target_pairs={{0,1},{1,0},{2,3},{3,2},{4,5},{5,4},{6,7},{7,6},{8,9},{9,8},{10,11... | collective-permute-start | bytes 786440 | tf_op jit(solution)/shard_map/ppermute | solution.py:64
  70.6 9.5 %collective-permute-start.23 = (f32[128,512]{1,0:T(8,128)S(1)}, f32[128,512]{1,0:T(8,128)}, u32[]{:S(2)}, u32[]{:S(2)}) collective-permute-start(f32[128,512]{1,0:T(8,128)S(1)} %pad_maximum_fusion.refs_0_), channel_id=1, source_target_pairs={{0,4},{1,133},{2,6},{3,135},{4,128},{5,1},{6,130},{7,3},{128,132},... | collective-permute-start | bytes 786440 | tf_op jit(solution)/shard_map/ppermute | solution.py:59
  70.6 13.5 %collective-permute-start.22 = (f32[128,512]{1,0:T(8,128)S(1)}, f32[128,512]{1,0:T(8,128)}, u32[]{:S(2)}, u32[]{:S(2)}) collective-permute-start(f32[128,512]{1,0:T(8,128)S(1)} %pad_maximum_fusion.refs_0_), channel_id=1, source_target_pairs={{0,6},{1,7},{2,128},{3,129},{4,130},{5,131},{6,132},{7,133},{128,1... | collective-permute-start | bytes 786440 | tf_op jit(solution)/shard_map/ppermute | solution.py:59
  73.4 73.0 %collective-permute-start.2 = (f32[128,1024]{1,0:T(8,128)S(1)}, f32[128,1024]{1,0:T(8,128)S(1)}, u32[]{:S(2)}, u32[]{:S(2)}) collective-permute-start(f32[128,1024]{1,0:T(8,128)S(1)} %copy-done), channel_id=1, source_target_pairs={{0,6},{2,0},{4,2},{6,4},{1,7},{3,1},{5,3},{7,5},{8,14},{10,8},{12,... | collective-permute-start | bytes 1572872 | tf_op jit(solution)/shard_map/ppermute | solution.py:68
  75.4 71.7 %collective-permute-start.1 = (f32[128,1024]{1,0:T(8,128)S(1)}, f32[128,1024]{1,0:T(8,128)S(1)}, u32[]{:S(2)}, u32[]{:S(2)}) collective-permute-start(f32[128,1024]{1,0:T(8,128)S(1)} %copy-done), channel_id=1, source_target_pairs={{0,4},{2,6},{4,0},{6,2},{1,5},{3,7},{5,1},{7,3},{8,12},{10,14},{12... | collective-permute-start | bytes 1572872 | tf_op jit(solution)/shard_map/ppermute | solution.py:68
  78.5 68.7 %collective-permute-start = (f32[128,1024]{1,0:T(8,128)S(1)}, f32[128,1024]{1,0:T(8,128)S(1)}, u32[]{:S(2)}, u32[]{:S(2)}) collective-permute-start(f32[128,1024]{1,0:T(8,128)S(1)} %copy-done), channel_id=1, source_target_pairs={{0,2},{2,4},{4,6},{6,0},{1,3},{3,5},{5,7},{7,1},{8,10},{10,12},{12... | collective-permute-start | bytes 1572872 | tf_op jit(solution)/shard_map/ppermute | solution.py:68
  80.1 64.9 %collective-permute-start.21 = (f32[128,512]{1,0:T(8,128)S(1)}, f32[128,512]{1,0:T(8,128)S(1)}, u32[]{:S(2)}, u32[]{:S(2)}) collective-permute-start(f32[128,512]{1,0:T(8,128)S(1)} %pad_maximum_fusion.refs_0_), channel_id=1, source_target_pairs={{0,2},{1,3},{2,4},{3,5},{4,6},{5,7},{6,128},{7,129},{128,130},{129... | collective-permute-start | bytes 786440 | tf_op jit(solution)/shard_map/ppermute | solution.py:59
  84.1 63.5 %collective-permute-start.27 = (f32[128,512]{1,0:T(8,128)}, f32[128,512]{1,0:T(8,128)}, u32[]{:S(2)}, u32[]{:S(2)}) collective-permute-start(f32[128,512]{1,0:T(8,128)} %collective-permute-done.23.refs_3_), channel_id=1, source_target_pairs={{0,1},{1,0},{2,3},{3,2},{4,5},{5,4},{6,7},{7,6},{8,9},{9,8},{10,11... | collective-permute-start | bytes 786440 | tf_op jit(solution)/shard_map/ppermute | solution.py:64
  145.0 2.9 %collective-permute-start.26 = (f32[128,512]{1,0:T(8,128)}, f32[128,512]{1,0:T(8,128)}, u32[]{:S(2)}, u32[]{:S(2)}) collective-permute-start(f32[128,512]{1,0:T(8,128)} %collective-permute-done.22.refs_2_), channel_id=1, source_target_pairs={{0,1},{1,0},{2,3},{3,2},{4,5},{5,4},{6,7},{7,6},{8,9},{9,8},{10,11... | collective-permute-start | bytes 786440 | tf_op jit(solution)/shard_map/ppermute | solution.py:64
  146.4 51.8 %collective-permute-start.3 = (f32[128,1024]{1,0:T(8,128)S(1)}, f32[128,1024]{1,0:T(8,128)S(1)}, u32[]{:S(2)}, u32[]{:S(2)}) collective-permute-start(f32[128,1024]{1,0:T(8,128)S(1)} %copy-done), channel_id=1, source_target_pairs={{0,1},{1,0},{2,3},{3,2},{4,5},{5,4},{6,7},{7,6},{8,9},{9,8},{10,11... | collective-permute-start | bytes 1572872 | tf_op jit(solution)/shard_map/ppermute | solution.py:64
  147.1 51.1 %collective-permute-start.6 = (f32[128,1024]{1,0:T(8,128)S(1)}, f32[128,1024]{1,0:T(8,128)S(1)}, u32[]{:S(2)}, u32[]{:S(2)}) collective-permute-start(f32[128,1024]{1,0:T(8,128)S(1)} %collective-permute-done.2.refs_3_), channel_id=1, source_target_pairs={{0,1},{1,0},{2,3},{3,2},{4,5},{5,4},{6,7},{7,6},{8,9},{9,8},{10,11... | collective-permute-start | bytes 1572872 | tf_op jit(solution)/shard_map/ppermute | solution.py:64
  147.2 51.0 %collective-permute-start.5 = (f32[128,1024]{1,0:T(8,128)S(1)}, f32[128,1024]{1,0:T(8,128)}, u32[]{:S(2)}, u32[]{:S(2)}) collective-permute-start(f32[128,1024]{1,0:T(8,128)S(1)} %collective-permute-done.1.refs_2_), channel_id=1, source_target_pairs={{0,1},{1,0},{2,3},{3,2},{4,5},{5,4},{6,7},{7,6},{8,9},{9,8},{10,11... | collective-permute-start | bytes 1572872 | tf_op jit(solution)/shard_map/ppermute | solution.py:64
  147.6 50.6 %collective-permute-start.4 = (f32[128,1024]{1,0:T(8,128)S(1)}, f32[128,1024]{1,0:T(8,128)}, u32[]{:S(2)}, u32[]{:S(2)}) collective-permute-start(f32[128,1024]{1,0:T(8,128)S(1)} %collective-permute-done.refs_1_), channel_id=1, source_target_pairs={{0,1},{1,0},{2,3},{3,2},{4,5},{5,4},{6,7},{7,6},{8,9},{9,8},{10,11... | collective-permute-start | bytes 1572872 | tf_op jit(solution)/shard_map/ppermute | solution.py:64
  147.9 3.5 %collective-permute-start.25 = (f32[128,512]{1,0:T(8,128)}, f32[128,512]{1,0:T(8,128)}, u32[]{:S(2)}, u32[]{:S(2)}) collective-permute-start(f32[128,512]{1,0:T(8,128)} %copy-done.8), channel_id=1, source_target_pairs={{0,1},{1,0},{2,3},{3,2},{4,5},{5,4},{6,7},{7,6},{8,9},{9,8},{10,11... | collective-permute-start | bytes 786440 | tf_op jit(solution)/shard_map/ppermute | solution.py:64
  (7 other events, 158.9 us)
Sparse Core Ops, SparseCore 0:
  39.7 61.3 all-gather.1

commit v4 on v3

--- a/solution.py
+++ b/solution.py
@@ -54,7 +54,7 @@
     for k in LEAD_SHIFTS[1:]:
         pairs = []
         for y, x, z, core in itertools.product(range(4), range(4), range(8), range(2)):
-            to = (z + (-k if k == 2 and core else k)) % 8
+            to = (z + (-1 if k == 3 else -2 if k == 2 and core else k)) % 8
             pairs.append((device_id(z // 4, y, x, z % 4, core), device_id(to // 4, y, x, to % 4, core)))
         line.append(lax.ppermute(mine, AXES, pairs))
     return swap_cores(line)
@@ -112,17 +112,43 @@
     return dot(a[0], b[0], dims) + (dot(a[0], b[1], dims) + dot(a[1], b[0], dims))
 
 
+def parts(a):
+    first = a.astype(jnp.bfloat16).astype(jnp.float32)
+    rest = a - first
+    second = rest.astype(jnp.bfloat16).astype(jnp.float32)
+    return first, second, rest - second
+
+
+def rank8(a, b):
+    a1, a2, a3 = parts(a)
+    b1, b2, b3 = parts(b)
+    left = jnp.concatenate([a1, a1, a2, a2, a1, a3]).astype(jnp.bfloat16)
+    right = jnp.concatenate([b1, b2, b1, b2, b3, b1]).astype(jnp.bfloat16)
+    return dot(left, right, ((0,), (0,)))
+
+
 def eliminate(m_ref):
     lane = lax.broadcasted_iota(jnp.int32, (8, SUB), 1)
     sub = lax.broadcasted_iota(jnp.int32, (8, SUB), 0)
+
+    def entry(row, column):
+        return jnp.broadcast_to(row[:, column : column + 1], (8, SUB))
+
+    def load(o):
+        return [
+            [jnp.broadcast_to(m_ref[o + i : o + i + 1, h * SUB : (h + 1) * SUB], (8, SUB)) for i in range(8)]
+            for h in range(2)
+        ]
+
+    def stacked(rows):
+        strip = rows[7]
+        for i in range(7):
+            strip = jnp.where(sub == i, rows[i], strip)
+        return strip
+
+    left, right = load(0)
     for o in range(0, SUB, 8):
-        left = [jnp.broadcast_to(m_ref[o + i : o + i + 1, :SUB], (8, SUB)) for i in range(8)]
-        right = [jnp.broadcast_to(m_ref[o + i : o + i + 1, SUB:], (8, SUB)) for i in range(8)]
-        e = {
-            (i, j): jnp.broadcast_to(left[i][:, o + j : o + j + 1], (8, SUB)) for i in range(8) for j in range(i, 8)
-        }
-        strip_left = jnp.zeros((8, SUB), jnp.float32)
-        strip_right = strip_left
+        e = {(i, j): entry(left[i], o + j) for i in range(8) for j in range(i, 8)}
         for i in range(8):
             r = lax.rsqrt(e[i, i])
             for j in range(i + 1, 8):
@@ -130,19 +156,26 @@
             for j in range(i + 1, 8):
                 for k in range(j, 8):
                     e[j, k] = e[j, k] - e[i, j] * e[i, k]
-            a, b = left[i] * r, right[i] * r
+            left[i], right[i] = left[i] * r, right[i] * r
             for j in range(i + 1, 8):
-                left[j] = left[j] - e[i, j] * a
-                right[j] = right[j] - e[i, j] * b
-            strip_left = jnp.where(sub == i, a, strip_left)
-            strip_right = jnp.where(sub == i, b, strip_right)
+                left[j] = left[j] - e[i, j] * left[i]
+                right[j] = right[j] - e[i, j] * right[i]
+        strip_left, strip_right = stacked(left), stacked(right)
         m_ref[o : o + 8, :SUB] = strip_left
         m_ref[o : o + 8, SUB:] = strip_right
-        if o + 8 < SUB:
-            masked = jnp.where(lane >= o + 8, strip_left, 0.0)
-            strip = jnp.concatenate([strip_left, strip_right], axis=1)
-            update = dot(masked, strip, ((0,), (0,)), lax.Precision.HIGHEST)
-            m_ref[o + 8 :, :] = m_ref[o + 8 :, :] - update[o + 8 :, :]
+        n = o + 8
+        if n < SUB:
+            next_left, next_right = load(n)
+            for k in range(8):
+                for i in range(8):
+                    u = entry(left[i], n + k)
+                    next_left[k] = next_left[k] - u * left[i]
+                    next_right[k] = next_right[k] - u * right[i]
+            left, right = next_left, next_right
+        if n + 8 < SUB:
+            masked = jnp.where(lane >= n + 8, strip_left, 0.0)
+            update = rank8(masked, jnp.concatenate([strip_left, strip_right], axis=1))
+            m_ref[n + 8 :, :] = m_ref[n + 8 :, :] - update[n + 8 :, :]
 
 
 def lead_kernel(place_ref, *refs):

time: 235 us -> 201 us (0.86)
  the two profiles are of different devices: /device:TPU:65 before, /device:TPU:1 now
where the time goes in v4:
time: 201 us; the launch traced here: 200 us
  waiting for transfers between devices  67.6 us (34%)
  Pallas kernels  58 us (29%)
  starting transfers between devices  55.8 us (28%)
  between operations  13.7 us (7%)
  other arithmetic  3.23 us (2%)
  local copies, waits for them, and re-layouts  2.05 us (1%)
    ppermute x3, waiting for transfers between devices, spread_lead(): line.append(lax.ppermute(mine, AXES, pairs))  31.6 us
    pallas_call x1, Pallas kernels, lead_call(): pl.pallas_call(lead_kernel, out_shape=(jax.ShapeDtypeStruct((rows, BLOCK)...  29.2 us
    pallas_call x1, Pallas kernels, apply_call(): pl.pallas_call(apply_kernel, grid_spec=grid_spec, out_shape=jax.ShapeDtyp...  28.8 us
    ppermute x7, starting transfers between devices, permute_rows(): lax.ppermute(values[i], AXES, [(device_id(*s, *c), device_id(*t, *c)) for...  12.9 us
    ppermute x3, starting transfers between devices, spread_lead(): line.append(lax.ppermute(mine, AXES, pairs))  12.1 us
    ppermute x8, starting transfers between devices, swap_cores(): return line + [lax.ppermute(piece, 'core', ring(2, 1)) for piece in line]  11.8 us
    ppermute x2, starting transfers between devices, scatter_columns(): planes.append(lax.ppermute(halves[j], AXES, pairs))  9.32 us
    ppermute x2, waiting for transfers between devices, scatter_columns(): planes.append(lax.ppermute(halves[j], AXES, pairs))  9.17 us
  transfers between devices with their start and end apart: 29, of which 14 were waited for; matrix products, arithmetic and copies ran while one was open for 1% of the time, Pallas kernels for 15%

profile of v4, /device:TPU:1, one launch (start us, length us, event | category | flops | bytes accessed | tf_op | source)
XLA Modules:
  0.0 200.4 jit_solution(10569380905475265112)
XLA Ops:
  7.7 5.2 %collective-permute-start.8 = (f32[64,1024]{1,0:T(8,128)S(1)}, f32[64,1024]{1,0:T(8,128)S(1)}, u32[]{:S(2)}, u32[]{:S(2)}) collective-permute-start(f32[64,1024]{1,0:T(8,128)S(1)} %get-tuple-element.9), channel_id=1, source_target_pairs={{0,8},{1,25},{2,42},{3,59},{4,76},{5,93},{6,110},{7,127},{8,24},{9... | collective-permute-start | bytes 786440 | tf_op jit(solution)/shard_map/ppermute | solution.py:90
  12.9 4.1 %collective-permute-start.7 = (f32[64,1024]{1,0:T(8,128)S(1)}, f32[64,1024]{1,0:T(8,128)S(1)}, u32[]{:S(2)}, u32[]{:S(2)}) collective-permute-start(f32[64,1024]{1,0:T(8,128)S(1)} %get-tuple-element.10), channel_id=1, source_target_pairs={{0,0},{1,17},{2,34},{3,51},{4,68},{5,85},{6,102},{7,119},{8,16},{9... | collective-permute-start | bytes 786440 | tf_op jit(solution)/shard_map/ppermute | solution.py:90
  17.0 2.0 collective-permute-done.8
  19.0 7.2 %collective-permute-done.7 = f32[64,1024]{1,0:T(8,128)S(1)} collective-permute-done((f32[64,1024]{1,0:T(8,128)S(1)}, f32[64,1024]{1,0:T(8,128)S(1)}, u32[]{:S(2)}, u32[]{:S(2)}) %collective-permute-start.7) | collective-permute-done | bytes 262176 | tf_op jit(solution)/shard_map/ppermute | solution.py:90
  26.2 1.3 collective-permute-start.10
  27.5 4.0 %collective-permute-start.9 = (f32[64,1024]{1,0:T(8,128)S(1)}, f32[64,1024]{1,0:T(8,128)S(1)}, u32[]{:S(2)}, u32[]{:S(2)}) collective-permute-start(f32[64,1024]{1,0:T(8,128)S(1)} %add.82), channel_id=1, source_target_pairs={{0,0},{1,7},{2,6},{3,5},{4,4},{5,3},{6,2},{7,1},{8,8},{9,15},{10,1... | collective-permute-start | bytes 786440 | tf_op jit(solution)/shard_map/ppermute | solution.py:98
  31.5 4.4 %collective-permute-done.10 = f32[64,1024]{1,0:T(8,128)S(1)} collective-permute-done((f32[64,1024]{1,0:T(8,128)S(1)}, f32[64,1024]{1,0:T(8,128)S(1)}, u32[]{:S(2)}, u32[]{:S(2)}) %collective-permute-start.10) | collective-permute-done | bytes 262176 | tf_op jit(solution)/shard_map/ppermute | solution.py:98
  35.9 2.6 %collective-permute-done.9 = f32[64,1024]{1,0:T(8,128)S(1)} collective-permute-done((f32[64,1024]{1,0:T(8,128)S(1)}, f32[64,1024]{1,0:T(8,128)S(1)}, u32[]{:S(2)}, u32[]{:S(2)}) %collective-permute-start.9) | collective-permute-done | bytes 262176 | tf_op jit(solution)/shard_map/ppermute | solution.py:98
  40.3 1.3 collective-permute-start.12
  41.6 1.3 collective-permute-start.13
  42.9 1.3 collective-permute-start.11
  44.2 1.3 collective-permute-done.11
  45.5 5.2 %collective-permute-start.16 = (f32[32,512]{1,0:T(8,128)S(1)}, f32[32,512]{1,0:T(8,128)S(1)}, u32[]{:S(2)}, u32[]{:S(2)}) collective-permute-start(f32[32,512]{1,0:T(8,128)S(1)} %slice_add_fusion), channel_id=1, source_target_pairs={{0,64},{1,65},{2,66},{3,67},{4,68},{5,69},{6,70},{7,71},{8,72},{9,... | collective-permute-start | bytes 196616 | tf_op jit(solution)/shard_map/ppermute | solution.py:37
  50.7 1.3 collective-permute-start.15
  52.0 1.3 collective-permute-start.14
  53.3 1.3 collective-permute-done.14
  54.7 1.3 collective-permute-start.17
  56.0 1.3 collective-permute-done.17
  58.9 3.1 %collective-permute-done.20 = f32[32,512]{1,0:T(8,128)S(1)} collective-permute-done((f32[32,512]{1,0:T(8,128)S(1)}, f32[32,512]{1,0:T(8,128)S(1)}, u32[]{:S(2)}, u32[]{:S(2)}) %collective-permute-start.20) | collective-permute-done | bytes 65568 | tf_op jit(solution)/shard_map/ppermute | solution.py:52
  62.0 2.6 %collective-permute-done.18 = f32[32,512]{1,0:T(8,128)S(1)} collective-permute-done((f32[32,512]{1,0:T(8,128)S(1)}, f32[32,512]{1,0:T(8,128)S(1)}, u32[]{:S(2)}, u32[]{:S(2)}) %collective-permute-start.18) | collective-permute-done | bytes 65568 | tf_op jit(solution)/shard_map/ppermute | solution.py:52
  64.6 1.2 collective-permute-start.24
  65.8 12.1 %collective-permute-start.23 = (f32[128,512]{1,0:T(8,128)S(1)}, f32[128,512]{1,0:T(8,128)}, u32[]{:S(2)}, u32[]{:S(2)}) collective-permute-start(f32[128,512]{1,0:T(8,128)S(1)} %pad_maximum_fusion.refs_0_), channel_id=1, source_target_pairs={{0,4},{1,133},{2,6},{3,135},{4,128},{5,1},{6,130},{7,3},{128,132},... | collective-permute-start | bytes 786440 | tf_op jit(solution)/shard_map/ppermute | solution.py:59
  77.9 2.6 %collective-permute-start.1 = (f32[128,1024]{1,0:T(8,128)S(1)}, f32[128,1024]{1,0:T(8,128)S(1)}, u32[]{:S(2)}, u32[]{:S(2)}) collective-permute-start(f32[128,1024]{1,0:T(8,128)S(1)} %copy-done), channel_id=1, source_target_pairs={{0,4},{2,6},{4,0},{6,2},{1,5},{3,7},{5,1},{7,3},{8,12},{10,14},{12... | collective-permute-start | bytes 1572872 | tf_op jit(solution)/shard_map/ppermute | solution.py:68
  80.6 5.0 %collective-permute-done.23.refs_3_ = f32[128,512]{1,0:T(8,128)} collective-permute-done((f32[128,512]{1,0:T(8,128)S(1)}, f32[128,512]{1,0:T(8,128)}, u32[]{:S(2)}, u32[]{:S(2)}) %collective-permute-start.23) | collective-permute-done | bytes 262176 | tf_op jit(solution)/shard_map/ppermute | solution.py:59
  85.6 6.5 %collective-permute-done.22.refs_2_ = f32[128,512]{1,0:T(8,128)} collective-permute-done((f32[128,512]{1,0:T(8,128)S(1)}, f32[128,512]{1,0:T(8,128)}, u32[]{:S(2)}, u32[]{:S(2)}) %collective-permute-start.22) | collective-permute-done | bytes 262176 | tf_op jit(solution)/shard_map/ppermute | solution.py:59
  92.1 6.6 %collective-permute-start.27 = (f32[128,512]{1,0:T(8,128)}, f32[128,512]{1,0:T(8,128)}, u32[]{:S(2)}, u32[]{:S(2)}) collective-permute-start(f32[128,512]{1,0:T(8,128)} %collective-permute-done.23.refs_3_), channel_id=1, source_target_pairs={{0,1},{1,0},{2,3},{3,2},{4,5},{5,4},{6,7},{7,6},{8,9},{9,8},{10,11... | collective-permute-start | bytes 786440 | tf_op jit(solution)/shard_map/ppermute | solution.py:64
  98.7 20.1 %collective-permute-done.21.refs_1_ = f32[128,512]{1,0:T(8,128)S(1)} collective-permute-done((f32[128,512]{1,0:T(8,128)S(1)}, f32[128,512]{1,0:T(8,128)S(1)}, u32[]{:S(2)}, u32[]{:S(2)}) %collective-permute-start.21) | collective-permute-done | bytes 262176 | tf_op jit(solution)/shard_map/ppermute | solution.py:59
  118.8 2.1 %collective-permute-start.26 = (f32[128,512]{1,0:T(8,128)}, f32[128,512]{1,0:T(8,128)}, u32[]{:S(2)}, u32[]{:S(2)}) collective-permute-start(f32[128,512]{1,0:T(8,128)} %collective-permute-done.22.refs_2_), channel_id=1, source_target_pairs={{0,1},{1,0},{2,3},{3,2},{4,5},{5,4},{6,7},{7,6},{8,9},{9,8},{10,11... | collective-permute-start | bytes 786440 | tf_op jit(solution)/shard_map/ppermute | solution.py:64
  121.6 9.0 %collective-permute-done.1.refs_2_ = f32[128,1024]{1,0:T(8,128)S(1)} collective-permute-done((f32[128,1024]{1,0:T(8,128)S(1)}, f32[128,1024]{1,0:T(8,128)S(1)}, u32[]{:S(2)}, u32[]{:S(2)}) %collective-permute-start.1) | collective-permute-done | bytes 524320 | tf_op jit(solution)/shard_map/ppermute | solution.py:68
  133.3 1.2 collective-permute-done.25.refs_5_
  134.5 29.2 %lead.1 = (f32[1024,512]{1,0:T(8,128)}, f32[512,512]{1,0:T(8,128)}) custom-call(s32[12]{0:T(128)} %pad_add_fusion.1.place_ref, f32[128,512]{1,0:T(8,128)} %copy-done.1, f32[128,512]{1,0:T(8,128)} %copy-done.8, f32[128,512]{1,0:T(8,128)} %collective-permute-done.22.refs_2_, f32[128,512]{1,0:T(8,128)} %collective-permute-done.23.refs_3_, ...), custom_call_target="tpu_custom_call" | custom-call | tf_op jit(solution)/shard_map/lead/pallas_call | solution.py:228
  164.8 28.8 %apply.1 = f32[1024,1024]{1,0:T(8,128)} custom-call(s32[10]{0:T(128)} %pad_add_fusion.where_ref, f32[128,1024]{1,0:T(8,128)} %refs_0_.1, f32[128,1024]{1,0:T(8,128)} %copy-done.4, f32[128,1024]{1,0:T(8,128)} %copy-done.3, f32[128,1024]{1,0:T(8,128)} %copy-done.2, f32[128,1024]{1,0:T(8,128)} %copy-done.5, f32[128,1024]{1,0:T(8,128)} %collective-permute-done.4.refs_5_, ...), custom_call_target="tpu_custom_call" | custom-call | tf_op jit(solution)/shard_map/apply/pallas_call | solution.py:317
  (65 shorter events, 8.9 us)
Async XLA Ops:
  6.5 92.2 %copy-start.9 = (s32[4]{0:T(128)S(1)}, s32[4]{0:T(128)}, u32[]{:S(2)}) copy-start(s32[4]{0:T(128)} %constant.41) | copy-start | bytes 52
  6.5 71.4 %copy-start = (f32[128,1024]{1,0:T(8,128)S(1)}, f32[128,1024]{1,0:T(8,128)}, u32[]{:S(2)}) copy-start(f32[128,1024]{1,0:T(8,128)} %refs_0_.1) | copy-start | bytes 1572868
  6.5 157.3 %all-gather.2.cloned.1.call-start = ((), (), s32[]{:S(2)}) async-start(), calls=%async_computation | async-start | bytes 4456448 | tf_op jit(solution)/shard_map/all_gather | solution.py:329
  7.7 11.3 %collective-permute-start.8 = (f32[64,1024]{1,0:T(8,128)S(1)}, f32[64,1024]{1,0:T(8,128)S(1)}, u32[]{:S(2)}, u32[]{:S(2)}) collective-permute-start(f32[64,1024]{1,0:T(8,128)S(1)} %get-tuple-element.9), channel_id=1, source_target_pairs={{0,8},{1,25},{2,42},{3,59},{4,76},{5,93},{6,110},{7,127},{8,24},{9... | collective-permute-start | bytes 786440 | tf_op jit(solution)/shard_map/ppermute | solution.py:90
  12.9 13.3 %collective-permute-start.7 = (f32[64,1024]{1,0:T(8,128)S(1)}, f32[64,1024]{1,0:T(8,128)S(1)}, u32[]{:S(2)}, u32[]{:S(2)}) collective-permute-start(f32[64,1024]{1,0:T(8,128)S(1)} %get-tuple-element.10), channel_id=1, source_target_pairs={{0,0},{1,17},{2,34},{3,51},{4,68},{5,85},{6,102},{7,119},{8,16},{9... | collective-permute-start | bytes 786440 | tf_op jit(solution)/shard_map/ppermute | solution.py:90
  26.2 9.7 %collective-permute-start.10 = (f32[64,1024]{1,0:T(8,128)S(1)}, f32[64,1024]{1,0:T(8,128)S(1)}, u32[]{:S(2)}, u32[]{:S(2)}) collective-permute-start(f32[64,1024]{1,0:T(8,128)S(1)} %add.82), channel_id=1, source_target_pairs={{0,128},{1,135},{2,134},{3,133},{4,132},{5,131},{6,130},{7,129},{8... | collective-permute-start | bytes 786440 | tf_op jit(solution)/shard_map/ppermute | solution.py:98
  27.5 11.0 %collective-permute-start.9 = (f32[64,1024]{1,0:T(8,128)S(1)}, f32[64,1024]{1,0:T(8,128)S(1)}, u32[]{:S(2)}, u32[]{:S(2)}) collective-permute-start(f32[64,1024]{1,0:T(8,128)S(1)} %add.82), channel_id=1, source_target_pairs={{0,0},{1,7},{2,6},{3,5},{4,4},{5,3},{6,2},{7,1},{8,8},{9,15},{10,1... | collective-permute-start | bytes 786440 | tf_op jit(solution)/shard_map/ppermute | solution.py:98
  40.3 3.9 %collective-permute-start.12 = (f32[32,512]{1,0:T(8,128)S(1)}, f32[32,512]{1,0:T(8,128)S(1)}, u32[]{:S(2)}, u32[]{:S(2)}) collective-permute-start(f32[32,512]{1,0:T(8,128)S(1)} %get-tuple-element.11), channel_id=1, source_target_pairs={{0,24},{1,25},{2,26},{3,27},{4,28},{5,29},{6,30},{7,31}} | collective-permute-start | bytes 196616 | tf_op jit(solution)/shard_map/ppermute | solution.py:37
  41.6 2.6 %collective-permute-start.13 = (f32[32,512]{1,0:T(8,128)S(1)}, f32[32,512]{1,0:T(8,128)S(1)}, u32[]{:S(2)}, u32[]{:S(2)}) collective-permute-start(f32[32,512]{1,0:T(8,128)S(1)} %get-tuple-element.12), channel_id=1, source_target_pairs={{0,16},{1,17},{2,18},{3,19},{4,20},{5,21},{6,22},{7,23}} | collective-permute-start | bytes 196616 | tf_op jit(solution)/shard_map/ppermute | solution.py:37
  42.9 2.6 %collective-permute-start.11 = (f32[32,512]{1,0:T(8,128)S(1)}, f32[32,512]{1,0:T(8,128)S(1)}, u32[]{:S(2)}, u32[]{:S(2)}) collective-permute-start(f32[32,512]{1,0:T(8,128)S(1)} %get-tuple-element.13), channel_id=1, source_target_pairs={{0,8},{1,9},{2,10},{3,11},{4,12},{5,13},{6,14},{7,15}} | collective-permute-start | bytes 196616 | tf_op jit(solution)/shard_map/ppermute | solution.py:37
  45.5 7.8 %collective-permute-start.16 = (f32[32,512]{1,0:T(8,128)S(1)}, f32[32,512]{1,0:T(8,128)S(1)}, u32[]{:S(2)}, u32[]{:S(2)}) collective-permute-start(f32[32,512]{1,0:T(8,128)S(1)} %slice_add_fusion), channel_id=1, source_target_pairs={{0,64},{1,65},{2,66},{3,67},{4,68},{5,69},{6,70},{7,71},{8,72},{9,... | collective-permute-start | bytes 196616 | tf_op jit(solution)/shard_map/ppermute | solution.py:37
  50.7 2.6 %collective-permute-start.15 = (f32[32,512]{1,0:T(8,128)S(1)}, f32[32,512]{1,0:T(8,128)S(1)}, u32[]{:S(2)}, u32[]{:S(2)}) collective-permute-start(f32[32,512]{1,0:T(8,128)S(1)} %slice_add_fusion), channel_id=1, source_target_pairs={{0,96},{1,97},{2,98},{3,99},{4,100},{5,101},{6,102},{7,103},{8,104... | collective-permute-start | bytes 196616 | tf_op jit(solution)/shard_map/ppermute | solution.py:37
  52.0 2.6 %collective-permute-start.14 = (f32[32,512]{1,0:T(8,128)S(1)}, f32[32,512]{1,0:T(8,128)S(1)}, u32[]{:S(2)}, u32[]{:S(2)}) collective-permute-start(f32[32,512]{1,0:T(8,128)S(1)} %slice_add_fusion), channel_id=1, source_target_pairs={{0,32},{1,33},{2,34},{3,35},{4,36},{5,37},{6,38},{7,39},{8,40},{9,... | collective-permute-start | bytes 196616 | tf_op jit(solution)/shard_map/ppermute | solution.py:37
  54.7 2.6 %collective-permute-start.17 = (f32[32,512]{1,0:T(8,128)S(1)}, f32[32,512]{1,0:T(8,128)S(1)}, u32[]{:S(2)}, u32[]{:S(2)}) collective-permute-start(f32[32,512]{1,0:T(8,128)S(1)} %add_add_fusion), channel_id=1, source_target_pairs={{0,128},{1,129},{2,130},{3,131},{4,132},{5,133},{6,134},{7,135},{8... | collective-permute-start | bytes 196616 | tf_op jit(solution)/shard_map/ppermute | solution.py:37
  57.3 4.7 %collective-permute-start.20 = (f32[32,512]{1,0:T(8,128)S(1)}, f32[32,512]{1,0:T(8,128)S(1)}, u32[]{:S(2)}, u32[]{:S(2)}) collective-permute-start(f32[32,512]{1,0:T(8,128)S(1)} %add.94), channel_id=1, source_target_pairs={{0,16},{8,24},{16,0},{24,8},{1,17},{9,25},{17,1},{25,9},{2,18},{10... | collective-permute-start | bytes 196616 | tf_op jit(solution)/shard_map/ppermute | solution.py:52
  57.4 4.6 %collective-permute-start.19 = (f32[32,512]{1,0:T(8,128)S(1)}, f32[32,512]{1,0:T(8,128)S(1)}, u32[]{:S(2)}, u32[]{:S(2)}) collective-permute-start(f32[32,512]{1,0:T(8,128)S(1)} %add.94), channel_id=1, source_target_pairs={{0,24},{8,0},{16,8},{24,16},{1,25},{9,1},{17,9},{25,17},{2,26},{10... | collective-permute-start | bytes 196616 | tf_op jit(solution)/shard_map/ppermute | solution.py:52
  58.4 6.2 %collective-permute-start.18 = (f32[32,512]{1,0:T(8,128)S(1)}, f32[32,512]{1,0:T(8,128)S(1)}, u32[]{:S(2)}, u32[]{:S(2)}) collective-permute-start(f32[32,512]{1,0:T(8,128)S(1)} %add.94), channel_id=1, source_target_pairs={{0,8},{8,16},{16,24},{24,0},{1,9},{9,17},{17,25},{25,1},{2,10},{10... | collective-permute-start | bytes 196616 | tf_op jit(solution)/shard_map/ppermute | solution.py:52
  64.6 69.9 %copy-start.1 = (f32[128,512]{1,0:T(8,128)}, f32[128,512]{1,0:T(8,128)S(1)}, u32[]{:S(2)}) copy-start(f32[128,512]{1,0:T(8,128)S(1)} %pad_maximum_fusion.refs_0_) | copy-start | bytes 786436
  64.6 15.9 %collective-permute-start.24 = (f32[128,512]{1,0:T(8,128)S(1)}, f32[128,512]{1,0:T(8,128)S(1)}, u32[]{:S(2)}, u32[]{:S(2)}) collective-permute-start(f32[128,512]{1,0:T(8,128)S(1)} %pad_maximum_fusion.refs_0_), channel_id=1, source_target_pairs={{0,1},{1,0},{2,3},{3,2},{4,5},{5,4},{6,7},{7,6},{8,9},{9,8},{10,11... | collective-permute-start | bytes 786440 | tf_op jit(solution)/shard_map/ppermute | solution.py:64
  65.8 19.8 %collective-permute-start.23 = (f32[128,512]{1,0:T(8,128)S(1)}, f32[128,512]{1,0:T(8,128)}, u32[]{:S(2)}, u32[]{:S(2)}) collective-permute-start(f32[128,512]{1,0:T(8,128)S(1)} %pad_maximum_fusion.refs_0_), channel_id=1, source_target_pairs={{0,4},{1,133},{2,6},{3,135},{4,128},{5,1},{6,130},{7,3},{128,132},... | collective-permute-start | bytes 786440 | tf_op jit(solution)/shard_map/ppermute | solution.py:59
  77.9 14.2 %collective-permute-start.22 = (f32[128,512]{1,0:T(8,128)S(1)}, f32[128,512]{1,0:T(8,128)}, u32[]{:S(2)}, u32[]{:S(2)}) collective-permute-start(f32[128,512]{1,0:T(8,128)S(1)} %pad_maximum_fusion.refs_0_), channel_id=1, source_target_pairs={{0,134},{1,135},{2,0},{3,1},{4,2},{5,3},{6,4},{7,5},{128,6},{129,7... | collective-permute-start | bytes 786440 | tf_op jit(solution)/shard_map/ppermute | solution.py:59
  77.9 43.0 %collective-permute-start.2 = (f32[128,1024]{1,0:T(8,128)S(1)}, f32[128,1024]{1,0:T(8,128)S(1)}, u32[]{:S(2)}, u32[]{:S(2)}) collective-permute-start(f32[128,1024]{1,0:T(8,128)S(1)} %copy-done), channel_id=1, source_target_pairs={{0,6},{2,0},{4,2},{6,4},{1,7},{3,1},{5,3},{7,5},{8,14},{10,8},{12,... | collective-permute-start | bytes 1572872 | tf_op jit(solution)/shard_map/ppermute | solution.py:68
  77.9 52.7 %collective-permute-start.1 = (f32[128,1024]{1,0:T(8,128)S(1)}, f32[128,1024]{1,0:T(8,128)S(1)}, u32[]{:S(2)}, u32[]{:S(2)}) collective-permute-start(f32[128,1024]{1,0:T(8,128)S(1)} %copy-done), channel_id=1, source_target_pairs={{0,4},{2,6},{4,0},{6,2},{1,5},{3,7},{5,1},{7,3},{8,12},{10,14},{12... | collective-permute-start | bytes 1572872 | tf_op jit(solution)/shard_map/ppermute | solution.py:68
  80.6 50.1 %collective-permute-start = (f32[128,1024]{1,0:T(8,128)S(1)}, f32[128,1024]{1,0:T(8,128)S(1)}, u32[]{:S(2)}, u32[]{:S(2)}) collective-permute-start(f32[128,1024]{1,0:T(8,128)S(1)} %copy-done), channel_id=1, source_target_pairs={{0,2},{2,4},{4,6},{6,0},{1,3},{3,5},{5,7},{7,1},{8,10},{10,12},{12... | collective-permute-start | bytes 1572872 | tf_op jit(solution)/shard_map/ppermute | solution.py:68
  85.6 33.2 %collective-permute-start.21 = (f32[128,512]{1,0:T(8,128)S(1)}, f32[128,512]{1,0:T(8,128)S(1)}, u32[]{:S(2)}, u32[]{:S(2)}) collective-permute-start(f32[128,512]{1,0:T(8,128)S(1)} %pad_maximum_fusion.refs_0_), channel_id=1, source_target_pairs={{0,2},{1,3},{2,4},{3,5},{4,6},{5,7},{6,128},{7,129},{128,130},{129... | collective-permute-start | bytes 786440 | tf_op jit(solution)/shard_map/ppermute | solution.py:59
  92.1 39.1 %collective-permute-start.27 = (f32[128,512]{1,0:T(8,128)}, f32[128,512]{1,0:T(8,128)}, u32[]{:S(2)}, u32[]{:S(2)}) collective-permute-start(f32[128,512]{1,0:T(8,128)} %collective-permute-done.23.refs_3_), channel_id=1, source_target_pairs={{0,1},{1,0},{2,3},{3,2},{4,5},{5,4},{6,7},{7,6},{8,9},{9,8},{10,11... | collective-permute-start | bytes 786440 | tf_op jit(solution)/shard_map/ppermute | solution.py:64
  118.8 12.6 %collective-permute-start.26 = (f32[128,512]{1,0:T(8,128)}, f32[128,512]{1,0:T(8,128)}, u32[]{:S(2)}, u32[]{:S(2)}) collective-permute-start(f32[128,512]{1,0:T(8,128)} %collective-permute-done.22.refs_2_), channel_id=1, source_target_pairs={{0,1},{1,0},{2,3},{3,2},{4,5},{5,4},{6,7},{7,6},{8,9},{9,8},{10,11... | collective-permute-start | bytes 786440 | tf_op jit(solution)/shard_map/ppermute | solution.py:64
  120.9 42.8 %collective-permute-start.3 = (f32[128,1024]{1,0:T(8,128)S(1)}, f32[128,1024]{1,0:T(8,128)S(1)}, u32[]{:S(2)}, u32[]{:S(2)}) collective-permute-start(f32[128,1024]{1,0:T(8,128)S(1)} %copy-done), channel_id=1, source_target_pairs={{0,1},{1,0},{2,3},{3,2},{4,5},{5,4},{6,7},{7,6},{8,9},{9,8},{10,11... | collective-permute-start | bytes 1572872 | tf_op jit(solution)/shard_map/ppermute | solution.py:64
  130.6 33.2 %collective-permute-start.6 = (f32[128,1024]{1,0:T(8,128)S(1)}, f32[128,1024]{1,0:T(8,128)S(1)}, u32[]{:S(2)}, u32[]{:S(2)}) collective-permute-start(f32[128,1024]{1,0:T(8,128)S(1)} %collective-permute-done.2.refs_3_), channel_id=1, source_target_pairs={{0,1},{1,0},{2,3},{3,2},{4,5},{5,4},{6,7},{7,6},{8,9},{9,8},{10,11... | collective-permute-start | bytes 1572872 | tf_op jit(solution)/shard_map/ppermute | solution.py:64
  130.6 33.2 %collective-permute-start.5 = (f32[128,1024]{1,0:T(8,128)S(1)}, f32[128,1024]{1,0:T(8,128)}, u32[]{:S(2)}, u32[]{:S(2)}) collective-permute-start(f32[128,1024]{1,0:T(8,128)S(1)} %collective-permute-done.1.refs_2_), channel_id=1, source_target_pairs={{0,1},{1,0},{2,3},{3,2},{4,5},{5,4},{6,7},{7,6},{8,9},{9,8},{10,11... | collective-permute-start | bytes 1572872 | tf_op jit(solution)/shard_map/ppermute | solution.py:64
  131.1 32.7 %collective-permute-start.4 = (f32[128,1024]{1,0:T(8,128)S(1)}, f32[128,1024]{1,0:T(8,128)}, u32[]{:S(2)}, u32[]{:S(2)}) collective-permute-start(f32[128,1024]{1,0:T(8,128)S(1)} %collective-permute-done.refs_1_), channel_id=1, source_target_pairs={{0,1},{1,0},{2,3},{3,2},{4,5},{5,4},{6,7},{7,6},{8,9},{9,8},{10,11... | collective-permute-start | bytes 1572872 | tf_op jit(solution)/shard_map/ppermute | solution.py:64
  131.4 3.1 %collective-permute-start.25 = (f32[128,512]{1,0:T(8,128)}, f32[128,512]{1,0:T(8,128)}, u32[]{:S(2)}, u32[]{:S(2)}) collective-permute-start(f32[128,512]{1,0:T(8,128)} %copy-done.8), channel_id=1, source_target_pairs={{0,1},{1,0},{2,3},{3,2},{4,5},{5,4},{6,7},{7,6},{8,9},{9,8},{10,11... | collective-permute-start | bytes 786440 | tf_op jit(solution)/shard_map/ppermute | solution.py:64
  (7 other events, 118.4 us)
Sparse Core Ops, SparseCore 0:
  39.4 63.1 all-gather.1

commit v5 on v4

--- a/solution.py
+++ b/solution.py
@@ -12,8 +12,9 @@
 
 BLOCK = 512
 SUB = 128
-TILE = 256
+TILE = 512
 PIECES = 8
+PLACE = 2 + PIECES
 LEAD_SHIFTS = (0, 1, 3, 2)
 ROW_SHIFTS = (0, 1, 2, 3)
 AXES = ("zh", "y", "x", "zl", "core")
@@ -178,22 +179,36 @@
             m_ref[n + 8 :, :] = m_ref[n + 8 :, :] - update[n + 8 :, :]
 
 
-def lead_kernel(place_ref, *refs):
-    pieces, (damping_ref, white_ref, inverse_ref, g_ref, m_ref) = refs[:PIECES], refs[PIECES:]
+def lead_kernel(where_ref, *refs):
+    pieces, (damping_ref, white_ref, inverse_ref, g_ref, m_ref, lead_ref, lh_ref, ll_ref) = refs[:PIECES], refs[PIECES:]
     highest = lax.Precision.HIGHEST
     depth = pieces[0].shape[0]
     same = lax.broadcasted_iota(jnp.int32, (BLOCK, BLOCK), 0) == lax.broadcasted_iota(jnp.int32, (BLOCK, BLOCK), 1)
-    gram = jnp.where(same, damping_ref[...], 0.0)
-    for i in range(0, PIECES, 4):
-        stack = jnp.concatenate([ref[...] for ref in pieces[i : i + 4]])
-        gram = gram + dot(stack, stack, ((0,), (0,)), highest)
-    g_ref[:, :BLOCK] = gram
+    for i, ref in enumerate(pieces):
+        part = depth // 4
+        for x in range(4):
+            start = pl.multiple_of(where_ref[PLACE + i] * depth + where_ref[PLACE + PIECES + x] * part, part)
+            lead_ref[pl.ds(start, part), :] = ref[x * part : (x + 1) * part]
+    g_ref[:, :BLOCK] = jnp.where(same, damping_ref[...], 0.0)
     g_ref[:, BLOCK:] = jnp.where(same, 1.0, 0.0)
+
+    def accumulate(i, carry):
+        chunk = lead_ref[pl.ds(pl.multiple_of(i * BLOCK, BLOCK), BLOCK), :]
+        g_ref[:, :BLOCK] += dot(chunk, chunk, ((0,), (0,)), highest)
+        lh_ref[pl.ds(pl.multiple_of(i * BLOCK, BLOCK), BLOCK), :], ll_ref[pl.ds(pl.multiple_of(i * BLOCK, BLOCK), BLOCK), :] = split(chunk)
+        return carry
+
+    lax.fori_loop(0, lead_ref.shape[0] // BLOCK, accumulate, 0)
+
+    def whiten(p):
+        here = pl.ds(pl.multiple_of(p * SUB, SUB), SUB)
+        white_ref[:, here] = dot3((lh_ref[...], ll_ref[...]), split(g_ref[here, BLOCK:]), ((1,), (1,)))
 
     def step(p, carry):
         start = pl.multiple_of(p * SUB, SUB)
         m_ref[:, :SUB] = g_ref[pl.ds(start, SUB), pl.ds(start, SUB)]
         m_ref[:, SUB:] = jnp.where(same[:SUB, :SUB], 1.0, 0.0)
+        whiten(jnp.maximum(p - 1, 0))
         eliminate(m_ref)
         inverse = m_ref[:, SUB:]
         for q in range(BLOCK // SUB):
@@ -211,18 +226,11 @@
         return carry
 
     lax.fori_loop(0, BLOCK // SUB, step, 0)
-    inverse = g_ref[:, BLOCK:]
-    inverse_ref[...] = inverse * damping_ref[...]
-    pair = split(inverse)
-    for i, ref in enumerate(pieces):
-        white = dot3(split(ref[...]), pair, ((1,), (1,)))
-        part = depth // 4
-        for x in range(4):
-            start = pl.multiple_of(place_ref[i] * depth + place_ref[PIECES + x] * part, part)
-            white_ref[pl.ds(start, part), :] = white[x * part : (x + 1) * part]
-
-
-def lead_call(pieces, place, damping):
+    whiten(BLOCK // SUB - 1)
+    inverse_ref[...] = g_ref[:, BLOCK:] * damping_ref[...]
+
+
+def lead_call(pieces, where, damping):
     vmem = pl.BlockSpec(memory_space=pltpu.VMEM)
     rows = PIECES * pieces[0].shape[0]
     return pl.pallas_call(
@@ -230,9 +238,14 @@
         out_shape=(jax.ShapeDtypeStruct((rows, BLOCK), jnp.float32), jax.ShapeDtypeStruct((BLOCK, BLOCK), jnp.float32)),
         in_specs=[pl.BlockSpec(memory_space=pltpu.SMEM)] + [vmem] * (PIECES + 1),
         out_specs=(vmem, vmem),
-        scratch_shapes=[pltpu.VMEM((BLOCK, 2 * BLOCK), jnp.float32), pltpu.VMEM((SUB, 2 * SUB), jnp.float32)],
+        scratch_shapes=[
+            pltpu.VMEM((BLOCK, 2 * BLOCK), jnp.float32),
+            pltpu.VMEM((SUB, 2 * SUB), jnp.float32),
+            pltpu.VMEM((rows, BLOCK), jnp.float32),
+        ]
+        + [pltpu.VMEM((rows, BLOCK), jnp.bfloat16)] * 2,
         name="lead",
-    )(place, *pieces, damping.reshape(1, BLOCK))
+    )(where, *pieces, damping.reshape(1, BLOCK))
 
 
 def apply_kernel(where_ref, *refs):
@@ -323,13 +336,13 @@
     row = lax.axis_index(ROW)
     col = lax.axis_index(COL)
     quarter = (lax.axis_index("x") + 4 - jnp.array(LEAD_SHIFTS, jnp.int32)) & 3
-    place = jnp.concatenate([(places(LEAD_SHIFTS) + col) & 7, quarter]).astype(jnp.int32)
     slots = inverse_of((places(ROW_SHIFTS) + col) & 7)
-    where = jnp.concatenate([jnp.stack([row, col]), slots]).astype(jnp.int32)
+    place = (places(LEAD_SHIFTS) + col) & 7
+    where = jnp.concatenate([jnp.stack([row, col]), slots, place, quarter]).astype(jnp.int32)
     columns = lax.all_gather(scatter_columns(design), ("y", "x"), tiled=True)
     lead = spread_lead(design, row == 0)
     rows = gather_rows(design)
-    white, inverse = lead_call(lead, place, damping)
+    white, inverse = lead_call(lead, where, damping)
     return apply_call(where, rows, columns, white, inverse)
 
 

time: 201 us -> 192 us (0.955); the launches traced: 200 us -> 189 us
  Pallas kernels: 58 us -> 49.8 us
  starting transfers between devices: 55.8 us -> 51.5 us
    pallas_call x1, Pallas kernels: 28.8 us -> 21.8 us  [apply_call(): pl.pallas_call(apply_kernel, grid_spec=grid_spec, out_shape=jax.ShapeDtyp...]
    ppermute x8, starting transfers between devices: 11.8 us -> 5.29 us  [swap_cores(): return line + [lax.ppermute(piece, 'core', ring(2, 1)) for piece in line]]
    ppermute x3, waiting for transfers between devices: 31.6 us -> 35.9 us  [spread_lead(): line.append(lax.ppermute(mine, AXES, pairs))]
    ppermute x3, starting transfers between devices: 12.1 us -> 15.6 us  [spread_lead(): line.append(lax.ppermute(mine, AXES, pairs))]
    ppermute x3, waiting for transfers between devices: 8.98 us -> 6.08 us  [gather_rows(): lax.ppermute(design, 'zl', ring(4, k))]
where the time goes in v5:
time: 192 us; the launch traced here: 189 us
  waiting for transfers between devices  69.6 us (36%)
  starting transfers between devices  51.5 us (27%)
  Pallas kernels  49.8 us (26%)
  between operations  13.7 us (7%)
  local copies, waits for them, and re-layouts  2.63 us (1%)
  other arithmetic  2.08 us (1%)
    ppermute x3, waiting for transfers between devices, spread_lead(): line.append(lax.ppermute(mine, AXES, pairs))  35.9 us
    pallas_call x1, Pallas kernels, lead_call(): pl.pallas_call(lead_kernel, out_shape=(jax.ShapeDtypeStruct((rows, BLOCK)...  28.1 us
    pallas_call x1, Pallas kernels, apply_call(): pl.pallas_call(apply_kernel, grid_spec=grid_spec, out_shape=jax.ShapeDtyp...  21.8 us
    ppermute x3, starting transfers between devices, spread_lead(): line.append(lax.ppermute(mine, AXES, pairs))  15.6 us
    ppermute x7, starting transfers between devices, permute_rows(): lax.ppermute(values[i], AXES, [(device_id(*s, *c), device_id(*t, *c)) for...  12.9 us
    ppermute x2, starting transfers between devices, scatter_columns(): planes.append(lax.ppermute(halves[j], AXES, pairs))  9.32 us
    ppermute x2, waiting for transfers between devices, scatter_columns(): planes.append(lax.ppermute(halves[j], AXES, pairs))  9.17 us
    ppermute x2, waiting for transfers between devices, scatter_columns(): lines.append(lax.ppermute(mine, AXES, pairs))  7 us
  transfers between devices with their start and end apart: 29, of which 14 were waited for; matrix products, arithmetic and copies ran while one was open for 1% of the time, Pallas kernels for 15%

profile of v5, /device:TPU:1, one launch (start us, length us, event | category | flops | bytes accessed | tf_op | source)
XLA Modules:
  0.0 189.3 jit_solution(14547720622779961613)
XLA Ops:
  6.5 1.1 fusion.3
  7.7 5.2 %collective-permute-start.8 = (f32[64,1024]{1,0:T(8,128)S(1)}, f32[64,1024]{1,0:T(8,128)S(1)}, u32[]{:S(2)}, u32[]{:S(2)}) collective-permute-start(f32[64,1024]{1,0:T(8,128)S(1)} %get-tuple-element.9), channel_id=1, source_target_pairs={{0,8},{1,25},{2,42},{3,59},{4,76},{5,93},{6,110},{7,127},{8,24},{9... | collective-permute-start | bytes 786440 | tf_op jit(solution)/shard_map/ppermute | solution.py:91
  12.9 4.1 %collective-permute-start.7 = (f32[64,1024]{1,0:T(8,128)S(1)}, f32[64,1024]{1,0:T(8,128)S(1)}, u32[]{:S(2)}, u32[]{:S(2)}) collective-permute-start(f32[64,1024]{1,0:T(8,128)S(1)} %get-tuple-element.10), channel_id=1, source_target_pairs={{0,0},{1,17},{2,34},{3,51},{4,68},{5,85},{6,102},{7,119},{8,16},{9... | collective-permute-start | bytes 786440 | tf_op jit(solution)/shard_map/ppermute | solution.py:91
  17.0 2.0 %collective-permute-done.8 = f32[64,1024]{1,0:T(8,128)S(1)} collective-permute-done((f32[64,1024]{1,0:T(8,128)S(1)}, f32[64,1024]{1,0:T(8,128)S(1)}, u32[]{:S(2)}, u32[]{:S(2)}) %collective-permute-start.8) | collective-permute-done | bytes 262176 | tf_op jit(solution)/shard_map/ppermute | solution.py:91
  19.0 7.2 %collective-permute-done.7 = f32[64,1024]{1,0:T(8,128)S(1)} collective-permute-done((f32[64,1024]{1,0:T(8,128)S(1)}, f32[64,1024]{1,0:T(8,128)S(1)}, u32[]{:S(2)}, u32[]{:S(2)}) %collective-permute-start.7) | collective-permute-done | bytes 262176 | tf_op jit(solution)/shard_map/ppermute | solution.py:91
  26.2 1.3 collective-permute-start.10
  27.5 4.0 %collective-permute-start.9 = (f32[64,1024]{1,0:T(8,128)S(1)}, f32[64,1024]{1,0:T(8,128)S(1)}, u32[]{:S(2)}, u32[]{:S(2)}) collective-permute-start(f32[64,1024]{1,0:T(8,128)S(1)} %add.86), channel_id=1, source_target_pairs={{0,0},{1,7},{2,6},{3,5},{4,4},{5,3},{6,2},{7,1},{8,8},{9,15},{10,1... | collective-permute-start | bytes 786440 | tf_op jit(solution)/shard_map/ppermute | solution.py:99
  31.5 4.4 %collective-permute-done.10 = f32[64,1024]{1,0:T(8,128)S(1)} collective-permute-done((f32[64,1024]{1,0:T(8,128)S(1)}, f32[64,1024]{1,0:T(8,128)S(1)}, u32[]{:S(2)}, u32[]{:S(2)}) %collective-permute-start.10) | collective-permute-done | bytes 262176 | tf_op jit(solution)/shard_map/ppermute | solution.py:99
  35.9 2.6 %collective-permute-done.9 = f32[64,1024]{1,0:T(8,128)S(1)} collective-permute-done((f32[64,1024]{1,0:T(8,128)S(1)}, f32[64,1024]{1,0:T(8,128)S(1)}, u32[]{:S(2)}, u32[]{:S(2)}) %collective-permute-start.9) | collective-permute-done | bytes 262176 | tf_op jit(solution)/shard_map/ppermute | solution.py:99
  40.3 1.3 collective-permute-start.12
  41.6 1.3 collective-permute-start.13
  42.9 1.3 collective-permute-start.11
  44.2 1.3 collective-permute-done.11
  45.5 5.2 %collective-permute-start.16 = (f32[32,512]{1,0:T(8,128)S(1)}, f32[32,512]{1,0:T(8,128)S(1)}, u32[]{:S(2)}, u32[]{:S(2)}) collective-permute-start(f32[32,512]{1,0:T(8,128)S(1)} %slice_add_fusion), channel_id=1, source_target_pairs={{0,64},{1,65},{2,66},{3,67},{4,68},{5,69},{6,70},{7,71},{8,72},{9,... | collective-permute-start | bytes 196616 | tf_op jit(solution)/shard_map/ppermute | solution.py:38
  50.7 1.3 collective-permute-start.15
  52.0 1.3 collective-permute-start.14
  53.3 1.3 collective-permute-done.14
  54.7 1.3 collective-permute-start.17
  56.0 1.3 collective-permute-done.17
  58.9 3.1 %collective-permute-done.20 = f32[32,512]{1,0:T(8,128)S(1)} collective-permute-done((f32[32,512]{1,0:T(8,128)S(1)}, f32[32,512]{1,0:T(8,128)S(1)}, u32[]{:S(2)}, u32[]{:S(2)}) %collective-permute-start.20) | collective-permute-done | bytes 65568 | tf_op jit(solution)/shard_map/ppermute | solution.py:53
  62.0 2.6 %collective-permute-done.18 = f32[32,512]{1,0:T(8,128)S(1)} collective-permute-done((f32[32,512]{1,0:T(8,128)S(1)}, f32[32,512]{1,0:T(8,128)S(1)}, u32[]{:S(2)}, u32[]{:S(2)}) %collective-permute-start.18) | collective-permute-done | bytes 65568 | tf_op jit(solution)/shard_map/ppermute | solution.py:53
  64.6 1.2 collective-permute-start.24
  65.8 12.1 %collective-permute-start.23 = (f32[128,512]{1,0:T(8,128)S(1)}, f32[128,512]{1,0:T(8,128)}, u32[]{:S(2)}, u32[]{:S(2)}) collective-permute-start(f32[128,512]{1,0:T(8,128)S(1)} %pad_maximum_fusion.refs_0_), channel_id=1, source_target_pairs={{0,4},{1,133},{2,6},{3,135},{4,128},{5,1},{6,130},{7,3},{128,132},... | collective-permute-start | bytes 786440 | tf_op jit(solution)/shard_map/ppermute | solution.py:60
  80.4 2.8 %collective-permute-done.23.refs_3_ = f32[128,512]{1,0:T(8,128)} collective-permute-done((f32[128,512]{1,0:T(8,128)S(1)}, f32[128,512]{1,0:T(8,128)}, u32[]{:S(2)}, u32[]{:S(2)}) %collective-permute-start.23) | collective-permute-done | bytes 262176 | tf_op jit(solution)/shard_map/ppermute | solution.py:60
  83.2 2.5 %collective-permute-start.21 = (f32[128,512]{1,0:T(8,128)S(1)}, f32[128,512]{1,0:T(8,128)S(1)}, u32[]{:S(2)}, u32[]{:S(2)}) collective-permute-start(f32[128,512]{1,0:T(8,128)S(1)} %pad_maximum_fusion.refs_0_), channel_id=1, source_target_pairs={{0,2},{1,3},{2,4},{3,5},{4,6},{5,7},{6,128},{7,129},{128,130},{129... | collective-permute-start | bytes 786440 | tf_op jit(solution)/shard_map/ppermute | solution.py:60
  85.6 16.1 %collective-permute-done.22.refs_2_ = f32[128,512]{1,0:T(8,128)} collective-permute-done((f32[128,512]{1,0:T(8,128)S(1)}, f32[128,512]{1,0:T(8,128)}, u32[]{:S(2)}, u32[]{:S(2)}) %collective-permute-start.22) | collective-permute-done | bytes 262176 | tf_op jit(solution)/shard_map/ppermute | solution.py:60
  101.8 17.0 %collective-permute-done.21.refs_1_ = f32[128,512]{1,0:T(8,128)S(1)} collective-permute-done((f32[128,512]{1,0:T(8,128)S(1)}, f32[128,512]{1,0:T(8,128)S(1)}, u32[]{:S(2)}, u32[]{:S(2)}) %collective-permute-start.21) | collective-permute-done | bytes 262176 | tf_op jit(solution)/shard_map/ppermute | solution.py:60
  118.8 2.1 %collective-permute-start.26 = (f32[128,512]{1,0:T(8,128)}, f32[128,512]{1,0:T(8,128)}, u32[]{:S(2)}, u32[]{:S(2)}) collective-permute-start(f32[128,512]{1,0:T(8,128)} %collective-permute-done.22.refs_2_), channel_id=1, source_target_pairs={{0,1},{1,0},{2,3},{3,2},{4,5},{5,4},{6,7},{7,6},{8,9},{9,8},{10,11... | collective-permute-start | bytes 786440 | tf_op jit(solution)/shard_map/ppermute | solution.py:65
  121.6 6.1 %collective-permute-done.1.refs_2_ = f32[128,1024]{1,0:T(8,128)S(1)} collective-permute-done((f32[128,1024]{1,0:T(8,128)S(1)}, f32[128,1024]{1,0:T(8,128)S(1)}, u32[]{:S(2)}, u32[]{:S(2)}) %collective-permute-start.1) | collective-permute-done | bytes 524320 | tf_op jit(solution)/shard_map/ppermute | solution.py:69
  129.9 1.8 collective-permute-done.25.refs_5_
  131.6 28.1 %lead.1 = (f32[1024,512]{1,0:T(8,128)}, f32[512,512]{1,0:T(8,128)}) custom-call(s32[22]{0:T(128)} %concatenate.18.where_ref, f32[128,512]{1,0:T(8,128)} %copy-done.1, f32[128,512]{1,0:T(8,128)} %copy-done.8, f32[128,512]{1,0:T(8,128)} %collective-permute-done.22.refs_2_, f32[128,512]{1,0:T(8,128)} %collective-permute-done.23.refs_3_, f32[128,512]{1,0:T(8,128)} %copy-done.7, ...), custom_call_target="tpu_custom_call" | custom-call | tf_op jit(solution)/shard_map/lead/pallas_call | solution.py:236
  160.7 21.8 %apply.1 = f32[1024,1024]{1,0:T(8,128)} custom-call(s32[22]{0:T(128)} %concatenate.18.where_ref, f32[128,1024]{1,0:T(8,128)} %refs_0_.1, f32[128,1024]{1,0:T(8,128)} %copy-done.4, f32[128,1024]{1,0:T(8,128)} %copy-done.3, f32[128,1024]{1,0:T(8,128)} %copy-done.2, f32[128,1024]{1,0:T(8,128)} %copy-done.5, f32[128,1024]{1,0:T(8,128)} %collective-permute-done.4.refs_5_, ...), custom_call_target="tpu_custom_call" | custom-call | tf_op jit(solution)/shard_map/apply/pallas_call | solution.py:330
  (64 shorter events, 9.7 us)
Async XLA Ops:
  6.5 121.8 %copy-start.9 = (s32[4]{0:T(128)S(1)}, s32[4]{0:T(128)}, u32[]{:S(2)}) copy-start(s32[4]{0:T(128)} %constant.41) | copy-start | bytes 52
  6.5 71.4 %copy-start = (f32[128,1024]{1,0:T(8,128)S(1)}, f32[128,1024]{1,0:T(8,128)}, u32[]{:S(2)}) copy-start(f32[128,1024]{1,0:T(8,128)} %refs_0_.1) | copy-start | bytes 1572868
  6.5 153.2 %all-gather.2.cloned.1.call-start = ((), (), s32[]{:S(2)}) async-start(), calls=%async_computation | async-start | bytes 4456448 | tf_op jit(solution)/shard_map/all_gather | solution.py:342
  7.7 11.3 %collective-permute-start.8 = (f32[64,1024]{1,0:T(8,128)S(1)}, f32[64,1024]{1,0:T(8,128)S(1)}, u32[]{:S(2)}, u32[]{:S(2)}) collective-permute-start(f32[64,1024]{1,0:T(8,128)S(1)} %get-tuple-element.9), channel_id=1, source_target_pairs={{0,8},{1,25},{2,42},{3,59},{4,76},{5,93},{6,110},{7,127},{8,24},{9... | collective-permute-start | bytes 786440 | tf_op jit(solution)/shard_map/ppermute | solution.py:91
  12.9 13.3 %collective-permute-start.7 = (f32[64,1024]{1,0:T(8,128)S(1)}, f32[64,1024]{1,0:T(8,128)S(1)}, u32[]{:S(2)}, u32[]{:S(2)}) collective-permute-start(f32[64,1024]{1,0:T(8,128)S(1)} %get-tuple-element.10), channel_id=1, source_target_pairs={{0,0},{1,17},{2,34},{3,51},{4,68},{5,85},{6,102},{7,119},{8,16},{9... | collective-permute-start | bytes 786440 | tf_op jit(solution)/shard_map/ppermute | solution.py:91
  26.2 9.7 %collective-permute-start.10 = (f32[64,1024]{1,0:T(8,128)S(1)}, f32[64,1024]{1,0:T(8,128)S(1)}, u32[]{:S(2)}, u32[]{:S(2)}) collective-permute-start(f32[64,1024]{1,0:T(8,128)S(1)} %add.86), channel_id=1, source_target_pairs={{0,128},{1,135},{2,134},{3,133},{4,132},{5,131},{6,130},{7,129},{8... | collective-permute-start | bytes 786440 | tf_op jit(solution)/shard_map/ppermute | solution.py:99
  27.5 11.0 %collective-permute-start.9 = (f32[64,1024]{1,0:T(8,128)S(1)}, f32[64,1024]{1,0:T(8,128)S(1)}, u32[]{:S(2)}, u32[]{:S(2)}) collective-permute-start(f32[64,1024]{1,0:T(8,128)S(1)} %add.86), channel_id=1, source_target_pairs={{0,0},{1,7},{2,6},{3,5},{4,4},{5,3},{6,2},{7,1},{8,8},{9,15},{10,1... | collective-permute-start | bytes 786440 | tf_op jit(solution)/shard_map/ppermute | solution.py:99
  40.3 3.9 %collective-permute-start.12 = (f32[32,512]{1,0:T(8,128)S(1)}, f32[32,512]{1,0:T(8,128)S(1)}, u32[]{:S(2)}, u32[]{:S(2)}) collective-permute-start(f32[32,512]{1,0:T(8,128)S(1)} %get-tuple-element.11), channel_id=1, source_target_pairs={{0,24},{1,25},{2,26},{3,27},{4,28},{5,29},{6,30},{7,31}} | collective-permute-start | bytes 196616 | tf_op jit(solution)/shard_map/ppermute | solution.py:38
  41.6 2.6 %collective-permute-start.13 = (f32[32,512]{1,0:T(8,128)S(1)}, f32[32,512]{1,0:T(8,128)S(1)}, u32[]{:S(2)}, u32[]{:S(2)}) collective-permute-start(f32[32,512]{1,0:T(8,128)S(1)} %get-tuple-element.12), channel_id=1, source_target_pairs={{0,16},{1,17},{2,18},{3,19},{4,20},{5,21},{6,22},{7,23}} | collective-permute-start | bytes 196616 | tf_op jit(solution)/shard_map/ppermute | solution.py:38
  42.9 2.6 %collective-permute-start.11 = (f32[32,512]{1,0:T(8,128)S(1)}, f32[32,512]{1,0:T(8,128)S(1)}, u32[]{:S(2)}, u32[]{:S(2)}) collective-permute-start(f32[32,512]{1,0:T(8,128)S(1)} %get-tuple-element.13), channel_id=1, source_target_pairs={{0,8},{1,9},{2,10},{3,11},{4,12},{5,13},{6,14},{7,15}} | collective-permute-start | bytes 196616 | tf_op jit(solution)/shard_map/ppermute | solution.py:38
  45.5 7.8 %collective-permute-start.16 = (f32[32,512]{1,0:T(8,128)S(1)}, f32[32,512]{1,0:T(8,128)S(1)}, u32[]{:S(2)}, u32[]{:S(2)}) collective-permute-start(f32[32,512]{1,0:T(8,128)S(1)} %slice_add_fusion), channel_id=1, source_target_pairs={{0,64},{1,65},{2,66},{3,67},{4,68},{5,69},{6,70},{7,71},{8,72},{9,... | collective-permute-start | bytes 196616 | tf_op jit(solution)/shard_map/ppermute | solution.py:38
  50.7 2.6 %collective-permute-start.15 = (f32[32,512]{1,0:T(8,128)S(1)}, f32[32,512]{1,0:T(8,128)S(1)}, u32[]{:S(2)}, u32[]{:S(2)}) collective-permute-start(f32[32,512]{1,0:T(8,128)S(1)} %slice_add_fusion), channel_id=1, source_target_pairs={{0,96},{1,97},{2,98},{3,99},{4,100},{5,101},{6,102},{7,103},{8,104... | collective-permute-start | bytes 196616 | tf_op jit(solution)/shard_map/ppermute | solution.py:38
  52.0 2.6 %collective-permute-start.14 = (f32[32,512]{1,0:T(8,128)S(1)}, f32[32,512]{1,0:T(8,128)S(1)}, u32[]{:S(2)}, u32[]{:S(2)}) collective-permute-start(f32[32,512]{1,0:T(8,128)S(1)} %slice_add_fusion), channel_id=1, source_target_pairs={{0,32},{1,33},{2,34},{3,35},{4,36},{5,37},{6,38},{7,39},{8,40},{9,... | collective-permute-start | bytes 196616 | tf_op jit(solution)/shard_map/ppermute | solution.py:38
  54.7 2.6 %collective-permute-start.17 = (f32[32,512]{1,0:T(8,128)S(1)}, f32[32,512]{1,0:T(8,128)S(1)}, u32[]{:S(2)}, u32[]{:S(2)}) collective-permute-start(f32[32,512]{1,0:T(8,128)S(1)} %add_add_fusion), channel_id=1, source_target_pairs={{0,128},{1,129},{2,130},{3,131},{4,132},{5,133},{6,134},{7,135},{8... | collective-permute-start | bytes 196616 | tf_op jit(solution)/shard_map/ppermute | solution.py:38
  57.3 4.7 %collective-permute-start.20 = (f32[32,512]{1,0:T(8,128)S(1)}, f32[32,512]{1,0:T(8,128)S(1)}, u32[]{:S(2)}, u32[]{:S(2)}) collective-permute-start(f32[32,512]{1,0:T(8,128)S(1)} %add.94), channel_id=1, source_target_pairs={{0,16},{8,24},{16,0},{24,8},{1,17},{9,25},{17,1},{25,9},{2,18},{10... | collective-permute-start | bytes 196616 | tf_op jit(solution)/shard_map/ppermute | solution.py:53
  57.4 4.6 %collective-permute-start.19 = (f32[32,512]{1,0:T(8,128)S(1)}, f32[32,512]{1,0:T(8,128)S(1)}, u32[]{:S(2)}, u32[]{:S(2)}) collective-permute-start(f32[32,512]{1,0:T(8,128)S(1)} %add.94), channel_id=1, source_target_pairs={{0,24},{8,0},{16,8},{24,16},{1,25},{9,1},{17,9},{25,17},{2,26},{10... | collective-permute-start | bytes 196616 | tf_op jit(solution)/shard_map/ppermute | solution.py:53
  58.4 6.2 %collective-permute-start.18 = (f32[32,512]{1,0:T(8,128)S(1)}, f32[32,512]{1,0:T(8,128)S(1)}, u32[]{:S(2)}, u32[]{:S(2)}) collective-permute-start(f32[32,512]{1,0:T(8,128)S(1)} %add.94), channel_id=1, source_target_pairs={{0,8},{8,16},{16,24},{24,0},{1,9},{9,17},{17,25},{25,1},{2,10},{10... | collective-permute-start | bytes 196616 | tf_op jit(solution)/shard_map/ppermute | solution.py:53
  64.6 67.0 %copy-start.1 = (f32[128,512]{1,0:T(8,128)}, f32[128,512]{1,0:T(8,128)S(1)}, u32[]{:S(2)}) copy-start(f32[128,512]{1,0:T(8,128)S(1)} %pad_maximum_fusion.refs_0_) | copy-start | bytes 786436
  64.6 14.8 %collective-permute-start.24 = (f32[128,512]{1,0:T(8,128)S(1)}, f32[128,512]{1,0:T(8,128)S(1)}, u32[]{:S(2)}, u32[]{:S(2)}) collective-permute-start(f32[128,512]{1,0:T(8,128)S(1)} %pad_maximum_fusion.refs_0_), channel_id=1, source_target_pairs={{0,1},{1,0},{2,3},{3,2},{4,5},{5,4},{6,7},{7,6},{8,9},{9,8},{10,11... | collective-permute-start | bytes 786440 | tf_op jit(solution)/shard_map/ppermute | solution.py:65
  65.8 17.4 %collective-permute-start.23 = (f32[128,512]{1,0:T(8,128)S(1)}, f32[128,512]{1,0:T(8,128)}, u32[]{:S(2)}, u32[]{:S(2)}) collective-permute-start(f32[128,512]{1,0:T(8,128)S(1)} %pad_maximum_fusion.refs_0_), channel_id=1, source_target_pairs={{0,4},{1,133},{2,6},{3,135},{4,128},{5,1},{6,130},{7,3},{128,132},... | collective-permute-start | bytes 786440 | tf_op jit(solution)/shard_map/ppermute | solution.py:60
  77.9 43.0 %collective-permute-start.2 = (f32[128,1024]{1,0:T(8,128)S(1)}, f32[128,1024]{1,0:T(8,128)S(1)}, u32[]{:S(2)}, u32[]{:S(2)}) collective-permute-start(f32[128,1024]{1,0:T(8,128)S(1)} %copy-done), channel_id=1, source_target_pairs={{0,6},{2,0},{4,2},{6,4},{1,7},{3,1},{5,3},{7,5},{8,14},{10,8},{12,... | collective-permute-start | bytes 1572872 | tf_op jit(solution)/shard_map/ppermute | solution.py:69
  77.9 49.8 %collective-permute-start.1 = (f32[128,1024]{1,0:T(8,128)S(1)}, f32[128,1024]{1,0:T(8,128)S(1)}, u32[]{:S(2)}, u32[]{:S(2)}) collective-permute-start(f32[128,1024]{1,0:T(8,128)S(1)} %copy-done), channel_id=1, source_target_pairs={{0,4},{2,6},{4,0},{6,2},{1,5},{3,7},{5,1},{7,3},{8,12},{10,14},{12... | collective-permute-start | bytes 1572872 | tf_op jit(solution)/shard_map/ppermute | solution.py:69
  78.4 49.3 %collective-permute-start = (f32[128,1024]{1,0:T(8,128)S(1)}, f32[128,1024]{1,0:T(8,128)S(1)}, u32[]{:S(2)}, u32[]{:S(2)}) collective-permute-start(f32[128,1024]{1,0:T(8,128)S(1)} %copy-done), channel_id=1, source_target_pairs={{0,2},{2,4},{4,6},{6,0},{1,3},{3,5},{5,7},{7,1},{8,10},{10,12},{12... | collective-permute-start | bytes 1572872 | tf_op jit(solution)/shard_map/ppermute | solution.py:69
  79.4 22.4 %collective-permute-start.22 = (f32[128,512]{1,0:T(8,128)S(1)}, f32[128,512]{1,0:T(8,128)}, u32[]{:S(2)}, u32[]{:S(2)}) collective-permute-start(f32[128,512]{1,0:T(8,128)S(1)} %pad_maximum_fusion.refs_0_), channel_id=1, source_target_pairs={{0,134},{1,135},{2,0},{3,1},{4,2},{5,3},{6,4},{7,5},{128,6},{129,7... | collective-permute-start | bytes 786440 | tf_op jit(solution)/shard_map/ppermute | solution.py:60
  83.2 35.6 %collective-permute-start.21 = (f32[128,512]{1,0:T(8,128)S(1)}, f32[128,512]{1,0:T(8,128)S(1)}, u32[]{:S(2)}, u32[]{:S(2)}) collective-permute-start(f32[128,512]{1,0:T(8,128)S(1)} %pad_maximum_fusion.refs_0_), channel_id=1, source_target_pairs={{0,2},{1,3},{2,4},{3,5},{4,6},{5,7},{6,128},{7,129},{128,130},{129... | collective-permute-start | bytes 786440 | tf_op jit(solution)/shard_map/ppermute | solution.py:60
  101.7 26.5 %collective-permute-start.27 = (f32[128,512]{1,0:T(8,128)}, f32[128,512]{1,0:T(8,128)}, u32[]{:S(2)}, u32[]{:S(2)}) collective-permute-start(f32[128,512]{1,0:T(8,128)} %collective-permute-done.23.refs_3_), channel_id=1, source_target_pairs={{0,1},{1,0},{2,3},{3,2},{4,5},{5,4},{6,7},{7,6},{8,9},{9,8},{10,11... | collective-permute-start | bytes 786440 | tf_op jit(solution)/shard_map/ppermute | solution.py:65
  118.8 9.6 %collective-permute-start.26 = (f32[128,512]{1,0:T(8,128)}, f32[128,512]{1,0:T(8,128)}, u32[]{:S(2)}, u32[]{:S(2)}) collective-permute-start(f32[128,512]{1,0:T(8,128)} %collective-permute-done.22.refs_2_), channel_id=1, source_target_pairs={{0,1},{1,0},{2,3},{3,2},{4,5},{5,4},{6,7},{7,6},{8,9},{9,8},{10,11... | collective-permute-start | bytes 786440 | tf_op jit(solution)/shard_map/ppermute | solution.py:65
  120.9 38.7 %collective-permute-start.3 = (f32[128,1024]{1,0:T(8,128)S(1)}, f32[128,1024]{1,0:T(8,128)S(1)}, u32[]{:S(2)}, u32[]{:S(2)}) collective-permute-start(f32[128,1024]{1,0:T(8,128)S(1)} %copy-done), channel_id=1, source_target_pairs={{0,1},{1,0},{2,3},{3,2},{4,5},{5,4},{6,7},{7,6},{8,9},{9,8},{10,11... | collective-permute-start | bytes 1572872 | tf_op jit(solution)/shard_map/ppermute | solution.py:65
  127.7 32.0 %collective-permute-start.6 = (f32[128,1024]{1,0:T(8,128)S(1)}, f32[128,1024]{1,0:T(8,128)S(1)}, u32[]{:S(2)}, u32[]{:S(2)}) collective-permute-start(f32[128,1024]{1,0:T(8,128)S(1)} %collective-permute-done.2.refs_3_), channel_id=1, source_target_pairs={{0,1},{1,0},{2,3},{3,2},{4,5},{5,4},{6,7},{7,6},{8,9},{9,8},{10,11... | collective-permute-start | bytes 1572872 | tf_op jit(solution)/shard_map/ppermute | solution.py:65
  127.7 32.0 %collective-permute-start.5 = (f32[128,1024]{1,0:T(8,128)S(1)}, f32[128,1024]{1,0:T(8,128)}, u32[]{:S(2)}, u32[]{:S(2)}) collective-permute-start(f32[128,1024]{1,0:T(8,128)S(1)} %collective-permute-done.1.refs_2_), channel_id=1, source_target_pairs={{0,1},{1,0},{2,3},{3,2},{4,5},{5,4},{6,7},{7,6},{8,9},{9,8},{10,11... | collective-permute-start | bytes 1572872 | tf_op jit(solution)/shard_map/ppermute | solution.py:65
  128.2 31.5 %collective-permute-start.4 = (f32[128,1024]{1,0:T(8,128)S(1)}, f32[128,1024]{1,0:T(8,128)}, u32[]{:S(2)}, u32[]{:S(2)}) collective-permute-start(f32[128,1024]{1,0:T(8,128)S(1)} %collective-permute-done.refs_1_), channel_id=1, source_target_pairs={{0,1},{1,0},{2,3},{3,2},{4,5},{5,4},{6,7},{7,6},{8,9},{9,8},{10,11... | collective-permute-start | bytes 1572872 | tf_op jit(solution)/shard_map/ppermute | solution.py:65
  128.3 3.3 %collective-permute-start.25 = (f32[128,512]{1,0:T(8,128)}, f32[128,512]{1,0:T(8,128)}, u32[]{:S(2)}, u32[]{:S(2)}) collective-permute-start(f32[128,512]{1,0:T(8,128)} %copy-done.8), channel_id=1, source_target_pairs={{0,1},{1,0},{2,3},{3,2},{4,5},{5,4},{6,7},{7,6},{8,9},{9,8},{10,11... | collective-permute-start | bytes 786440 | tf_op jit(solution)/shard_map/ppermute | solution.py:65
  (7 other events, 129.3 us)
Sparse Core Ops, SparseCore 0:
  39.4 63.1 all-gather.1

commit v6 on v5

--- a/solution.py
+++ b/solution.py
@@ -193,9 +193,12 @@
     g_ref[:, BLOCK:] = jnp.where(same, 1.0, 0.0)
 
     def accumulate(i, carry):
-        chunk = lead_ref[pl.ds(pl.multiple_of(i * BLOCK, BLOCK), BLOCK), :]
-        g_ref[:, :BLOCK] += dot(chunk, chunk, ((0,), (0,)), highest)
-        lh_ref[pl.ds(pl.multiple_of(i * BLOCK, BLOCK), BLOCK), :], ll_ref[pl.ds(pl.multiple_of(i * BLOCK, BLOCK), BLOCK), :] = split(chunk)
+        here = pl.ds(pl.multiple_of(i * BLOCK, BLOCK), BLOCK)
+        chunk = lead_ref[here, :]
+        for lo in range(0, BLOCK, TILE // 2):
+            hi = lo + TILE // 2
+            g_ref[lo:hi, lo:BLOCK] += dot(chunk[:, lo:hi], chunk[:, lo:], ((0,), (0,)), highest)
+        lh_ref[here, :], ll_ref[here, :] = split(chunk)
         return carry
 
     lax.fori_loop(0, lead_ref.shape[0] // BLOCK, accumulate, 0)

time: 192 us -> 192 us (level)
  no operation moved by 1% of the time
where the time goes in v6:
time: 192 us; the launch traced here: 189 us
  waiting for transfers between devices  69.6 us (36%)
  starting transfers between devices  51.5 us (27%)
  Pallas kernels  49.2 us (26%)
  between operations  13.7 us (7%)
  local copies, waits for them, and re-layouts  2.63 us (1%)
  other arithmetic  2.08 us (1%)
    ppermute x3, waiting for transfers between devices, spread_lead(): line.append(lax.ppermute(mine, AXES, pairs))  35.9 us
    pallas_call x1, Pallas kernels, lead_call(): pl.pallas_call(lead_kernel, out_shape=(jax.ShapeDtypeStruct((rows, BLOCK)...  27.4 us
    pallas_call x1, Pallas kernels, apply_call(): pl.pallas_call(apply_kernel, grid_spec=grid_spec, out_shape=jax.ShapeDtyp...  21.8 us
    ppermute x3, starting transfers between devices, spread_lead(): line.append(lax.ppermute(mine, AXES, pairs))  15.6 us
    ppermute x7, starting transfers between devices, permute_rows(): lax.ppermute(values[i], AXES, [(device_id(*s, *c), device_id(*t, *c)) for...  12.9 us
    ppermute x2, starting transfers between devices, scatter_columns(): planes.append(lax.ppermute(halves[j], AXES, pairs))  9.32 us
    ppermute x2, waiting for transfers between devices, scatter_columns(): planes.append(lax.ppermute(halves[j], AXES, pairs))  9.17 us
    ppermute x2, waiting for transfers between devices, scatter_columns(): lines.append(lax.ppermute(mine, AXES, pairs))  7 us
  transfers between devices with their start and end apart: 29, of which 14 were waited for; matrix products, arithmetic and copies ran while one was open for 1% of the time, Pallas kernels for 15%

profile of v6, /device:TPU:1, one launch (start us, length us, event | category | flops | bytes accessed | tf_op | source)
XLA Modules:
  0.0 188.6 jit_solution(11262920422520004285)
XLA Ops:
  6.5 1.1 fusion.3
  7.7 5.2 %collective-permute-start.8 = (f32[64,1024]{1,0:T(8,128)S(1)}, f32[64,1024]{1,0:T(8,128)S(1)}, u32[]{:S(2)}, u32[]{:S(2)}) collective-permute-start(f32[64,1024]{1,0:T(8,128)S(1)} %get-tuple-element.9), channel_id=1, source_target_pairs={{0,8},{1,25},{2,42},{3,59},{4,76},{5,93},{6,110},{7,127},{8,24},{9... | collective-permute-start | bytes 786440 | tf_op jit(solution)/shard_map/ppermute | solution.py:91
  12.9 4.1 %collective-permute-start.7 = (f32[64,1024]{1,0:T(8,128)S(1)}, f32[64,1024]{1,0:T(8,128)S(1)}, u32[]{:S(2)}, u32[]{:S(2)}) collective-permute-start(f32[64,1024]{1,0:T(8,128)S(1)} %get-tuple-element.10), channel_id=1, source_target_pairs={{0,0},{1,17},{2,34},{3,51},{4,68},{5,85},{6,102},{7,119},{8,16},{9... | collective-permute-start | bytes 786440 | tf_op jit(solution)/shard_map/ppermute | solution.py:91
  17.0 2.0 %collective-permute-done.8 = f32[64,1024]{1,0:T(8,128)S(1)} collective-permute-done((f32[64,1024]{1,0:T(8,128)S(1)}, f32[64,1024]{1,0:T(8,128)S(1)}, u32[]{:S(2)}, u32[]{:S(2)}) %collective-permute-start.8) | collective-permute-done | bytes 262176 | tf_op jit(solution)/shard_map/ppermute | solution.py:91
  19.0 7.2 %collective-permute-done.7 = f32[64,1024]{1,0:T(8,128)S(1)} collective-permute-done((f32[64,1024]{1,0:T(8,128)S(1)}, f32[64,1024]{1,0:T(8,128)S(1)}, u32[]{:S(2)}, u32[]{:S(2)}) %collective-permute-start.7) | collective-permute-done | bytes 262176 | tf_op jit(solution)/shard_map/ppermute | solution.py:91
  26.2 1.3 collective-permute-start.10
  27.5 4.0 %collective-permute-start.9 = (f32[64,1024]{1,0:T(8,128)S(1)}, f32[64,1024]{1,0:T(8,128)S(1)}, u32[]{:S(2)}, u32[]{:S(2)}) collective-permute-start(f32[64,1024]{1,0:T(8,128)S(1)} %add.86), channel_id=1, source_target_pairs={{0,0},{1,7},{2,6},{3,5},{4,4},{5,3},{6,2},{7,1},{8,8},{9,15},{10,1... | collective-permute-start | bytes 786440 | tf_op jit(solution)/shard_map/ppermute | solution.py:99
  31.5 4.4 %collective-permute-done.10 = f32[64,1024]{1,0:T(8,128)S(1)} collective-permute-done((f32[64,1024]{1,0:T(8,128)S(1)}, f32[64,1024]{1,0:T(8,128)S(1)}, u32[]{:S(2)}, u32[]{:S(2)}) %collective-permute-start.10) | collective-permute-done | bytes 262176 | tf_op jit(solution)/shard_map/ppermute | solution.py:99
  35.9 2.6 %collective-permute-done.9 = f32[64,1024]{1,0:T(8,128)S(1)} collective-permute-done((f32[64,1024]{1,0:T(8,128)S(1)}, f32[64,1024]{1,0:T(8,128)S(1)}, u32[]{:S(2)}, u32[]{:S(2)}) %collective-permute-start.9) | collective-permute-done | bytes 262176 | tf_op jit(solution)/shard_map/ppermute | solution.py:99
  40.3 1.3 collective-permute-start.12
  41.6 1.3 collective-permute-start.13
  42.9 1.3 collective-permute-start.11
  44.2 1.3 collective-permute-done.11
  45.5 5.2 %collective-permute-start.16 = (f32[32,512]{1,0:T(8,128)S(1)}, f32[32,512]{1,0:T(8,128)S(1)}, u32[]{:S(2)}, u32[]{:S(2)}) collective-permute-start(f32[32,512]{1,0:T(8,128)S(1)} %slice_add_fusion), channel_id=1, source_target_pairs={{0,64},{1,65},{2,66},{3,67},{4,68},{5,69},{6,70},{7,71},{8,72},{9,... | collective-permute-start | bytes 196616 | tf_op jit(solution)/shard_map/ppermute | solution.py:38
  50.7 1.3 collective-permute-start.15
  52.0 1.3 collective-permute-start.14
  53.3 1.3 collective-permute-done.14
  54.7 1.3 collective-permute-start.17
  56.0 1.3 collective-permute-done.17
  58.9 3.1 %collective-permute-done.20 = f32[32,512]{1,0:T(8,128)S(1)} collective-permute-done((f32[32,512]{1,0:T(8,128)S(1)}, f32[32,512]{1,0:T(8,128)S(1)}, u32[]{:S(2)}, u32[]{:S(2)}) %collective-permute-start.20) | collective-permute-done | bytes 65568 | tf_op jit(solution)/shard_map/ppermute | solution.py:53
  62.0 2.6 %collective-permute-done.18 = f32[32,512]{1,0:T(8,128)S(1)} collective-permute-done((f32[32,512]{1,0:T(8,128)S(1)}, f32[32,512]{1,0:T(8,128)S(1)}, u32[]{:S(2)}, u32[]{:S(2)}) %collective-permute-start.18) | collective-permute-done | bytes 65568 | tf_op jit(solution)/shard_map/ppermute | solution.py:53
  64.6 1.2 collective-permute-start.24
  65.8 12.1 %collective-permute-start.23 = (f32[128,512]{1,0:T(8,128)S(1)}, f32[128,512]{1,0:T(8,128)}, u32[]{:S(2)}, u32[]{:S(2)}) collective-permute-start(f32[128,512]{1,0:T(8,128)S(1)} %pad_maximum_fusion.refs_0_), channel_id=1, source_target_pairs={{0,4},{1,133},{2,6},{3,135},{4,128},{5,1},{6,130},{7,3},{128,132},... | collective-permute-start | bytes 786440 | tf_op jit(solution)/shard_map/ppermute | solution.py:60
  80.4 2.8 %collective-permute-done.23.refs_3_ = f32[128,512]{1,0:T(8,128)} collective-permute-done((f32[128,512]{1,0:T(8,128)S(1)}, f32[128,512]{1,0:T(8,128)}, u32[]{:S(2)}, u32[]{:S(2)}) %collective-permute-start.23) | collective-permute-done | bytes 262176 | tf_op jit(solution)/shard_map/ppermute | solution.py:60
  83.2 2.5 %collective-permute-start.21 = (f32[128,512]{1,0:T(8,128)S(1)}, f32[128,512]{1,0:T(8,128)S(1)}, u32[]{:S(2)}, u32[]{:S(2)}) collective-permute-start(f32[128,512]{1,0:T(8,128)S(1)} %pad_maximum_fusion.refs_0_), channel_id=1, source_target_pairs={{0,2},{1,3},{2,4},{3,5},{4,6},{5,7},{6,128},{7,129},{128,130},{129... | collective-permute-start | bytes 786440 | tf_op jit(solution)/shard_map/ppermute | solution.py:60
  85.6 16.1 %collective-permute-done.22.refs_2_ = f32[128,512]{1,0:T(8,128)} collective-permute-done((f32[128,512]{1,0:T(8,128)S(1)}, f32[128,512]{1,0:T(8,128)}, u32[]{:S(2)}, u32[]{:S(2)}) %collective-permute-start.22) | collective-permute-done | bytes 262176 | tf_op jit(solution)/shard_map/ppermute | solution.py:60
  101.8 17.0 %collective-permute-done.21.refs_1_ = f32[128,512]{1,0:T(8,128)S(1)} collective-permute-done((f32[128,512]{1,0:T(8,128)S(1)}, f32[128,512]{1,0:T(8,128)S(1)}, u32[]{:S(2)}, u32[]{:S(2)}) %collective-permute-start.21) | collective-permute-done | bytes 262176 | tf_op jit(solution)/shard_map/ppermute | solution.py:60
  118.8 2.1 %collective-permute-start.26 = (f32[128,512]{1,0:T(8,128)}, f32[128,512]{1,0:T(8,128)}, u32[]{:S(2)}, u32[]{:S(2)}) collective-permute-start(f32[128,512]{1,0:T(8,128)} %collective-permute-done.22.refs_2_), channel_id=1, source_target_pairs={{0,1},{1,0},{2,3},{3,2},{4,5},{5,4},{6,7},{7,6},{8,9},{9,8},{10,11... | collective-permute-start | bytes 786440 | tf_op jit(solution)/shard_map/ppermute | solution.py:65
  121.6 6.1 %collective-permute-done.1.refs_2_ = f32[128,1024]{1,0:T(8,128)S(1)} collective-permute-done((f32[128,1024]{1,0:T(8,128)S(1)}, f32[128,1024]{1,0:T(8,128)S(1)}, u32[]{:S(2)}, u32[]{:S(2)}) %collective-permute-start.1) | collective-permute-done | bytes 524320 | tf_op jit(solution)/shard_map/ppermute | solution.py:69
  129.9 1.8 collective-permute-done.25.refs_5_
  131.6 27.4 %lead.1 = (f32[1024,512]{1,0:T(8,128)}, f32[512,512]{1,0:T(8,128)}) custom-call(s32[22]{0:T(128)} %concatenate.18.where_ref, f32[128,512]{1,0:T(8,128)} %copy-done.1, f32[128,512]{1,0:T(8,128)} %copy-done.8, f32[128,512]{1,0:T(8,128)} %collective-permute-done.22.refs_2_, f32[128,512]{1,0:T(8,128)} %collective-permute-done.23.refs_3_, f32[128,512]{1,0:T(8,128)} %copy-done.7, ...), custom_call_target="tpu_custom_call" | custom-call | tf_op jit(solution)/shard_map/lead/pallas_call | solution.py:239
  160.0 21.8 %apply.1 = f32[1024,1024]{1,0:T(8,128)} custom-call(s32[22]{0:T(128)} %concatenate.18.where_ref, f32[128,1024]{1,0:T(8,128)} %refs_0_.1, f32[128,1024]{1,0:T(8,128)} %copy-done.4, f32[128,1024]{1,0:T(8,128)} %copy-done.3, f32[128,1024]{1,0:T(8,128)} %copy-done.2, f32[128,1024]{1,0:T(8,128)} %copy-done.5, f32[128,1024]{1,0:T(8,128)} %collective-permute-done.4.refs_5_, ...), custom_call_target="tpu_custom_call" | custom-call | tf_op jit(solution)/shard_map/apply/pallas_call | solution.py:333
  (64 shorter events, 9.7 us)
Async XLA Ops:
  6.5 121.8 %copy-start.9 = (s32[4]{0:T(128)S(1)}, s32[4]{0:T(128)}, u32[]{:S(2)}) copy-start(s32[4]{0:T(128)} %constant.41) | copy-start | bytes 52
  6.5 71.4 %copy-start = (f32[128,1024]{1,0:T(8,128)S(1)}, f32[128,1024]{1,0:T(8,128)}, u32[]{:S(2)}) copy-start(f32[128,1024]{1,0:T(8,128)} %refs_0_.1) | copy-start | bytes 1572868
  6.5 152.6 %all-gather.2.cloned.1.call-start = ((), (), s32[]{:S(2)}) async-start(), calls=%async_computation | async-start | bytes 4456448 | tf_op jit(solution)/shard_map/all_gather | solution.py:345
  7.7 11.3 %collective-permute-start.8 = (f32[64,1024]{1,0:T(8,128)S(1)}, f32[64,1024]{1,0:T(8,128)S(1)}, u32[]{:S(2)}, u32[]{:S(2)}) collective-permute-start(f32[64,1024]{1,0:T(8,128)S(1)} %get-tuple-element.9), channel_id=1, source_target_pairs={{0,8},{1,25},{2,42},{3,59},{4,76},{5,93},{6,110},{7,127},{8,24},{9... | collective-permute-start | bytes 786440 | tf_op jit(solution)/shard_map/ppermute | solution.py:91
  12.9 13.3 %collective-permute-start.7 = (f32[64,1024]{1,0:T(8,128)S(1)}, f32[64,1024]{1,0:T(8,128)S(1)}, u32[]{:S(2)}, u32[]{:S(2)}) collective-permute-start(f32[64,1024]{1,0:T(8,128)S(1)} %get-tuple-element.10), channel_id=1, source_target_pairs={{0,0},{1,17},{2,34},{3,51},{4,68},{5,85},{6,102},{7,119},{8,16},{9... | collective-permute-start | bytes 786440 | tf_op jit(solution)/shard_map/ppermute | solution.py:91
  26.2 9.7 %collective-permute-start.10 = (f32[64,1024]{1,0:T(8,128)S(1)}, f32[64,1024]{1,0:T(8,128)S(1)}, u32[]{:S(2)}, u32[]{:S(2)}) collective-permute-start(f32[64,1024]{1,0:T(8,128)S(1)} %add.86), channel_id=1, source_target_pairs={{0,128},{1,135},{2,134},{3,133},{4,132},{5,131},{6,130},{7,129},{8... | collective-permute-start | bytes 786440 | tf_op jit(solution)/shard_map/ppermute | solution.py:99
  27.5 11.0 %collective-permute-start.9 = (f32[64,1024]{1,0:T(8,128)S(1)}, f32[64,1024]{1,0:T(8,128)S(1)}, u32[]{:S(2)}, u32[]{:S(2)}) collective-permute-start(f32[64,1024]{1,0:T(8,128)S(1)} %add.86), channel_id=1, source_target_pairs={{0,0},{1,7},{2,6},{3,5},{4,4},{5,3},{6,2},{7,1},{8,8},{9,15},{10,1... | collective-permute-start | bytes 786440 | tf_op jit(solution)/shard_map/ppermute | solution.py:99
  40.3 3.9 %collective-permute-start.12 = (f32[32,512]{1,0:T(8,128)S(1)}, f32[32,512]{1,0:T(8,128)S(1)}, u32[]{:S(2)}, u32[]{:S(2)}) collective-permute-start(f32[32,512]{1,0:T(8,128)S(1)} %get-tuple-element.11), channel_id=1, source_target_pairs={{0,24},{1,25},{2,26},{3,27},{4,28},{5,29},{6,30},{7,31}} | collective-permute-start | bytes 196616 | tf_op jit(solution)/shard_map/ppermute | solution.py:38
  41.6 2.6 %collective-permute-start.13 = (f32[32,512]{1,0:T(8,128)S(1)}, f32[32,512]{1,0:T(8,128)S(1)}, u32[]{:S(2)}, u32[]{:S(2)}) collective-permute-start(f32[32,512]{1,0:T(8,128)S(1)} %get-tuple-element.12), channel_id=1, source_target_pairs={{0,16},{1,17},{2,18},{3,19},{4,20},{5,21},{6,22},{7,23}} | collective-permute-start | bytes 196616 | tf_op jit(solution)/shard_map/ppermute | solution.py:38
  42.9 2.6 %collective-permute-start.11 = (f32[32,512]{1,0:T(8,128)S(1)}, f32[32,512]{1,0:T(8,128)S(1)}, u32[]{:S(2)}, u32[]{:S(2)}) collective-permute-start(f32[32,512]{1,0:T(8,128)S(1)} %get-tuple-element.13), channel_id=1, source_target_pairs={{0,8},{1,9},{2,10},{3,11},{4,12},{5,13},{6,14},{7,15}} | collective-permute-start | bytes 196616 | tf_op jit(solution)/shard_map/ppermute | solution.py:38
  45.5 7.8 %collective-permute-start.16 = (f32[32,512]{1,0:T(8,128)S(1)}, f32[32,512]{1,0:T(8,128)S(1)}, u32[]{:S(2)}, u32[]{:S(2)}) collective-permute-start(f32[32,512]{1,0:T(8,128)S(1)} %slice_add_fusion), channel_id=1, source_target_pairs={{0,64},{1,65},{2,66},{3,67},{4,68},{5,69},{6,70},{7,71},{8,72},{9,... | collective-permute-start | bytes 196616 | tf_op jit(solution)/shard_map/ppermute | solution.py:38
  50.7 2.6 %collective-permute-start.15 = (f32[32,512]{1,0:T(8,128)S(1)}, f32[32,512]{1,0:T(8,128)S(1)}, u32[]{:S(2)}, u32[]{:S(2)}) collective-permute-start(f32[32,512]{1,0:T(8,128)S(1)} %slice_add_fusion), channel_id=1, source_target_pairs={{0,96},{1,97},{2,98},{3,99},{4,100},{5,101},{6,102},{7,103},{8,104... | collective-permute-start | bytes 196616 | tf_op jit(solution)/shard_map/ppermute | solution.py:38
  52.0 2.6 %collective-permute-start.14 = (f32[32,512]{1,0:T(8,128)S(1)}, f32[32,512]{1,0:T(8,128)S(1)}, u32[]{:S(2)}, u32[]{:S(2)}) collective-permute-start(f32[32,512]{1,0:T(8,128)S(1)} %slice_add_fusion), channel_id=1, source_target_pairs={{0,32},{1,33},{2,34},{3,35},{4,36},{5,37},{6,38},{7,39},{8,40},{9,... | collective-permute-start | bytes 196616 | tf_op jit(solution)/shard_map/ppermute | solution.py:38
  54.7 2.6 %collective-permute-start.17 = (f32[32,512]{1,0:T(8,128)S(1)}, f32[32,512]{1,0:T(8,128)S(1)}, u32[]{:S(2)}, u32[]{:S(2)}) collective-permute-start(f32[32,512]{1,0:T(8,128)S(1)} %add_add_fusion), channel_id=1, source_target_pairs={{0,128},{1,129},{2,130},{3,131},{4,132},{5,133},{6,134},{7,135},{8... | collective-permute-start | bytes 196616 | tf_op jit(solution)/shard_map/ppermute | solution.py:38
  57.3 4.7 %collective-permute-start.20 = (f32[32,512]{1,0:T(8,128)S(1)}, f32[32,512]{1,0:T(8,128)S(1)}, u32[]{:S(2)}, u32[]{:S(2)}) collective-permute-start(f32[32,512]{1,0:T(8,128)S(1)} %add.94), channel_id=1, source_target_pairs={{0,16},{8,24},{16,0},{24,8},{1,17},{9,25},{17,1},{25,9},{2,18},{10... | collective-permute-start | bytes 196616 | tf_op jit(solution)/shard_map/ppermute | solution.py:53
  57.4 4.6 %collective-permute-start.19 = (f32[32,512]{1,0:T(8,128)S(1)}, f32[32,512]{1,0:T(8,128)S(1)}, u32[]{:S(2)}, u32[]{:S(2)}) collective-permute-start(f32[32,512]{1,0:T(8,128)S(1)} %add.94), channel_id=1, source_target_pairs={{0,24},{8,0},{16,8},{24,16},{1,25},{9,1},{17,9},{25,17},{2,26},{10... | collective-permute-start | bytes 196616 | tf_op jit(solution)/shard_map/ppermute | solution.py:53
  58.4 6.2 %collective-permute-start.18 = (f32[32,512]{1,0:T(8,128)S(1)}, f32[32,512]{1,0:T(8,128)S(1)}, u32[]{:S(2)}, u32[]{:S(2)}) collective-permute-start(f32[32,512]{1,0:T(8,128)S(1)} %add.94), channel_id=1, source_target_pairs={{0,8},{8,16},{16,24},{24,0},{1,9},{9,17},{17,25},{25,1},{2,10},{10... | collective-permute-start | bytes 196616 | tf_op jit(solution)/shard_map/ppermute | solution.py:53
  64.6 67.0 %copy-start.1 = (f32[128,512]{1,0:T(8,128)}, f32[128,512]{1,0:T(8,128)S(1)}, u32[]{:S(2)}) copy-start(f32[128,512]{1,0:T(8,128)S(1)} %pad_maximum_fusion.refs_0_) | copy-start | bytes 786436
  64.6 14.8 %collective-permute-start.24 = (f32[128,512]{1,0:T(8,128)S(1)}, f32[128,512]{1,0:T(8,128)S(1)}, u32[]{:S(2)}, u32[]{:S(2)}) collective-permute-start(f32[128,512]{1,0:T(8,128)S(1)} %pad_maximum_fusion.refs_0_), channel_id=1, source_target_pairs={{0,1},{1,0},{2,3},{3,2},{4,5},{5,4},{6,7},{7,6},{8,9},{9,8},{10,11... | collective-permute-start | bytes 786440 | tf_op jit(solution)/shard_map/ppermute | solution.py:65
  65.8 17.4 %collective-permute-start.23 = (f32[128,512]{1,0:T(8,128)S(1)}, f32[128,512]{1,0:T(8,128)}, u32[]{:S(2)}, u32[]{:S(2)}) collective-permute-start(f32[128,512]{1,0:T(8,128)S(1)} %pad_maximum_fusion.refs_0_), channel_id=1, source_target_pairs={{0,4},{1,133},{2,6},{3,135},{4,128},{5,1},{6,130},{7,3},{128,132},... | collective-permute-start | bytes 786440 | tf_op jit(solution)/shard_map/ppermute | solution.py:60
  77.9 43.0 %collective-permute-start.2 = (f32[128,1024]{1,0:T(8,128)S(1)}, f32[128,1024]{1,0:T(8,128)S(1)}, u32[]{:S(2)}, u32[]{:S(2)}) collective-permute-start(f32[128,1024]{1,0:T(8,128)S(1)} %copy-done), channel_id=1, source_target_pairs={{0,6},{2,0},{4,2},{6,4},{1,7},{3,1},{5,3},{7,5},{8,14},{10,8},{12,... | collective-permute-start | bytes 1572872 | tf_op jit(solution)/shard_map/ppermute | solution.py:69
  77.9 49.8 %collective-permute-start.1 = (f32[128,1024]{1,0:T(8,128)S(1)}, f32[128,1024]{1,0:T(8,128)S(1)}, u32[]{:S(2)}, u32[]{:S(2)}) collective-permute-start(f32[128,1024]{1,0:T(8,128)S(1)} %copy-done), channel_id=1, source_target_pairs={{0,4},{2,6},{4,0},{6,2},{1,5},{3,7},{5,1},{7,3},{8,12},{10,14},{12... | collective-permute-start | bytes 1572872 | tf_op jit(solution)/shard_map/ppermute | solution.py:69
  78.4 49.3 %collective-permute-start = (f32[128,1024]{1,0:T(8,128)S(1)}, f32[128,1024]{1,0:T(8,128)S(1)}, u32[]{:S(2)}, u32[]{:S(2)}) collective-permute-start(f32[128,1024]{1,0:T(8,128)S(1)} %copy-done), channel_id=1, source_target_pairs={{0,2},{2,4},{4,6},{6,0},{1,3},{3,5},{5,7},{7,1},{8,10},{10,12},{12... | collective-permute-start | bytes 1572872 | tf_op jit(solution)/shard_map/ppermute | solution.py:69
  79.4 22.4 %collective-permute-start.22 = (f32[128,512]{1,0:T(8,128)S(1)}, f32[128,512]{1,0:T(8,128)}, u32[]{:S(2)}, u32[]{:S(2)}) collective-permute-start(f32[128,512]{1,0:T(8,128)S(1)} %pad_maximum_fusion.refs_0_), channel_id=1, source_target_pairs={{0,134},{1,135},{2,0},{3,1},{4,2},{5,3},{6,4},{7,5},{128,6},{129,7... | collective-permute-start | bytes 786440 | tf_op jit(solution)/shard_map/ppermute | solution.py:60
  83.2 35.6 %collective-permute-start.21 = (f32[128,512]{1,0:T(8,128)S(1)}, f32[128,512]{1,0:T(8,128)S(1)}, u32[]{:S(2)}, u32[]{:S(2)}) collective-permute-start(f32[128,512]{1,0:T(8,128)S(1)} %pad_maximum_fusion.refs_0_), channel_id=1, source_target_pairs={{0,2},{1,3},{2,4},{3,5},{4,6},{5,7},{6,128},{7,129},{128,130},{129... | collective-permute-start | bytes 786440 | tf_op jit(solution)/shard_map/ppermute | solution.py:60
  101.7 26.5 %collective-permute-start.27 = (f32[128,512]{1,0:T(8,128)}, f32[128,512]{1,0:T(8,128)}, u32[]{:S(2)}, u32[]{:S(2)}) collective-permute-start(f32[128,512]{1,0:T(8,128)} %collective-permute-done.23.refs_3_), channel_id=1, source_target_pairs={{0,1},{1,0},{2,3},{3,2},{4,5},{5,4},{6,7},{7,6},{8,9},{9,8},{10,11... | collective-permute-start | bytes 786440 | tf_op jit(solution)/shard_map/ppermute | solution.py:65
  118.8 9.6 %collective-permute-start.26 = (f32[128,512]{1,0:T(8,128)}, f32[128,512]{1,0:T(8,128)}, u32[]{:S(2)}, u32[]{:S(2)}) collective-permute-start(f32[128,512]{1,0:T(8,128)} %collective-permute-done.22.refs_2_), channel_id=1, source_target_pairs={{0,1},{1,0},{2,3},{3,2},{4,5},{5,4},{6,7},{7,6},{8,9},{9,8},{10,11... | collective-permute-start | bytes 786440 | tf_op jit(solution)/shard_map/ppermute | solution.py:65
  120.9 38.1 %collective-permute-start.3 = (f32[128,1024]{1,0:T(8,128)S(1)}, f32[128,1024]{1,0:T(8,128)S(1)}, u32[]{:S(2)}, u32[]{:S(2)}) collective-permute-start(f32[128,1024]{1,0:T(8,128)S(1)} %copy-done), channel_id=1, source_target_pairs={{0,1},{1,0},{2,3},{3,2},{4,5},{5,4},{6,7},{7,6},{8,9},{9,8},{10,11... | collective-permute-start | bytes 1572872 | tf_op jit(solution)/shard_map/ppermute | solution.py:65
  127.7 31.3 %collective-permute-start.6 = (f32[128,1024]{1,0:T(8,128)S(1)}, f32[128,1024]{1,0:T(8,128)S(1)}, u32[]{:S(2)}, u32[]{:S(2)}) collective-permute-start(f32[128,1024]{1,0:T(8,128)S(1)} %collective-permute-done.2.refs_3_), channel_id=1, source_target_pairs={{0,1},{1,0},{2,3},{3,2},{4,5},{5,4},{6,7},{7,6},{8,9},{9,8},{10,11... | collective-permute-start | bytes 1572872 | tf_op jit(solution)/shard_map/ppermute | solution.py:65
  127.7 31.3 %collective-permute-start.5 = (f32[128,1024]{1,0:T(8,128)S(1)}, f32[128,1024]{1,0:T(8,128)}, u32[]{:S(2)}, u32[]{:S(2)}) collective-permute-start(f32[128,1024]{1,0:T(8,128)S(1)} %collective-permute-done.1.refs_2_), channel_id=1, source_target_pairs={{0,1},{1,0},{2,3},{3,2},{4,5},{5,4},{6,7},{7,6},{8,9},{9,8},{10,11... | collective-permute-start | bytes 1572872 | tf_op jit(solution)/shard_map/ppermute | solution.py:65
  128.2 30.9 %collective-permute-start.4 = (f32[128,1024]{1,0:T(8,128)S(1)}, f32[128,1024]{1,0:T(8,128)}, u32[]{:S(2)}, u32[]{:S(2)}) collective-permute-start(f32[128,1024]{1,0:T(8,128)S(1)} %collective-permute-done.refs_1_), channel_id=1, source_target_pairs={{0,1},{1,0},{2,3},{3,2},{4,5},{5,4},{6,7},{7,6},{8,9},{9,8},{10,11... | collective-permute-start | bytes 1572872 | tf_op jit(solution)/shard_map/ppermute | solution.py:65
  128.3 3.3 %collective-permute-start.25 = (f32[128,512]{1,0:T(8,128)}, f32[128,512]{1,0:T(8,128)}, u32[]{:S(2)}, u32[]{:S(2)}) collective-permute-start(f32[128,512]{1,0:T(8,128)} %copy-done.8), channel_id=1, source_target_pairs={{0,1},{1,0},{2,3},{3,2},{4,5},{5,4},{6,7},{7,6},{8,9},{9,8},{10,11... | collective-permute-start | bytes 786440 | tf_op jit(solution)/shard_map/ppermute | solution.py:65
  (7 other events, 127.3 us)
Sparse Core Ops, SparseCore 0:
  39.4 63.1 all-gather.1
